TPU v7x, 32 devices: a whole 2x2x4 slice. The times are simulated.
32 devices in a mesh: dp: 8 (over z, x), tensor: 4 (over y, core).
Axes of the slice: x: 2, y: 2, z: 4, core: 2. Of those that a mesh axis runs over, the one named last changes fastest.
Arguments:
- hidden_in: bfloat16 [10240, 2048], P(('dp', 'tensor')), may hold values from -6 to 6
- skip_mask: int32 [10240], P(('dp', 'tensor')), may hold values 0 or 1
- parents: int32 [8, 10], P('dp'), may hold values from 0 to 5, as said below
- attention_gain: bfloat16 [2048], P('dp'), may hold values from 0.099609375 to 1.8984375
- query_weight: bfloat16 [2048, 2048], P('dp', 'tensor'), may hold values from -0.25 to 0.25
- key_weight: bfloat16 [2048, 512], P('dp', 'tensor'), may hold values from -0.125 to 0.125
- value_weight: bfloat16 [2048, 512], P('dp', 'tensor'), may hold values from -0.125 to 0.125
- output_weight: bfloat16 [2048, 2048], P('dp', 'tensor'), may hold values from -0.5 to 0.5
- feedforward_gain: bfloat16 [2048], P('dp'), may hold values from 0.099609375 to 1.8984375
- gate_weight: bfloat16 [2048, 5632], P('dp', 'tensor'), may hold values from -0.125 to 0.125
- up_weight: bfloat16 [2048, 5632], P('dp', 'tensor'), may hold values from -0.125 to 0.125
- down_weight: bfloat16 [2048, 5632], P('dp', 'tensor'), may hold values from -0.15625 to 0.15625
- grad_out: bfloat16 [10240, 2048], P(('dp', 'tensor')), may hold values from -6 to 6
Outputs:
- layer_out: bfloat16 [10240, 2048], P(('dp', 'tensor'))
- input_grad: float32 [10240, 2048], P(('dp', 'tensor'))
- grad_attention_gain: float32 [2048], P('dp')
- grad_query_weight: float32 [2048, 2048], P('dp', 'tensor')
- grad_key_weight: float32 [2048, 512], P('dp', 'tensor')
- grad_value_weight: float32 [2048, 512], P('dp', 'tensor')
- grad_output_weight: float32 [2048, 2048], P('dp', 'tensor')
- grad_feedforward_gain: float32 [2048], P('dp')
- grad_gate_weight: float32 [2048, 5632], P('dp', 'tensor')
- grad_up_weight: float32 [2048, 5632], P('dp', 'tensor')
- grad_down_weight: float32 [2048, 5632], P('dp', 'tensor')
Inputs may be any that keep to these rules, and one draw needn't show every extreme that they name: `parents`: in every tree, blocks 0 to 3 form a chain (block 0 is its own parent, block b has parent b - 1); the next 2 blocks have parent 4 - 1; each of the last 4 blocks has one of those 2 blocks as parent, and each of those 2 blocks is parent of exactly 2 of the last 4 blocks.
All inputs are finite; a program needn't handle non-finite values. No bound on the sum of `skip_mask` on one device may be relied on, other than what follows from the above.
Results may differ from a plain program's by a relative error of at most 0.023.
Values may be sent and summed in bfloat16 or wider, within the bound.
No kernel may reach another device: no remote copies, remote signals or barrier semaphores. Data moves between devices by JAX's collectives and lax.ppermute only.
A program may use at most 192 MiB of HBM per device.

v0:
```python
import math

import jax
import jax.numpy as jnp
from jax import lax
from jax.sharding import PartitionSpec as P

HD = 128


epsilon = 1e-05
masked_score = -1000000000.0


def tree_layout(parent_ids):
    count = parent_ids.shape[0]
    blocks = jnp.arange(count, dtype=jnp.int32)
    ancestor = blocks[:, None] == blocks[None, :]
    current = blocks
    for sweep in range(count):
        current = jnp.sum(
            jnp.where(blocks[None, :] == current[:, None], parent_ids[None, :], 0), axis=1
        )
        ancestor = ancestor | (blocks[None, :] == current[:, None])
    depth = jnp.sum(ancestor.astype(jnp.int32), axis=1) - 1
    return (ancestor, depth)


def tree_tables(ancestor, depth, block_len, head_size):
    count = depth.shape[0]
    length = count * block_len
    visible = jnp.broadcast_to(
        ancestor[:, None, :, None], (count, block_len, count, block_len)
    ).reshape(length, length)
    places = jnp.arange(length, dtype=jnp.int32)
    block_of = places // block_len
    later = (block_of[:, None] == block_of[None, :]) & (places[None, :] > places[:, None])
    allowed = visible & jnp.logical_not(later)
    block_ids = jnp.arange(count, dtype=jnp.int32)
    row_depth = jnp.sum(
        jnp.where(block_of[:, None] == block_ids[None, :], depth[None, :], 0), axis=1
    )
    position = (row_depth * block_len + places % block_len).astype(jnp.float32)
    half_size = head_size // 2
    freqs = jnp.exp(
        jnp.arange(half_size, dtype=jnp.float32) * (-2.0 * math.log(10000.0) / head_size)
    )
    angles = position[:, None] * freqs[None, :]
    cosine = jnp.concatenate([jnp.cos(angles), jnp.cos(angles)], axis=1)[:, None, :]
    sine = jnp.concatenate([jnp.sin(angles), jnp.sin(angles)], axis=1)[:, None, :]
    return (allowed, cosine, sine)


def rotate(values_in, cosine, sine):
    half_size = values_in.shape[-1] // 2
    turned = jnp.concatenate([-values_in[..., half_size:], values_in[..., :half_size]], axis=-1)
    return values_in * cosine + turned * sine


def rotate_back(grads_in, cosine, sine):
    half_size = grads_in.shape[-1] // 2
    scaled = grads_in * sine
    return grads_in * cosine + jnp.concatenate(
        [scaled[..., half_size:], -scaled[..., :half_size]], axis=-1
    )


def rms_scale(values_in):
    return lax.rsqrt(jnp.mean(values_in * values_in, axis=-1, keepdims=True) + epsilon)


def body(
    hidden_in,
    skip_mask,
    parents,
    attention_gain,
    query_weight,
    key_weight,
    value_weight,
    output_weight,
    feedforward_gain,
    gate_weight,
    up_weight,
    down_weight,
    grad_out,
):
    local_rows = hidden_in.shape[0]
    length = local_rows * lax.axis_size("tensor")
    parent_ids = parents[0]
    block_len = length // parent_ids.shape[0]
    ancestor, depth = tree_layout(parent_ids)
    allowed, cosine, sine = tree_tables(ancestor, depth, block_len, HD)
    keep = (1 - skip_mask).astype(jnp.float32)[:, None]

    def attention_weights():
        return (
            lax.all_gather(attention_gain, "dp", axis=0, tiled=True),
            lax.all_gather(query_weight, "dp", axis=0, tiled=True),
            lax.all_gather(key_weight, "dp", axis=0, tiled=True),
            lax.all_gather(value_weight, "dp", axis=0, tiled=True),
            lax.all_gather(output_weight, "dp", axis=0, tiled=True),
        )

    def feedforward_weights():
        return (
            lax.all_gather(feedforward_gain, "dp", axis=0, tiled=True),
            lax.all_gather(gate_weight, "dp", axis=0, tiled=True),
            lax.all_gather(up_weight, "dp", axis=0, tiled=True),
            lax.all_gather(down_weight, "dp", axis=0, tiled=True),
        )

    def gain_total(partial_sum):
        return lax.psum(partial_sum, "tensor")

    gain_one, weight_query, weight_key, weight_value, weight_output = attention_weights()
    inputs = hidden_in.astype(jnp.float32)
    scale_one = rms_scale(inputs)
    unit_one = inputs * scale_one
    normed = (unit_one * gain_one.astype(jnp.float32)).astype(jnp.bfloat16)
    normed_all = lax.all_gather(normed, "tensor", axis=0, tiled=True)
    heads_dev = weight_query.shape[1] // HD
    kv_dev = weight_key.shape[1] // HD
    group = heads_dev // kv_dev
    scale = HD ** (-0.5)
    half_len = length // 2
    items = heads_dev * 2
    query_raw = jnp.dot(normed_all, weight_query, preferred_element_type=jnp.float32).reshape(
        length, heads_dev, HD
    )
    key_raw = jnp.dot(normed_all, weight_key, preferred_element_type=jnp.float32).reshape(
        length, kv_dev, HD
    )
    values_all = jnp.dot(normed_all, weight_value, preferred_element_type=jnp.float32).astype(
        jnp.bfloat16
    )
    queries = rotate(query_raw, cosine, sine).astype(jnp.bfloat16)
    keys_rot = rotate(key_raw, cosine, sine).astype(jnp.bfloat16)
    query_items = queries.transpose(1, 0, 2).reshape(items, half_len, HD)
    key_heads = keys_rot.transpose(1, 0, 2)
    value_heads = values_all.reshape(length, kv_dev, HD).transpose(1, 0, 2)
    item_ids = jnp.arange(items, dtype=jnp.int32)

    def item_scores(query_block, item):
        kv_index = item // 2 // group
        key_block = lax.dynamic_index_in_dim(key_heads, kv_index, 0, keepdims=False)
        value_block = lax.dynamic_index_in_dim(value_heads, kv_index, 0, keepdims=False)
        mask_rows = lax.dynamic_slice_in_dim(allowed, item % 2 * half_len, half_len, 0)
        scores = (
            jnp.einsum("rd,md->rm", query_block, key_block, preferred_element_type=jnp.float32)
            * scale
        )
        return (jnp.where(mask_rows, scores, masked_score), key_block, value_block)

    def attend_item(operands):
        query_block, item = operands
        scores, key_block, value_block = item_scores(query_block, item)
        top = jnp.max(scores, axis=-1, keepdims=True)
        weights_raw = jnp.exp(scores - top)
        total = jnp.sum(weights_raw, axis=-1, keepdims=True)
        probs = weights_raw / total
        mixed_block = jnp.dot(
            probs.astype(jnp.bfloat16), value_block, preferred_element_type=jnp.float32
        ).astype(jnp.bfloat16)
        return (mixed_block, (top + jnp.log(total))[:, 0])

    mixed_items, log_totals = lax.map(attend_item, (query_items, item_ids))
    mixed = (
        mixed_items.reshape(heads_dev, length, HD)
        .transpose(1, 0, 2)
        .reshape(length, heads_dev * HD)
    )
    attended = lax.psum_scatter(
        jnp.einsum("lc,dc->ld", mixed, weight_output, preferred_element_type=jnp.float32),
        "tensor",
        scatter_dimension=0,
        tiled=True,
    )
    middle = inputs + keep * attended
    gain_two, weight_gate, weight_up, weight_down = feedforward_weights()
    scale_two = rms_scale(middle)
    unit_two = middle * scale_two
    normed_ff = (unit_two * gain_two.astype(jnp.float32)).astype(jnp.bfloat16)
    normed_ff_all = lax.all_gather(normed_ff, "tensor", axis=0, tiled=True)
    gate = jnp.dot(normed_ff_all, weight_gate, preferred_element_type=jnp.float32)
    upward = jnp.dot(normed_ff_all, weight_up, preferred_element_type=jnp.float32)
    sigma = jax.nn.sigmoid(gate)
    active = gate * sigma
    hidden_ff = (active * upward).astype(jnp.bfloat16)
    branch = lax.psum_scatter(
        jnp.einsum("lf,df->ld", hidden_ff, weight_down, preferred_element_type=jnp.float32).astype(
            jnp.bfloat16
        ),
        "tensor",
        scatter_dimension=0,
        tiled=True,
    ).astype(jnp.float32)
    layer_out = (middle + keep * branch).astype(jnp.bfloat16)
    cotangent = grad_out.astype(jnp.float32)
    gain_two, weight_gate, weight_up, weight_down = feedforward_weights()
    branch_grad = (keep * cotangent).astype(jnp.bfloat16)
    branch_grad_all = lax.all_gather(branch_grad, "tensor", axis=0, tiled=True)
    hidden_grad = jnp.dot(branch_grad_all, weight_down, preferred_element_type=jnp.float32)
    grad_down = jnp.einsum(
        "ld,lf->df", branch_grad_all, hidden_ff, preferred_element_type=jnp.float32
    )
    gate_grad = (hidden_grad * upward * sigma * (1.0 + gate * (1.0 - sigma))).astype(jnp.bfloat16)
    up_grad = (hidden_grad * active).astype(jnp.bfloat16)
    grad_gate = jnp.einsum(
        "ld,lf->df", normed_ff_all, gate_grad, preferred_element_type=jnp.float32
    )
    grad_up = jnp.einsum("ld,lf->df", normed_ff_all, up_grad, preferred_element_type=jnp.float32)
    gate_part = jnp.einsum("lf,df->ld", gate_grad, weight_gate, preferred_element_type=jnp.float32)
    up_part = jnp.einsum("lf,df->ld", up_grad, weight_up, preferred_element_type=jnp.float32)
    normed_ff_grad = lax.psum_scatter(
        gate_part + up_part, "tensor", scatter_dimension=0, tiled=True
    )
    grad_gain_two = jnp.sum(normed_ff_grad * unit_two, axis=0)
    scaled_two = normed_ff_grad * gain_two.astype(jnp.float32)
    middle_grad = cotangent + scale_two * (
        scaled_two - unit_two * jnp.mean(scaled_two * unit_two, axis=-1, keepdims=True)
    )
    feedforward_grads = (
        lax.psum_scatter(
            gain_total(grad_gain_two).astype(jnp.bfloat16), "dp", scatter_dimension=0, tiled=True
        ).astype(jnp.float32),
        lax.psum_scatter(
            grad_gate.astype(jnp.bfloat16), "dp", scatter_dimension=0, tiled=True
        ).astype(jnp.float32),
        lax.psum_scatter(
            grad_up.astype(jnp.bfloat16), "dp", scatter_dimension=0, tiled=True
        ).astype(jnp.float32),
        lax.psum_scatter(
            grad_down.astype(jnp.bfloat16), "dp", scatter_dimension=0, tiled=True
        ).astype(jnp.float32),
    )
    gain_one, weight_query, weight_key, weight_value, weight_output = attention_weights()
    attended_grad = (keep * middle_grad).astype(jnp.bfloat16)
    attended_grad_all = lax.all_gather(attended_grad, "tensor", axis=0, tiled=True)
    mixed_grad = jnp.dot(
        attended_grad_all, weight_output, preferred_element_type=jnp.float32
    ).astype(jnp.bfloat16)
    grad_output = jnp.einsum(
        "ld,lc->dc", attended_grad_all, mixed, preferred_element_type=jnp.float32
    )
    mixed_grad_items = (
        mixed_grad.reshape(length, heads_dev, HD).transpose(1, 0, 2).reshape(items, half_len, HD)
    )

    def back_item(carry, operands):
        key_acc, value_acc = carry
        query_block, grad_block, log_total, item = operands
        scores, key_block, value_block = item_scores(query_block, item)
        probs = jnp.exp(scores - log_total[:, None])
        prob_grad = jnp.einsum(
            "rd,md->rm", grad_block, value_block, preferred_element_type=jnp.float32
        )
        score_grad = (
            probs * (prob_grad - jnp.sum(prob_grad * probs, axis=-1, keepdims=True))
        ).astype(jnp.bfloat16)
        query_grad = jnp.dot(score_grad, key_block, preferred_element_type=jnp.float32) * scale
        key_part = (
            jnp.einsum("rm,rd->md", score_grad, query_block, preferred_element_type=jnp.float32)
            * scale
        )
        value_part = jnp.einsum(
            "rm,rd->md", probs.astype(jnp.bfloat16), grad_block, preferred_element_type=jnp.float32
        )
        kv_index = item // 2 // group
        key_acc = key_acc.at[kv_index].add(key_part)
        value_acc = value_acc.at[kv_index].add(value_part)
        return ((key_acc, value_acc), query_grad)

    empty_heads = jnp.zeros((kv_dev, length, HD), jnp.float32)
    (key_acc, value_acc), query_grads = lax.scan(
        back_item, (empty_heads, empty_heads), (query_items, mixed_grad_items, log_totals, item_ids)
    )
    query_rot_grad = query_grads.reshape(heads_dev, length, HD).transpose(1, 0, 2)
    query_raw_grad = (
        rotate_back(query_rot_grad, cosine, sine)
        .astype(jnp.bfloat16)
        .reshape(length, heads_dev * HD)
    )
    key_raw_grad = (
        rotate_back(key_acc.transpose(1, 0, 2), cosine, sine)
        .astype(jnp.bfloat16)
        .reshape(length, kv_dev * HD)
    )
    value_grad = value_acc.transpose(1, 0, 2).astype(jnp.bfloat16).reshape(length, kv_dev * HD)
    grad_query = jnp.einsum(
        "ld,lc->dc", normed_all, query_raw_grad, preferred_element_type=jnp.float32
    )
    grad_key = jnp.einsum("ld,lc->dc", normed_all, key_raw_grad, preferred_element_type=jnp.float32)
    grad_value = jnp.einsum("ld,lc->dc", normed_all, value_grad, preferred_element_type=jnp.float32)
    query_part = jnp.einsum(
        "lc,dc->ld", query_raw_grad, weight_query, preferred_element_type=jnp.float32
    )
    key_part = jnp.einsum("lc,dc->ld", key_raw_grad, weight_key, preferred_element_type=jnp.float32)
    value_part = jnp.einsum(
        "lc,dc->ld", value_grad, weight_value, preferred_element_type=jnp.float32
    )
    normed_grad = lax.psum_scatter(
        (query_part + key_part + value_part).astype(jnp.bfloat16),
        "tensor",
        scatter_dimension=0,
        tiled=True,
    ).astype(jnp.float32)
    grad_gain_one = jnp.sum(normed_grad * unit_one, axis=0)
    scaled_one = normed_grad * gain_one.astype(jnp.float32)
    input_grad = middle_grad + scale_one * (
        scaled_one - unit_one * jnp.mean(scaled_one * unit_one, axis=-1, keepdims=True)
    )
    attention_grads = (
        lax.psum_scatter(
            gain_total(grad_gain_one).astype(jnp.bfloat16), "dp", scatter_dimension=0, tiled=True
        ).astype(jnp.float32),
        lax.psum_scatter(
            grad_query.astype(jnp.bfloat16), "dp", scatter_dimension=0, tiled=True
        ).astype(jnp.float32),
        lax.psum_scatter(
            grad_key.astype(jnp.bfloat16), "dp", scatter_dimension=0, tiled=True
        ).astype(jnp.float32),
        lax.psum_scatter(
            grad_value.astype(jnp.bfloat16), "dp", scatter_dimension=0, tiled=True
        ).astype(jnp.float32),
        lax.psum_scatter(
            grad_output.astype(jnp.bfloat16), "dp", scatter_dimension=0, tiled=True
        ).astype(jnp.float32),
    )
    return (
        layer_out,
        input_grad,
        attention_grads[0],
        attention_grads[1],
        attention_grads[2],
        attention_grads[3],
        attention_grads[4],
        feedforward_grads[0],
        feedforward_grads[1],
        feedforward_grads[2],
        feedforward_grads[3],
    )


def solution(mesh):
    return jax.shard_map(
        body,
        mesh=mesh,
        in_specs=(
            P(("dp", "tensor"), None),
            P(("dp", "tensor")),
            P("dp", None),
            P("dp"),
            P("dp", "tensor"),
            P("dp", "tensor"),
            P("dp", "tensor"),
            P("dp", "tensor"),
            P("dp"),
            P("dp", "tensor"),
            P("dp", "tensor"),
            P("dp", "tensor"),
            P(("dp", "tensor"), None),
        ),
        out_specs=(
            P(("dp", "tensor"), None),
            P(("dp", "tensor"), None),
            P("dp"),
            P("dp", "tensor"),
            P("dp", "tensor"),
            P("dp", "tensor"),
            P("dp", "tensor"),
            P("dp"),
            P("dp", "tensor"),
            P("dp", "tensor"),
            P("dp", "tensor"),
        ),
        check_vma=False,
    )
```

profile of v0, /device:TPU:0, one launch (start us, length us, event | category | flops | bytes accessed | tf_op | source)
XLA Modules:
  0.0 1618.3 jit_solution(11621017453243583606)
XLA Ops:
  7.9 22.2 %all-gather = bf16[8,1,256]{2,1,0:T(2,128)(2,1)S(1)} all-gather(bf16[1,1,256]{2,1,0:T(2,128)(2,1)S(1)} %reshape.568), channel_id=1, replica_groups=mesh['dp'=8,'tensor'=4] {'dp'}, dimensions={0}, use_global_device_ids=true | all-gather | bytes 4608 | tf_op jit(solution)/shard_map/all_gather | solution.py:97
  38.9 31.5 %all_gather.51 = bf16[2048,128]{1,0:T(8,128)(2,1)S(1)} all-gather(bf16[256,128]{1,0:T(8,128)(2,1)S(1)} %copy-done.25), channel_id=1, replica_groups=mesh['dp'=8,'tensor'=4] {'dp'}, dimensions={0}, use_global_device_ids=true | all-gather | bytes 589824 | tf_op jit(solution)/shard_map/all_gather | solution.py:99
  71.2 4.3 fusion.41
  75.4 31.9 %all_gather.52 = bf16[2048,128]{1,0:T(8,128)(2,1)S(1)} all-gather(bf16[256,128]{1,0:T(8,128)(2,1)S(1)} %copy-done.26), channel_id=1, replica_groups=mesh['dp'=8,'tensor'=4] {'dp'}, dimensions={0}, use_global_device_ids=true | all-gather | bytes 589824 | tf_op jit(solution)/shard_map/all_gather | solution.py:100
  109.3 4.5 fusion.94
  113.8 12.9 all-gather.14.cloned.1.call-done
  126.6 6.2 fusion.93
  137.1 4.7 fusion.58
  141.8 72.3 %while.34 = (s32[]{:T(128)}, bf16[8,640,128]{2,1,0:T(8,128)(2,1)}, f32[8,640]{1,0:T(8,128)}, s32[8]{0:T(128)S(1)}, pred[1280,1280]{1,0:T(32,128)(4,1)}, /*index=...) while((s32[]{:T(128)}, bf16[8,640,128]{2,1,0:T(8,128)(2,1)}, ...), condition=%wide.region_16.17_spmd, body=%wide.region_13.16_spmd.sunk | while | flops 426065280 | bytes 11664684 | solution.py:166
  215.8 7.6 fusion.95
  224.1 18.1 %all-gather.1 = bf16[8,1,256]{2,1,0:T(2,128)(2,1)S(1)} all-gather(bf16[1,1,256]{2,1,0:T(2,128)(2,1)S(1)} %reshape.570), channel_id=1, replica_groups=mesh['dp'=8,'tensor'=4] {'dp'}, dimensions={0}, use_global_device_ids=true | all-gather | bytes 4608 | tf_op jit(solution)/shard_map/all_gather | solution.py:106
  242.2 65.2 %reduce-scatter.12.cloned.1.call-done = f32[320,2048]{1,0:T(8,128)} async-done(((f32[1280,2048]{1,0:T(8,128)}), f32[320,2048]{1,0:T(8,128)}) %reduce-scatter.12.cloned.1.call-update) | async-done | bytes 2621456 | tf_op jit(solution)/shard_map/reduce_scatter | solution.py:172
  307.4 4.4 multiply_reduce_fusion.3
  315.6 86.5 %all-gather.20.cloned.1.call-done = bf16[2048,1408]{1,0:T(8,128)(2,1)} async-done(((bf16[256,1408]{1,0:T(8,128)(2,1)}), bf16[2048,1408]{1,0:T(8,128)(2,1)}) %all-gather.20.cloned.1.call-update) | async-done | bytes 5767184 | tf_op jit(solution)/shard_map/all_gather | solution.py:107
  402.1 40.6 %all-gather.18.cloned.1.call-done = bf16[1280,2048]{1,0:T(8,128)(2,1)} async-done(((bf16[320,2048]{1,0:T(8,128)(2,1)}), bf16[1280,2048]{1,0:T(8,128)(2,1)}) %all-gather.18.cloned.1.call-update) | async-done | bytes 5242896 | tf_op jit(solution)/shard_map/all_gather | solution.py:183
  442.7 13.9 fusion.96
  456.6 81.0 %all-gather.22.cloned.1.call-done = bf16[2048,1408]{1,0:T(8,128)(2,1)} async-done(((bf16[256,1408]{1,0:T(8,128)(2,1)}), bf16[2048,1408]{1,0:T(8,128)(2,1)}) %all-gather.22.cloned.1.call-update) | async-done | bytes 5767184 | tf_op jit(solution)/shard_map/all_gather | solution.py:108
  537.6 13.8 fusion.97
  551.4 79.3 %all-gather.24.cloned.1.call-done = bf16[2048,1408]{1,0:T(8,128)(2,1)} async-done(((bf16[256,1408]{1,0:T(8,128)(2,1)}), bf16[2048,1408]{1,0:T(8,128)(2,1)}) %all-gather.24.cloned.1.call-update) | async-done | bytes 5767184 | tf_op jit(solution)/shard_map/all_gather | solution.py:109
  630.6 40.8 %all-gather.26.cloned.1.call-done = bf16[1280,2048]{1,0:T(8,128)(2,1)} async-done(((bf16[320,2048]{1,0:T(8,128)(2,1)}), bf16[1280,2048]{1,0:T(8,128)(2,1)}) %all-gather.26.cloned.1.call-update) | async-done | bytes 5242896 | tf_op jit(solution)/shard_map/all_gather | solution.py:201
  671.4 19.3 %multiply_convert_fusion.1 = (bf16[1280,1408]{1,0:T(8,128)(2,1)S(1)}, bf16[1280,1408]{1,0:T(8,128)(2,1)}, bf16[1280,1408]{1,0:T(8,128)(2,1)}) fusion(f32[1280,1408]{1,0:T(8,128)} %fusion.96, f32[1280,1408]{1,0:T(8,128)} %fusion.97, bf16[1280,2048]{1,0:T(8,128)(2,1)} %all-gather.26.cloned.1.call-done, bf16[2048,1408]{1,0:T(8,128)(2,1)} %all-gather.24.cloned.1.call-done), kind=kOutput, calls=%fused_computation.56 | convolution fusion | flops 7409008640 | bytes 36241408 | tf_op jit(solution)/shard_map/dot_general | solution.py:202
  690.7 15.1 fusion.98
  705.8 13.3 convolution_add_fusion
  719.2 13.3 convolution_convert_fusion.3
  732.6 72.0 %reduce-scatter.16.cloned.1.call-done = f32[320,2048]{1,0:T(8,128)} async-done(((f32[1280,2048]{1,0:T(8,128)}), f32[320,2048]{1,0:T(8,128)}) %reduce-scatter.16.cloned.1.call-update) | async-done | bytes 2621456 | tf_op jit(solution)/shard_map/reduce_scatter | solution.py:214
  807.7 50.9 %reduce-scatter.14.cloned.1.call-done = bf16[320,2048]{1,0:T(8,128)(2,1)} async-done(((bf16[1280,2048]{1,0:T(8,128)(2,1)}), bf16[320,2048]{1,0:T(8,128)(2,1)}) %reduce-scatter.14.cloned.1.call-update) | async-done | bytes 1310736 | tf_op jit(solution)/shard_map/reduce_scatter | solution.py:189
  858.6 5.1 multiply_convert_fusion.4
  863.8 13.0 convolution_convert_fusion.2
  876.9 13.3 convolution_convert_fusion.1
  893.4 13.1 convolution_convert_fusion
  908.1 5.4 convolution_convert_fusion.6
  915.2 150.3 %while.35 = (s32[]{:T(128)}, f32[1,1280,128]{2,1,0:T(8,128)}, f32[1,1280,128]{2,1,0:T(8,128)}, f32[8,640,128]{2,1,0:T(8,128)}, s32[8]{0:T(128)S(1)}, /*index=5*/...) while((s32[]{:T(128)}, f32[1,1280,128]{2,1,0:T(8,128)}, ...), condition=%wide.region_25.26_spmd.clone, body=%wide.region_22.25_spmd.clone.sunk | while | flops 1057176960 | bytes 39174844 | solution.py:274
  1068.2 5.1 convolution_convert_fusion.8
  1075.4 5.2 convolution_convert_fusion.7
  1088.7 6.9 convolution_convert_fusion.5
  1095.7 7.1 convolution_convert_fusion.4
  1104.5 5.5 fusion.99
  1110.0 8.3 add_convert_fusion
  1122.5 9.7 reduce-scatter.30.cloned.1.call-done
  1134.5 111.4 %reduce-scatter.32.cloned.1.call-done = bf16[256,1408]{1,0:T(8,128)(2,1)} async-done(((bf16[2048,1408]{1,0:T(8,128)(2,1)}), bf16[256,1408]{1,0:T(8,128)(2,1)}) %reduce-scatter.32.cloned.1.call-update) | async-done | bytes 720912 | tf_op jit(solution)/shard_map/reduce_scatter | solution.py:232
  1248.2 62.9 %reduce-scatter.22.cloned.1.call-done = bf16[256,128]{1,0:T(8,128)(2,1)} async-done(((bf16[2048,128]{1,0:T(8,128)(2,1)}), bf16[256,128]{1,0:T(8,128)(2,1)}) %reduce-scatter.22.cloned.1.call-update) | async-done | bytes 65552 | tf_op jit(solution)/shard_map/reduce_scatter | solution.py:319
  1312.7 62.7 %reduce-scatter.24.cloned.1.call-done = bf16[256,128]{1,0:T(8,128)(2,1)} async-done(((bf16[2048,128]{1,0:T(8,128)(2,1)}), bf16[256,128]{1,0:T(8,128)(2,1)}) %reduce-scatter.24.cloned.1.call-update) | async-done | bytes 65552 | tf_op jit(solution)/shard_map/reduce_scatter | solution.py:322
  1376.8 69.5 %reduce-scatter.20.cloned.1.call-done = bf16[256,512]{1,0:T(8,128)(2,1)} async-done(((bf16[2048,512]{1,0:T(8,128)(2,1)}), bf16[256,512]{1,0:T(8,128)(2,1)}) %reduce-scatter.20.cloned.1.call-update) | async-done | bytes 262160 | tf_op jit(solution)/shard_map/reduce_scatter | solution.py:316
  1448.2 68.8 %reduce-scatter.26.cloned.1.call-done = bf16[256,512]{1,0:T(8,128)(2,1)} async-done(((bf16[2048,512]{1,0:T(8,128)(2,1)}), bf16[256,512]{1,0:T(8,128)(2,1)}) %reduce-scatter.26.cloned.1.call-update) | async-done | bytes 262160 | tf_op jit(solution)/shard_map/reduce_scatter | solution.py:325
  1518.8 51.2 %reduce-scatter.18.cloned.1.call-done = bf16[320,2048]{1,0:T(8,128)(2,1)} async-done(((bf16[1280,2048]{1,0:T(8,128)(2,1)}), bf16[320,2048]{1,0:T(8,128)(2,1)}) %reduce-scatter.18.cloned.1.call-update) | async-done | bytes 1310736 | tf_op jit(solution)/shard_map/reduce_scatter | solution.py:301
  1572.7 10.2 all-reduce.2
  1582.8 21.7 %all-reduce.3 = (bf16[2048]{0:T(1024)(128)(2,1)S(1)}, bf16[2048]{0:T(1024)(128)(2,1)S(1)}) all-reduce(bf16[2048]{0:T(1024)(128)(2,1)S(1)} %get-tuple-element.495, bf16[2048]{0:T(1024)(128)(2,1)S(1)} %get-tuple-element.496), channel_id=6, replica_groups=mesh['dp'=8,'tensor'=4] {'dp'}, use_global_device_ids=true, to_apply=%region_30.31.clone | all-reduce | flops 4096 | bytes 16384
  1605.2 5.8 fusion.48
  (365 shorter events, 250.0 us)
Async XLA Ops:
  7.2 102.1 %all-gather.12.cloned.1.call-start = ((), (), s32[]{:S(2)}) async-start(), calls=%async_computation.11 | async-start | bytes 6553600 | tf_op jit(solution)/shard_map/all_gather | solution.py:120
  30.1 6.7 copy-start.38
  30.1 8.8 copy-start.25
  35.2 91.4 %all-gather.14.cloned.1.call-start = ((), (), s32[]{:S(2)}) async-start(), calls=%async_computation.12 | async-start | bytes 2359296 | tf_op jit(solution)/shard_map/all_gather | solution.py:98
  36.0 179.8 %all-gather.16.cloned.1.call-start = ((), (), s32[]{:S(2)}) async-start(), calls=%async_computation.13 | async-start | bytes 2359296 | tf_op jit(solution)/shard_map/all_gather | solution.py:101
  36.7 270.7 %reduce-scatter.12.cloned.1.call-start = ((), (), s32[]{:S(2)}) async-start(), calls=%async_computation.14 | async-start | bytes 13107200 | tf_op jit(solution)/shard_map/reduce_scatter | solution.py:172
  70.4 38.9 %copy-start.9 = (bf16[2048,128]{1,0:T(8,128)(2,1)}, bf16[2048,128]{1,0:T(8,128)(2,1)S(1)}, u32[]{:S(2)}) copy-start(bf16[2048,128]{1,0:T(8,128)(2,1)S(1)} %all_gather.51) | copy-start | bytes 1572868
  71.1 4.3 copy-start.26
  107.3 29.8 %copy-start.15 = (bf16[2048,128]{1,0:T(8,128)(2,1)}, bf16[2048,128]{1,0:T(8,128)(2,1)S(1)}, u32[]{:S(2)}) copy-start(bf16[2048,128]{1,0:T(8,128)(2,1)S(1)} %all_gather.52) | copy-start | bytes 1572868
  109.2 23.9 %copy-start.11 = (f32[1280,64]{0,1:T(8,128)}, f32[1280,64]{0,1:T(8,128)S(1)}, u32[]{:S(2)}) copy-start(f32[1280,64]{0,1:T(8,128)S(1)} %get-tuple-element.525) | copy-start | bytes 983044
  215.7 7.6 copy-start.19
  223.4 18.8 %copy-start.34 = (s32[320]{0:T(512)S(1)}, s32[320]{0:T(512)}, u32[]{:S(2)}) copy-start(s32[320]{0:T(512)} %param.22) | copy-start | bytes 3844
  223.4 178.7 %all-gather.20.cloned.1.call-start = ((), (), s32[]{:S(2)}) async-start(), calls=%async_computation.16 | async-start | bytes 6488064 | tf_op jit(solution)/shard_map/all_gather | solution.py:107
  224.0 218.8 %all-gather.18.cloned.1.call-start = ((), (), s32[]{:S(2)}) async-start(), calls=%async_computation.15 | async-start | bytes 6553600 | tf_op jit(solution)/shard_map/all_gather | solution.py:183
  242.2 616.4 %copy-start.21 = (f32[8,1,256]{2,1,0:T(1,128)}, f32[8,1,256]{2,1,0:T(1,128)S(1)}, u32[]{:S(2)}) copy-start(f32[8,1,256]{2,1,0:T(1,128)S(1)} %convert_element_type.220) | copy-start | bytes 24580
  311.8 546.8 %copy-start.1 = (f32[320,2048]{1,0:T(8,128)}, f32[320,2048]{1,0:T(8,128)S(1)}, u32[]{:S(2)}) copy-start(f32[320,2048]{1,0:T(8,128)S(1)} %get-tuple-element.500) | copy-start | bytes 7864324
  311.8 546.8 %copy-start.27 = (f32[320]{0:T(512)}, f32[320]{0:T(512)S(1)}, u32[]{:S(2)}) copy-start(f32[320]{0:T(512)S(1)} %add_rsqrt_fusion) | copy-start | bytes 3844
  313.4 224.2 %all-gather.22.cloned.1.call-start = ((), (), s32[]{:S(2)}) async-start(), calls=%async_computation.17 | async-start | bytes 6488064 | tf_op jit(solution)/shard_map/all_gather | solution.py:108
  314.1 316.5 %all-gather.24.cloned.1.call-start = ((), (), s32[]{:S(2)}) async-start(), calls=%async_computation.18 | async-start | bytes 6488064 | tf_op jit(solution)/shard_map/all_gather | solution.py:109
  314.9 356.6 %all-gather.26.cloned.1.call-start = ((), (), s32[]{:S(2)}) async-start(), calls=%async_computation.20 | async-start | bytes 6553600 | tf_op jit(solution)/shard_map/all_gather | solution.py:201
  315.6 489.0 %reduce-scatter.16.cloned.1.call-start = ((), (), s32[]{:S(2)}) async-start(), calls=%async_computation.21 | async-start | bytes 13107200 | tf_op jit(solution)/shard_map/reduce_scatter | solution.py:214
  690.7 15.1 copy-start.41
  690.7 15.1 copy-start.35
  719.2 139.4 %reduce-scatter.14.cloned.1.call-start = ((), (), s32[]{:S(2)}) async-start(), calls=%async_computation.19 | async-start | bytes 6553600 | tf_op jit(solution)/shard_map/reduce_scatter | solution.py:189
  732.6 174.0 %all-gather.28.cloned.1.call-start = ((), (), s32[]{:S(2)}) async-start(), calls=%async_computation.22 | async-start | bytes 6553600 | tf_op jit(solution)/shard_map/all_gather | solution.py:238
  807.7 56.1 %copy-start.32 = (f32[320]{0:T(512)}, f32[320]{0:T(512)S(1)}, u32[]{:S(2)}) copy-start(f32[320]{0:T(512)S(1)} %broadcast_multiply_fusion.1) | copy-start | bytes 3844
  863.7 256.5 %reduce-scatter.28.cloned.1.call-start = ((), (), s32[]{:S(2)}) async-start(), calls=%async_computation.28 | async-start | bytes 6488064 | tf_op jit(solution)/shard_map/reduce_scatter | solution.py:226
  876.8 255.4 %reduce-scatter.30.cloned.1.call-start = ((), (), s32[]{:S(2)}) async-start(), calls=%async_computation.29 | async-start | bytes 6488064 | tf_op jit(solution)/shard_map/reduce_scatter | solution.py:229
  890.2 355.7 %reduce-scatter.32.cloned.1.call-start = ((), (), s32[]{:S(2)}) async-start(), calls=%async_computation.30 | async-start | bytes 6488064 | tf_op jit(solution)/shard_map/reduce_scatter | solution.py:232
  906.5 404.6 %reduce-scatter.22.cloned.1.call-start = ((), (), s32[]{:S(2)}) async-start(), calls=%async_computation.25 | async-start | bytes 589824 | tf_op jit(solution)/shard_map/reduce_scatter | solution.py:319
  1068.2 5.1 copy-start.17
  1068.2 5.1 copy-start.14
  1075.3 300.0 %reduce-scatter.24.cloned.1.call-start = ((), (), s32[]{:S(2)}) async-start(), calls=%async_computation.26 | async-start | bytes 589824 | tf_op jit(solution)/shard_map/reduce_scatter | solution.py:322
  1080.5 3.3 copy-start.13
  1083.8 362.6 %reduce-scatter.20.cloned.1.call-start = ((), (), s32[]{:S(2)}) async-start(), calls=%async_computation.24 | async-start | bytes 2359296 | tf_op jit(solution)/shard_map/reduce_scatter | solution.py:316
  1088.7 7.0 copy-start.20
  1095.6 7.3 copy-start.10
  1095.6 7.3 copy-start.18
  1095.6 421.3 %reduce-scatter.26.cloned.1.call-start = ((), (), s32[]{:S(2)}) async-start(), calls=%async_computation.27 | async-start | bytes 2359296 | tf_op jit(solution)/shard_map/reduce_scatter | solution.py:325
  1102.8 467.1 %reduce-scatter.18.cloned.1.call-start = ((), (), s32[]{:S(2)}) async-start(), calls=%async_computation.23 | async-start | bytes 6553600 | tf_op jit(solution)/shard_map/reduce_scatter | solution.py:301
  1104.5 5.5 copy-start.16
  1122.5 447.4 %copy-start.24 = (f32[8,1,256]{2,1,0:T(1,128)S(1)}, f32[8,1,256]{2,1,0:T(1,128)}, u32[]{:S(2)}) copy-start(f32[8,1,256]{2,1,0:T(1,128)} %copy-done.23) | copy-start | bytes 24580
  1122.5 447.4 %copy-start.31 = (f32[320]{0:T(512)S(1)}, f32[320]{0:T(512)}, u32[]{:S(2)}) copy-start(f32[320]{0:T(512)} %copy-done.30) | copy-start | bytes 3844
  1248.2 324.5 %copy-start.29 = (f32[2048]{0:T(1024)S(1)}, f32[2048]{0:T(1024)}, u32[]{:S(2)}) copy-start(f32[2048]{0:T(1024)} %get-tuple-element.453) | copy-start | bytes 24580
  1248.2 357.0 %copy-start.2 = (f32[320,2048]{1,0:T(8,128)S(1)}, f32[320,2048]{1,0:T(8,128)}, u32[]{:S(2)}) copy-start(f32[320,2048]{1,0:T(8,128)} %copy-done.1) | copy-start | bytes 7864324
  1248.2 357.0 %copy-start.22 = (f32[8,1,256]{2,1,0:T(1,128)S(1)}, f32[8,1,256]{2,1,0:T(1,128)}, u32[]{:S(2)}) copy-start(f32[8,1,256]{2,1,0:T(1,128)} %copy-done.21) | copy-start | bytes 24580
  1248.2 357.0 %copy-start.28 = (f32[320]{0:T(512)S(1)}, f32[320]{0:T(512)}, u32[]{:S(2)}) copy-start(f32[320]{0:T(512)} %copy-done.27) | copy-start | bytes 3844
  1248.2 357.0 %copy-start.33 = (f32[320]{0:T(512)S(1)}, f32[320]{0:T(512)}, u32[]{:S(2)}) copy-start(f32[320]{0:T(512)} %copy-done.32) | copy-start | bytes 3844
  (35 other events, 63.0 us)
Sparse Core Ops, SparseCore 0:
  35.3 37.8 all-gather.11
  75.4 51.2 all-gather.13
  128.8 47.7 all-gather.15
  223.5 83.8 reduce-scatter.11
  309.4 92.6 all-gather.19
  404.1 38.6 all-gather.17
  444.9 92.6 all-gather.21
  539.8 90.8 all-gather.23
  632.8 38.6 all-gather.25
  719.3 85.2 reduce-scatter.15
  807.2 51.3 reduce-scatter.13
  863.9 40.4 all-gather.27
  908.4 109.9 reduce-scatter.27
  1022.4 109.7 reduce-scatter.29
  1136.1 109.7 reduce-scatter.31
  1249.5 61.6 reduce-scatter.21
  1314.3 60.9 reduce-scatter.23
  1379.7 66.6 reduce-scatter.19
  1450.3 66.5 reduce-scatter.25
  1519.5 50.3 reduce-scatter.17
where the time goes:
time: 1630 us; the launch traced here: 1620 us
  waiting for transfers between devices  970 us (60%)
  matrix products  330 us (20%)
  blocking collectives  136 us (8%)
  other arithmetic  76.7 us (5%)
  local copies, waits for them, and re-layouts  52.4 us (3%)
  loops' own time  37.5 us (2%)
    reduce_scatter x1, waiting for transfers between devices, body(): lax.psum_scatter(grad_down.astype(jnp.bfloat16), 'dp', scatter_dimension=...  111 us
    all_gather x1, waiting for transfers between devices, feedforward_weights(): lax.all_gather(gate_weight, 'dp', axis=0, tiled=True)  86.5 us
    all_gather x1, waiting for transfers between devices, feedforward_weights(): lax.all_gather(up_weight, 'dp', axis=0, tiled=True)  81 us
    all_gather x1, waiting for transfers between devices, feedforward_weights(): lax.all_gather(down_weight, 'dp', axis=0, tiled=True)  79.3 us
    reduce_scatter x1, waiting for transfers between devices, body(): lax.psum_scatter(gate_part + up_part, 'tensor', scatter_dimension=0, tile...  72 us
    reduce_scatter x1, waiting for transfers between devices, body(): lax.psum_scatter(grad_query.astype(jnp.bfloat16), 'dp', scatter_dimension...  69.5 us
    reduce_scatter x1, waiting for transfers between devices, body(): lax.psum_scatter(grad_output.astype(jnp.bfloat16), 'dp', scatter_dimensio...  68.8 us
    reduce_scatter x1, waiting for transfers between devices, body(): lax.psum_scatter(jnp.einsum('lc,dc->ld', mixed, weight_output, preferred_...  65.2 us
  transfers between devices with their start and end apart: 20, of which 16 were waited for; matrix products, arithmetic and copies ran while one was open for 23% of the time, Pallas kernels for 0%

commit v1 on v0

v1 whole, which is shorter than its diff:
```python
import math

import jax
import jax.numpy as jnp
from jax import lax
from jax.experimental import pallas as pl
from jax.experimental.pallas import tpu as pltpu
from jax.sharding import Mesh
from jax.sharding import PartitionSpec as P

HD = 128
TRUNK = 4
BRANCH = 2
PIECES = 4
SHARE = 4
VMEM = 32 * 2**20

epsilon = 1e-05
masked_score = -1000000000.0
bf16 = jnp.bfloat16
f32 = jnp.float32


def dot_nn(a, b):
    return lax.dot_general(a, b, (((1,), (0,)), ((), ())), preferred_element_type=f32)


def dot_nt(a, b):
    return lax.dot_general(a, b, (((1,), (1,)), ((), ())), preferred_element_type=f32)


def dot_tn(a, b):
    return lax.dot_general(a, b, (((0,), (0,)), ((), ())), preferred_element_type=f32)


def place_pieces(table, groups, tree, blocks, into_tree):
    size = tree.shape[0] // PIECES
    piece = 0
    for group in groups:
        for at in range(0, group.shape[0], size):
            start = pl.multiple_of(table[blocks + piece], 64)
            here = slice(at, at + size)
            if into_tree:
                tree[pl.ds(start, size), :] = group[here, :].astype(tree.dtype)
            else:
                group[here, :] = tree[pl.ds(start, size), :].astype(group.dtype)
            piece += 1


def segments(table, rows, block, block_len, key_at, value_at):
    def part(start, size):
        return (
            rows[pl.ds(start, size), key_at : key_at + HD],
            rows[pl.ds(start, size), value_at : value_at + HD],
        )

    found = []
    trunk = min(block, TRUNK)
    if trunk:
        found.append((0, trunk * block_len) + part(0, trunk * block_len))
    if block >= TRUNK + BRANCH:
        start = pl.multiple_of(table[block] * block_len, block_len)
        found.append((start, block_len) + part(start, block_len))
    start = block * block_len
    found.append((start, block_len) + part(start, block_len))
    return found


def block_probs(stacked, found, block_len, scale):
    rows = stacked.shape[0]
    scores = [dot_nt(stacked, keys) * scale for _, _, keys, _ in found]
    row = lax.broadcasted_iota(jnp.int32, (rows, block_len), 0) % block_len
    column = lax.broadcasted_iota(jnp.int32, (rows, block_len), 1)
    scores[-1] = jnp.where(column <= row, scores[-1], masked_score)
    top = jnp.max(scores[0], axis=-1, keepdims=True)
    for part in scores[1:]:
        top = jnp.maximum(top, jnp.max(part, axis=-1, keepdims=True))
    raw = [jnp.exp(part - top) for part in scores]
    total = jnp.sum(raw[0], axis=-1, keepdims=True)
    for part in raw[1:]:
        total = total + jnp.sum(part, axis=-1, keepdims=True)
    inverse = 1.0 / total
    return [part * inverse for part in raw]


def stack_heads(rows, block, block_len, heads):
    here = slice(block * block_len, (block + 1) * block_len)
    return jnp.concatenate([rows[here, h * HD : (h + 1) * HD] for h in range(heads)], axis=0)


def attend_kernel(
    blocks, heads, table, raw, cosine, sine, mixed_near, mixed_far, rotated, tree, result
):
    length = tree.shape[0]
    block_len = length // blocks
    key_at, value_at = heads * HD, (heads + 1) * HD
    place_pieces(table, [raw], tree, blocks, True)

    def turn(block, carry):
        here = pl.ds(pl.multiple_of(block * block_len, block_len), block_len)
        cos, sin = cosine[here, :], sine[here, :]
        for h in range(heads + 1):
            there = slice(h * HD, (h + 1) * HD)
            values = tree[here, there]
            turned = values * cos + pltpu.roll(values, HD // 2, 1) * sin
            rotated[here, there] = turned.astype(bf16)
        rotated[here, value_at : value_at + HD] = tree[here, value_at : value_at + HD].astype(bf16)
        return carry

    lax.fori_loop(0, blocks, turn, 0)
    for block in range(blocks):
        stacked = stack_heads(rotated, block, block_len, heads)
        found = segments(table, rotated, block, block_len, key_at, value_at)
        probs = block_probs(stacked, found, block_len, HD ** (-0.5))
        out = dot_nn(probs[0].astype(bf16), found[0][3])
        for part, (_, _, _, values) in zip(probs[1:], found[1:]):
            out = out + dot_nn(part.astype(bf16), values)
        out = out.astype(bf16)
        for h in range(heads):
            result[block * block_len : (block + 1) * block_len, h * HD : (h + 1) * HD] = out[
                h * block_len : (h + 1) * block_len, :
            ]
    place_pieces(table, [mixed_near, mixed_far], result, blocks, False)


def attend_back_kernel(
    blocks,
    heads,
    table,
    rotated,
    grads,
    cosine,
    sine,
    packed_near,
    packed_far,
    tree,
    keys,
    values,
    result,
):
    length = rotated.shape[0]
    block_len = length // blocks
    key_at, value_at = heads * HD, (heads + 1) * HD
    scale = HD ** (-0.5)
    place_pieces(table, [grads], tree, blocks, True)
    keys[...] = jnp.zeros_like(keys)
    values[...] = jnp.zeros_like(values)

    def turn_back(rows, here):
        return rows * cosine[here, :] + pltpu.roll(rows * sine[here, :], HD // 2, 1)

    for block in range(blocks):
        here = slice(block * block_len, (block + 1) * block_len)
        stacked = stack_heads(rotated, block, block_len, heads)
        cotangent = stack_heads(tree, block, block_len, heads)
        found = segments(table, rotated, block, block_len, key_at, value_at)
        probs = block_probs(stacked, found, block_len, scale)
        prob_grads = [dot_nt(cotangent, part) for _, _, _, part in found]
        delta = jnp.sum(probs[0] * prob_grads[0], axis=-1, keepdims=True)
        for part, grad in zip(probs[1:], prob_grads[1:]):
            delta = delta + jnp.sum(part * grad, axis=-1, keepdims=True)
        query_grad = None
        for (start, size, key_rows, _), part, grad in zip(found, probs, prob_grads):
            score_grad = (part * (grad - delta)).astype(bf16)
            term = dot_nn(score_grad, key_rows)
            query_grad = term if query_grad is None else query_grad + term
            there = pl.ds(start, size)
            keys[there, :] += dot_tn(score_grad, stacked) * scale
            values[there, :] += dot_tn(part.astype(bf16), cotangent)
        query_grad = query_grad * scale
        for h in range(heads):
            rows = query_grad[h * block_len : (h + 1) * block_len, :]
            result[here, h * HD : (h + 1) * HD] = turn_back(rows, here).astype(bf16)

    def finish(block, carry):
        here = pl.ds(pl.multiple_of(block * block_len, block_len), block_len)
        result[here, key_at : key_at + HD] = turn_back(keys[here, :], here).astype(bf16)
        result[here, value_at : value_at + HD] = values[here, :].astype(bf16)
        return carry

    lax.fori_loop(0, blocks, finish, 0)
    place_pieces(table, [packed_near, packed_far], result, blocks, False)


def attention_calls(length, blocks, heads):
    width = (heads + 2) * HD
    vmem = pl.BlockSpec(memory_space=pltpu.VMEM)
    smem = pl.BlockSpec(memory_space=pltpu.SMEM)
    params = pltpu.CompilerParams(vmem_limit_bytes=VMEM)
    pairs = (TRUNK * (TRUNK + 1) // 2 + (blocks - TRUNK) * (TRUNK + 1) + 4) * heads
    pairs = pairs * (length // blocks) ** 2

    def forward(*operands):
        return attend_kernel(blocks, heads, *operands)

    def backward(*operands):
        return attend_back_kernel(blocks, heads, *operands)

    ahead = pl.pallas_call(
        forward,
        in_specs=[smem] + [vmem] * 3,
        out_specs=[vmem] * 3,
        out_shape=[shaped(length // 2, heads * HD, bf16)] * 2 + [shaped(length, width, bf16)],
        scratch_shapes=[pltpu.VMEM((length, width), f32), pltpu.VMEM((length, heads * HD), bf16)],
        compiler_params=params,
        cost_estimate=cost(16 * pairs * HD, length * width * 8),
        name="attend",
    )
    back = pl.pallas_call(
        backward,
        in_specs=[smem] + [vmem] * 4,
        out_specs=[vmem] * 2,
        out_shape=[shaped(length // 2, width, bf16)] * 2,
        scratch_shapes=[
            pltpu.VMEM((length, heads * HD), bf16),
            pltpu.VMEM((length, HD), f32),
            pltpu.VMEM((length, HD), f32),
            pltpu.VMEM((length, width), bf16),
        ],
        compiler_params=params,
        cost_estimate=cost(24 * pairs * HD, length * width * 8),
        name="attend_back",
    )
    return ahead, back


def rotation_tables(blocks, block_len):
    depths = [min(block, TRUNK) + (block >= TRUNK + BRANCH) for block in range(blocks)]
    length = blocks * block_len
    places = jnp.arange(length, dtype=jnp.int32)
    row_depth = jnp.zeros((length,), jnp.int32)
    for block, depth in enumerate(depths):
        row_depth = jnp.where(places // block_len == block, depth, row_depth)
    position = (row_depth * block_len + places % block_len).astype(f32)
    half = HD // 2
    freqs = jnp.exp(jnp.arange(half, dtype=f32) * (-2.0 * math.log(10000.0) / HD))
    angles = position[:, None] * freqs[None, :]
    cosine, sine = jnp.cos(angles), jnp.sin(angles)
    return (
        jnp.concatenate([cosine, cosine], axis=1),
        jnp.concatenate([-sine, sine], axis=1),
    )


def spec(block, index):
    return pl.BlockSpec(block, index)


def whole(shape):
    return pl.BlockSpec(shape, lambda *_: (0,) * len(shape))


def cost(flops, moved):
    return pl.CostEstimate(flops=flops // SHARE, bytes_accessed=moved // SHARE, transcendentals=0)


def shaped(rows, columns, kind):
    return jax.ShapeDtypeStruct((rows, columns), kind)


def runs(order, width):
    run = width // order.shape[0]
    for j in range(order.shape[0]):
        yield slice(j * run, (j + 1) * run), pl.ds(pl.multiple_of(order[j] * run, HD), run)


def row_call(kernel, name, rows, tile, order, operands, results):
    def place(array, offset):
        if offset is None:
            return whole(array.shape)
        steps = array.shape[0] // tile
        return spec((tile, array.shape[1]), lambda i: ((i + offset) % steps, 0))

    return pl.pallas_call(
        kernel,
        grid=(rows // tile,),
        in_specs=[pl.BlockSpec(memory_space=pltpu.SMEM)] + [place(*pair) for pair in operands],
        out_specs=[spec((tile, columns), lambda i: (i, 0)) for columns, _ in results],
        out_shape=[shaped(rows, columns, kind) for columns, kind in results],
        compiler_params=pltpu.CompilerParams(vmem_limit_bytes=VMEM),
        cost_estimate=cost(rows * 2048 * 10, rows * 2048 * 8),
        name=name,
    )(order, *[array for array, _ in operands])


def row_mean(values):
    return jnp.mean(values, axis=-1, keepdims=True)


def norm_kernel(order, rows, gain, normed):
    values = rows[...].astype(f32)
    scale = lax.rsqrt(row_mean(values * values) + epsilon)
    for here, there in runs(order, rows.shape[1]):
        unit = rows[:, there].astype(f32) * scale
        normed[:, here] = (unit * gain[:, here]).astype(bf16)


def pack_kernel(*refs):
    gains, weights, result = refs[0], refs[1:-1], refs[-1]
    at = 0
    for weight in weights:
        result[:, at : at + weight.shape[1]] = weight[...]
        at += weight.shape[1]
    rows = jnp.concatenate([gains[...], jnp.zeros((HD - gains.shape[0], gains.shape[1]), f32)])
    result[:, at:] = rows.T.astype(bf16)


def kept_kernel(order, rows, keep, result):
    for here, there in runs(order, rows.shape[1]):
        result[:, here] = (rows[:, there].astype(f32) * keep[...]).astype(bf16)


def middle_kernel(order, rows, keep, mine, got, gain, middle, normed):
    for here, there in runs(order, rows.shape[1]):
        attended = mine[:, here].astype(f32) + got[:, here].astype(f32)
        middle[:, here] = rows[:, there].astype(f32) + keep[...] * attended
    values = middle[...]
    scale = lax.rsqrt(row_mean(values * values) + epsilon)
    normed[...] = (values * scale * gain[...]).astype(bf16)


def middle_back_kernel(order, cotangent, keep, mine, got, gain, middle, grad, kept):
    values = middle[...]
    scale = lax.rsqrt(row_mean(values * values) + epsilon)
    unit = values * scale
    scaled = (mine[...].astype(f32) + got[...].astype(f32)) * gain[...]
    mean = row_mean(scaled * unit)
    change = scale * (scaled - unit * mean)
    for here, there in runs(order, middle.shape[1]):
        total = cotangent[:, there].astype(f32) + change[:, here]
        grad[:, here] = total
        kept[:, here] = (keep[...] * total).astype(bf16)


def layer_kernel(order, middle, keep, mine, got, result):
    for here, there in runs(order, middle.shape[1]):
        branch = mine[:, here].astype(f32) + got[:, here].astype(f32)
        result[:, there] = (middle[:, here] + keep[...] * branch).astype(bf16)


def input_kernel(order, rows, mine, got, gain, middle_grad, result, scaled):
    values = rows[...].astype(f32)
    scale = lax.rsqrt(row_mean(values * values) + epsilon)
    scaled[...] = (mine[...].astype(f32) + got[...].astype(f32)) * gain[...]
    total = None
    for here, there in runs(order, rows.shape[1]):
        term = jnp.sum(scaled[:, here] * rows[:, there].astype(f32), axis=-1, keepdims=True)
        total = term if total is None else total + term
    mean = total * scale / rows.shape[1]
    for here, there in runs(order, rows.shape[1]):
        unit = rows[:, there].astype(f32) * scale
        result[:, there] = middle_grad[:, here] + scale * (scaled[:, here] - unit * mean)


def column_cuts(width):
    return [slice(at, min(at + 256, width)) for at in range(0, width, 256)]


def of_group(near, far, steps):
    tile = 2 * near.shape[0] // steps
    last = steps // 2 - 1
    return [
        spec((tile, near.shape[1]), lambda i: (jnp.minimum(i, last), 0)),
        spec((tile, far.shape[1]), lambda i: (jnp.maximum(i - last - 1, 0), 0)),
    ]


def resident(slots):
    return [
        pl.BlockSpec(slot.shape, lambda i: (0, 0), pipeline_mode=pl.Buffered(1)) for slot in slots
    ]


def in_halves(steps, work):
    for side in range(2):

        @pl.when(pl.program_id(0) // (steps // 2) == side)
        def _(side=side):
            work(side)


def product(rows, weights, cut):
    total, at = None, 0
    for weight in weights:
        term = dot_nn(rows[:, at : at + weight.shape[0]], weight[:, cut])
        total = term if total is None else total + term
        at += weight.shape[0]
    return total


def through(rows, weights, name, columns, kind):
    near, far = rows
    units = columns.stop - columns.start
    length, width = 2 * near.shape[0], near.shape[1]

    def kernel(*refs):
        slots, result = refs[2:-1], refs[-1]

        def work(side):
            for inside in column_cuts(units):
                cut = slice(columns.start + inside.start, columns.start + inside.stop)
                result[:, inside] = product(refs[side], slots, cut).astype(result.dtype)

        in_halves(2, work)

    return pl.pallas_call(
        kernel,
        grid=(2,),
        in_specs=of_group(near, far, 2) + resident(weights),
        out_specs=spec((length // 2, units), lambda i: (i, 0)),
        out_shape=shaped(length, units, kind),
        compiler_params=pltpu.CompilerParams(vmem_limit_bytes=VMEM),
        cost_estimate=cost(2 * length * width * units, 2 * width * (length + units)),
        name=name,
    )(near, far, *weights)


def gated(rows, hidden_grad, gates, ups):
    near, far = rows
    length, units = hidden_grad.shape
    width = near.shape[1]
    up_slots = [slot for slots, _, _ in ups for slot in slots]
    count = len(gates)

    def kernel(*refs):
        hidden_back, gate_refs = refs[2], refs[3 : 3 + count]
        up_refs = refs[3 + count : -3]
        hidden, gate_grad, up_grad = refs[-3:]

        def work(side):
            at = 0
            for slots, first, columns in ups:
                mine = up_refs[at : at + len(slots)]
                at += len(slots)
                for inside in column_cuts(columns.stop - columns.start):
                    cut = slice(first + inside.start, first + inside.stop)
                    there = slice(columns.start + inside.start, columns.start + inside.stop)
                    gate = product(refs[side], gate_refs, cut)
                    if len(slots) == 1 and count > 1:
                        step = mine[0].shape[1] // count
                        views = [
                            mine[0][:, slice(there.start + s * step, there.stop + s * step)]
                            for s in range(count)
                        ]
                        half = mine[0].shape[0]
                        upward = dot_nn(refs[side][:, :half], views[0])
                        for s in range(1, count):
                            rows_s = refs[side][:, s * half : (s + 1) * half]
                            upward = upward + dot_nn(rows_s, views[s])
                    else:
                        upward = product(refs[side], mine, there)
                    back = hidden_back[:, cut].astype(f32)
                    sigma = 1.0 / (1.0 + jnp.exp(-gate))
                    active = gate * sigma
                    hidden[:, cut] = (active * upward).astype(bf16)
                    slope = sigma * (1.0 + gate * (1.0 - sigma))
                    gate_grad[:, cut] = (back * upward * slope).astype(bf16)
                    up_grad[:, cut] = (back * active).astype(bf16)

        in_halves(4, work)

    here = spec((length // 4, units), lambda i: (i, 0))
    return pl.pallas_call(
        kernel,
        grid=(4,),
        in_specs=of_group(near, far, 4) + [here] + resident(list(gates) + up_slots),
        out_specs=[here] * 3,
        out_shape=[shaped(length, units, bf16)] * 3,
        compiler_params=pltpu.CompilerParams(vmem_limit_bytes=VMEM),
        cost_estimate=cost(4 * length * width * units, 2 * width * (length + 2 * units)),
        name="gated",
    )(near, far, hidden_grad, *gates, *up_slots)


def back_rows(grads, weights, side, name, far=None):
    width = sum(array.shape[0] for array in weights[0][0][0])
    tile = min(512, min(array.shape[0] for parts in weights for w in parts for array in w[0]))
    first = grads[0]
    count = first[0].shape[0] if isinstance(first, tuple) else first.shape[0] // 2
    operands, specs, plan = [], [], [[] for _ in range(width // tile)]
    work = 0
    for grad, parts in zip(grads, weights):
        at = len(operands)
        if isinstance(grad, tuple):
            specs.append(spec(grad[side].shape, lambda j: (0, 0)))
            operands.append(grad[side])
        else:
            specs.append(spec((count, grad.shape[1]), lambda j: (side, 0)))
            operands.append(grad)
        for arrays, unit, columns in parts:
            start = 0
            for array, cut in zip(arrays, columns):
                tiles = array.shape[0] // tile
                for j in range(start, start + tiles):
                    plan[j].append((at, unit, cut, len(operands)))
                operands.append(array)
                specs.append(
                    spec(
                        (tile, array.shape[1]),
                        lambda j, start=start, tiles=tiles: (jnp.clip(j - start, 0, tiles - 1), 0),
                    )
                )
                start += tiles
                work += 2 * count * array.shape[0] * (cut.stop - cut.start)
    if far is not None:
        operands.append(far)
        specs.append(spec((count, tile), lambda j: (0, j)))
    ranges = []
    for j, terms in enumerate(plan):
        if ranges and ranges[-1][2] == terms:
            ranges[-1][1] = j + 1
        else:
            ranges.append([j, j + 1, terms])

    def kernel(*refs):
        result = refs[-1]
        for low, high, terms in ranges:

            @pl.when((pl.program_id(0) >= low) & (pl.program_id(0) < high))
            def _(terms=terms):
                total = None
                for at, unit, cut, place in terms:
                    units = cut.stop - cut.start
                    term = dot_nt(refs[at][:, unit : unit + units], refs[place][:, cut])
                    total = term if total is None else total + term
                if far is not None:
                    total = total + refs[-2][...].astype(f32)
                result[...] = total.astype(result.dtype)

    return pl.pallas_call(
        kernel,
        grid=(width // tile,),
        in_specs=specs,
        out_specs=spec((count, tile), lambda j: (0, j)),
        out_shape=shaped(count, width, bf16),
        compiler_params=pltpu.CompilerParams(vmem_limit_bytes=VMEM),
        cost_estimate=cost(work, 2 * sum(operand.size for operand in operands)),
        name=name,
    )(*operands)


def weight_part(rows, grads, half, s, name, columns=None):
    near, far = rows
    pair = isinstance(grads, tuple)
    units = grads[0].shape[1] if pair else grads.shape[1]
    columns = slice(0, units) if columns is None else columns
    wide = columns.stop - columns.start
    tile = 512 if half % 512 == 0 else half
    tiles = half // tile
    count = near.shape[0]
    row_spec = spec((count, tile), lambda j: (0, s * tiles + j))

    def kernel(near_rows, far_rows, *refs):
        if pair:
            first, second = refs[0][:, columns], refs[1][:, columns]
        else:
            first, second = refs[0][:count, columns], refs[0][count:, columns]
        total = dot_tn(near_rows[...], first) + dot_tn(far_rows[...], second)
        refs[-1][...] = total.astype(bf16)

    operands = grads if pair else (grads,)
    return pl.pallas_call(
        kernel,
        grid=(tiles,),
        in_specs=[row_spec, row_spec] + [whole(operand.shape) for operand in operands],
        out_specs=spec((tile, wide), lambda j: (j, 0)),
        out_shape=shaped(half, wide, bf16),
        compiler_params=pltpu.CompilerParams(vmem_limit_bytes=VMEM),
        cost_estimate=cost(4 * count * half * wide, 4 * count * (half + wide)),
        name=name,
    )(near, far, *operands)


def make_body(outer, inner, rows_axis, cores_axis):
    def body(
        hidden_in,
        skip_mask,
        parents,
        attention_gain,
        query_weight,
        key_weight,
        value_weight,
        output_weight,
        feedforward_gain,
        gate_weight,
        up_weight,
        down_weight,
        grad_out,
    ):
        part = hidden_in.shape[0]
        shard = query_weight.shape[0]
        pieces = rows_axis * cores_axis
        length = part * pieces
        near = part * rows_axis
        blocks = parents.shape[1]
        heads = query_weight.shape[1] // HD
        half = outer * shard
        width = half * inner
        tile = part // 2
        at_inner = lax.axis_index("inner")
        at_row = lax.axis_index("row")
        at_core = lax.axis_index("core")
        slots = range(inner)
        fence = lax.optimization_barrier

        order = jnp.stack(
            [z * inner + (at_inner + s) % inner for s in slots for z in range(outer)]
        ).astype(jnp.int32)

        def from_inner(values, k):
            return lax.ppermute(values, "inner", [((i + k) % inner, i) for i in range(inner)])

        def swap(values, axis):
            return lax.ppermute(values, axis, [(0, 1), (1, 0)])

        def spread(values):
            return [values] + [from_inner(values, s) for s in range(1, inner)]

        def gather(values):
            return lax.all_gather(values, "outer", axis=0, tiled=True)

        def scatter(values):
            return lax.psum_scatter(values, "outer", scatter_dimension=0, tiled=True)

        def collect(parts):
            total = parts[0].astype(f32)
            for s in range(1, inner):
                total = total + from_inner(parts[s], inner - s).astype(f32)
            return total

        keep_own = (1 - skip_mask).astype(f32)
        units = up_weight.shape[1]
        late = units if inner > 1 else 0
        joint_width = (heads + 2) * HD
        packed = pl.pallas_call(
            pack_kernel,
            out_shape=shaped(shard, joint_width + heads * HD + HD, bf16),
            compiler_params=pltpu.CompilerParams(vmem_limit_bytes=VMEM),
            cost_estimate=cost(0, shard * joint_width * 4),
            name="pack",
        )(
            jnp.stack([attention_gain.astype(f32), feedforward_gain.astype(f32)]),
            query_weight,
            key_weight,
            value_weight,
            output_weight,
        )
        keep_got = swap(keep_own, "row")
        row_x = swap(hidden_in, "row")
        row_g = swap(grad_out, "row")
        up_late = jnp.concatenate(spread(up_weight[:, units - late :]), axis=1) if late else None
        row_x, keep_got, up_late = fence((row_x, keep_got, up_late))
        near_x = jnp.concatenate([hidden_in, row_x], axis=0)
        far_x = swap(near_x, "core")
        packed_own = gather(packed)
        packed_own, far_x = fence((packed_own, far_x))
        packed_slots = spread(packed_own)
        keep = jnp.concatenate([keep_own, keep_got], axis=0)[:, None]
        near_g = jnp.concatenate([grad_out, row_g], axis=0)
        (near_branch,) = row_call(
            kept_kernel, "kept", near, tile, order, [(near_g, 0), (keep, 0)], [(width, bf16)]
        )
        far_branch = swap(near_branch, "core")
        down_own = gather(down_weight)
        gate_own = gather(gate_weight)
        early = units - late
        up_own = gather(up_weight[:, :early]) if early else None
        up_both = [gather(up_late)] if late else []

        cosine, sine = rotation_tables(blocks, length // blocks)
        starts = [
            (((at_row + dy) % 2) * cores_axis + (at_core + dc) % 2) * part
            for dc in range(2)
            for dy in range(2)
        ]
        table = jnp.concatenate([parents[0], jnp.stack(starts).astype(jnp.int32)])
        packed_slots, near_branch, far_branch, down_own = fence(
            (packed_slots, near_branch, far_branch, down_own)
        )
        down_first = from_inner(down_own[: half // 2], 1) if inner > 1 else None
        gain_at = joint_width + heads * HD
        joint_columns = slice(0, joint_width)
        output_columns = slice(joint_width, gain_at)
        gains = [values[:, gain_at:].T[:2].astype(f32) for values in packed_slots]
        gain_one = jnp.concatenate([values[0:1] for values in gains], axis=1)
        gain_two = jnp.concatenate([values[1:2] for values in gains], axis=1)
        all_branch = (near_branch, far_branch)

        def norm(rows, name):
            (result,) = row_call(
                norm_kernel, name, near, tile, order, [(rows, 0), (gain_one, None)], [(width, bf16)]
            )
            return result

        normed = (norm(near_x, "norm_near"), norm(far_x, "norm_far"))

        def all_of(arrays):
            return [(arrays, 0, [slice(0, array.shape[1]) for array in arrays])]

        attend, attend_back = attention_calls(length, blocks, heads)
        raw = through(normed, packed_slots, "joint", joint_columns, f32)
        weight_down = [down_own]
        if inner > 1:
            raw, down_first, down_own = fence((raw, down_first, down_own))
            weight_down = [down_own, down_first, from_inner(down_own[half // 2 :], 1)]
        mixed_near, mixed_far, rotated = attend(table, raw, cosine, sine)
        mixed = (mixed_near, mixed_far)

        def packed_plan(columns):
            return [(packed_slots, 0, [columns] * inner)]

        attended_plan = [packed_plan(output_columns)]
        attended_far = swap(back_rows([mixed], attended_plan, 1, "attended_far"), "core")
        attended = back_rows([mixed], attended_plan, 0, "attended_near")
        attended = (attended.astype(f32) + attended_far.astype(f32)).astype(bf16)
        attended, gate_own = fence((attended, gate_own))
        got = swap(attended, "row")
        weight_gate = spread(gate_own)
        got, weight_down, up_own = fence((got, weight_down, up_own))
        weight_up = spread(up_own) if early else []
        swapped = part // tile
        middle, normed_ff = row_call(
            middle_kernel,
            "middle",
            near,
            tile,
            order,
            [(near_x, 0), (keep, 0), (attended, 0), (got, swapped), (gain_two, None)],
            [(width, f32), (width, bf16)],
        )
        all_ff = (normed_ff, swap(normed_ff, "core"))

        hidden_grad = through(all_branch, weight_down, "hidden_grad", slice(0, units), bf16)
        up_parts = [(weight_up, 0, slice(0, early))] if early else []
        up_plan = [(weight_up, 0, [slice(0, early)] * inner)] if early else []
        if late:
            up_parts.append((up_both, early, slice(0, late)))
            up_plan.append((up_both * inner, early, [slice(s * late, (s + 1) * late) for s in slots]))
        hidden_ff, gate_grad, up_grad = gated(all_ff, hidden_grad, weight_gate, up_parts)

        def weight_parts(rows, grads, name, columns=None):
            return [weight_part(rows, grads, half, s, name, columns) for s in slots]

        def core_sum(grads, weights, name):
            far = swap(back_rows(grads, weights, 1, name + "_far"), "core")
            return back_rows(grads, weights, 0, name + "_near", far)

        last = inner - 1
        up_late_sums = None
        if late:
            up_late_parts = weight_parts(all_ff, up_grad, "grad_up_late", slice(early, units))
            gate_grad, up_grad, hidden_ff, up_late_parts = fence(
                (gate_grad, up_grad, hidden_ff, up_late_parts)
            )
            up_late_sums = scatter(jnp.concatenate(up_late_parts, axis=1))
        down_last = weight_part(all_branch, hidden_ff, half, last, "grad_down")
        gate_grad, up_grad, down_last = fence((gate_grad, up_grad, down_last))
        back_plan = ([gate_grad, up_grad], [all_of(weight_gate), up_plan])
        ff_far = back_rows(*back_plan, 1, "normed_ff_grad_far")
        ff_far, gate_grad, up_grad = fence((ff_far, gate_grad, up_grad))
        ff_far = swap(ff_far, "core")
        gate_last = weight_part(all_ff, gate_grad, half, last, "grad_gate")
        gate_grad, up_grad, gate_last = fence((gate_grad, up_grad, gate_last))
        back_plan = ([gate_grad, up_grad], [all_of(weight_gate), up_plan])
        ff_grad = back_rows(*back_plan, 0, "normed_ff_grad_near", ff_far)
        ff_grad, gate_grad, up_grad, hidden_ff = fence((ff_grad, gate_grad, up_grad, hidden_ff))
        ff_got = swap(ff_grad, "row")

        def to_last(values):
            return from_inner(values, inner - last) if last else None

        def plus(values, got):
            if got is None:
                return values
            return (values.astype(f32) + got.astype(f32)).astype(bf16)

        down_got, gate_got = to_last(down_last), to_last(gate_last)
        up_last = up_got = None
        if early:
            up_last = weight_part(all_ff, up_grad, half, last, "grad_up", slice(0, early))
            up_got = to_last(up_last)
        own = [down_last, gate_last, up_last]
        if last:
            own = [
                weight_part(all_branch, hidden_ff, half, 0, "grad_down"),
                weight_part(all_ff, gate_grad, half, 0, "grad_gate"),
                weight_part(all_ff, up_grad, half, 0, "grad_up", slice(0, early))
                if early
                else None,
            ]
        ff_got, down_got, own, up_last = fence((ff_got, down_got, own, up_last))
        grad_down = scatter(plus(own[0], down_got))
        middle_grad, attended_grad = row_call(
            middle_back_kernel,
            "middle_back",
            near,
            tile,
            order,
            [
                (near_g, 0),
                (keep, 0),
                (ff_grad, 0),
                (ff_got, swapped),
                (gain_two, None),
                (middle, 0),
            ],
            [(width, f32), (width, bf16)],
        )
        all_attended = (attended_grad, swap(attended_grad, "core"))

        branch = core_sum([hidden_ff], [all_of(weight_down)], "branch")
        branch_got = swap(branch[part:], "row")
        (layer_out,) = row_call(
            layer_kernel,
            "layer",
            part,
            tile,
            order,
            [(middle, 0), (keep, 0), (branch, 0), (branch_got, 0)],
            [(width, bf16)],
        )

        mixed_grad = through(all_attended, packed_slots, "mixed_grad", output_columns, bf16)
        output_last = weight_part(all_attended, mixed, half, last, "grad_output")
        mixed_grad, output_last = fence((mixed_grad, output_last))
        packed_grad = tuple(attend_back(table, rotated, mixed_grad, cosine, sine))
        joint_last = weight_part(normed, packed_grad, half, last, "grad_joint")
        packed_grad, gate_got, up_late_sums, joint_last = fence(
            (packed_grad, gate_got, up_late_sums, joint_last)
        )
        grad_gate = scatter(plus(own[1], gate_got))
        output_sum, joint_sum = output_last, joint_last
        if last:
            output_sum = plus(
                weight_part(all_attended, mixed, half, 0, "grad_output"), to_last(output_last)
            )
            joint_sum = plus(
                weight_part(normed, packed_grad, half, 0, "grad_joint"), to_last(joint_last)
            )
        attention_sum = jnp.concatenate([output_sum, joint_sum], axis=1)
        grad_up = None
        if early:
            up_got, grad_down = fence((up_got, grad_down))
            grad_up = scatter(plus(own[2], up_got)).astype(f32)
        attention_sum, grad_down = fence((attention_sum, grad_down))
        attention_sum = scatter(attention_sum).astype(f32)
        grad_output = attention_sum[:, : heads * HD]
        grad_joint = attention_sum[:, heads * HD :]
        normed_grad = core_sum([packed_grad], [packed_plan(joint_columns)], "normed_grad")
        normed_got = swap(normed_grad[part:], "row")
        (input_grad,) = pl.pallas_call(
            input_kernel,
            grid=(part // tile,),
            in_specs=[
                pl.BlockSpec(memory_space=pltpu.SMEM),
                spec((tile, width), lambda i: (i, 0)),
                spec((tile, width), lambda i: (i, 0)),
                spec((tile, width), lambda i: (i, 0)),
                whole((1, width)),
                spec((tile, width), lambda i: (i, 0)),
            ],
            out_specs=[spec((tile, width), lambda i: (i, 0))],
            out_shape=[shaped(part, width, f32)],
            scratch_shapes=[pltpu.VMEM((tile, width), f32)],
            compiler_params=pltpu.CompilerParams(vmem_limit_bytes=VMEM),
            cost_estimate=cost(part * width * 10, part * width * 16),
            name="input_grad",
        )(order, hidden_in, normed_grad, normed_got, gain_one, middle_grad)
        if late:
            grad_late = collect([up_late_sums[:, s * late : (s + 1) * late] for s in slots])
            grad_up = grad_late if grad_up is None else jnp.concatenate([grad_up, grad_late], axis=1)
        grad_down, grad_gate, grad_up = [
            grad.astype(f32) for grad in (grad_down, grad_gate, grad_up)
        ]

        def gain_terms(pairs, gain):
            total = None
            for weight, grad in pairs:
                term = jnp.sum(weight.astype(f32) * grad, axis=1)
                total = term if total is None else total + term
            return total / gain.astype(f32)

        query_width = heads * HD
        grad_query = grad_joint[:, :query_width]
        grad_key = grad_joint[:, query_width : query_width + HD]
        grad_value = grad_joint[:, query_width + HD :]
        gain_grads = jnp.stack(
            [
                gain_terms(
                    [
                        (query_weight, grad_query),
                        (key_weight, grad_key),
                        (value_weight, grad_value),
                    ],
                    attention_gain,
                ),
                gain_terms([(gate_weight, grad_gate), (up_weight, grad_up)], feedforward_gain),
            ]
        )
        gain_grads = gain_grads + swap(gain_grads, "core")
        gain_grads = gain_grads + swap(gain_grads, "row")
        return (
            layer_out,
            input_grad,
            gain_grads[0],
            grad_query,
            grad_key,
            grad_value,
            grad_output,
            gain_grads[1],
            grad_gate,
            grad_up,
            grad_down,
        )

    return body


def solution(mesh):
    replicas = mesh.shape["dp"]
    inner = 2 if replicas % 2 == 0 else 1
    outer = replicas // inner
    cores = mesh.shape["tensor"] // 2
    grid = Mesh(mesh.devices.reshape(outer, inner, 2, cores), ("outer", "inner", "row", "core"))
    dp, tensor = ("outer", "inner"), ("row", "core")
    both = dp + tensor
    weight = P(dp, tensor)
    return jax.shard_map(
        make_body(outer, inner, 2, cores),
        mesh=grid,
        in_specs=(
            P(both, None),
            P(both),
            P(dp, None),
            P(dp),
            weight,
            weight,
            weight,
            weight,
            P(dp),
            weight,
            weight,
            weight,
            P(both, None),
        ),
        out_specs=(
            P(both, None),
            P(both, None),
            P(dp),
            weight,
            weight,
            weight,
            weight,
            P(dp),
            weight,
            weight,
            weight,
        ),
        check_vma=False,
    )
```

time: 1630 us -> 717 us (0.44)
  waiting for transfers between devices: 970 us -> 359 us
  matrix products: 330 us -> 0 us
  Pallas kernels: 0 us -> 190 us
  blocking collectives: 136 us -> 0 us
  other arithmetic: 76.7 us -> 32.5 us
  loops' own time: 37.5 us -> 0 us
  local copies, waits for them, and re-layouts: 52.4 us -> 85.6 us
  starting transfers between devices: 0.81 us -> 25 us
    reduce_scatter x11 -> x4, waiting for transfers between devices: 624 us -> 4.07 us  [scatter(): return lax.psum_scatter(values, 'outer', scatter_dimension=0, tiled=True)]
    dot_general x77 -> x0, matrix products: 330 us -> none  [the longest x16 35.6 us: item_scores(): jnp.einsum('rd,md->rm', query_block, key_block, preferred_element_type=jn...]
    ppermute x0 -> x27, waiting for transfers between devices: none -> 269 us  [the longest x10 182 us: from_inner(): lax.ppermute(values, 'inner', [((i + k) % inner, i) for i in range(inner)])]
    all_gather x9 -> x4, waiting for transfers between devices: 341 us -> 85.2 us  [gather(): return lax.all_gather(values, 'outer', axis=0, tiled=True)]
    pallas_call x0 -> x32, Pallas kernels: none -> 190 us  [the longest x10 51.7 us: weight_part(): pl.pallas_call(kernel, grid=(tiles,), in_specs=[row_spec, row_spec] + [wh...]
    all_gather x4 -> x0, blocking collectives: 104 us -> none  [the longest x1 31.9 us: attention_weights(): lax.all_gather(value_weight, 'dp', axis=0, tiled=True)]
    unnamed x81 -> x196, local copies, waits for them, and re-layouts: 6.12 us -> 64.6 us
    another operation x2 -> x0, loops' own time: 37.5 us -> none  [the longest x1 21.7 us: body(): lax.scan(back_item, (empty_heads, empty_heads), (query_items, mixed_grad_...]
  transfers between devices with their start and end apart: 20 -> 35, of which waited for: 16 -> 23; matrix products, arithmetic and copies ran while one was open for 23% -> 7% of each run, Pallas kernels for 0% -> 21%
where the time goes in v1:
time: 717 us; the launch traced here: 708 us
  waiting for transfers between devices  359 us (50%)
  Pallas kernels  190 us (26%)
  local copies, waits for them, and re-layouts  85.6 us (12%)
  other arithmetic  32.5 us (5%)
  starting transfers between devices  25 us (3%)
  between operations  15.7 us (2%)
    ppermute x10, waiting for transfers between devices, from_inner(): lax.ppermute(values, 'inner', [((i + k) % inner, i) for i in range(inner)])  182 us
    ppermute x17, waiting for transfers between devices, swap(): return lax.ppermute(values, axis, [(0, 1), (1, 0)])  86.8 us
    all_gather x4, waiting for transfers between devices, gather(): return lax.all_gather(values, 'outer', axis=0, tiled=True)  85.2 us
    unnamed x196, local copies, waits for them, and re-layouts  64.6 us
    pallas_call x10, Pallas kernels, weight_part(): pl.pallas_call(kernel, grid=(tiles,), in_specs=[row_spec, row_spec] + [wh...  51.7 us
    pallas_call x8, Pallas kernels, back_rows(): pl.pallas_call(kernel, grid=(width // tile,), in_specs=specs, out_specs=s...  47 us
    pallas_call x1, Pallas kernels, gated(): pl.pallas_call(kernel, grid=(4,), in_specs=of_group(near, far, 4) + [here...  24.9 us
    pallas_call x3, Pallas kernels, through(): pl.pallas_call(kernel, grid=(2,), in_specs=of_group(near, far, 2) + resid...  18.4 us
  transfers between devices with their start and end apart: 35, of which 23 were waited for; matrix products, arithmetic and copies ran while one was open for 7% of the time, Pallas kernels for 21%

profile of v1, /device:TPU:0, one launch (start us, length us, event | category | flops | bytes accessed | tf_op | source)
XLA Modules:
  0.0 708.0 jit_solution(6406000655896004995)
XLA Ops:
  14.2 3.0 collective-permute-start
  20.7 14.2 %collective-permute-done.2 = bf16[256,1408]{1,0:T(8,128)(2,1)S(1)} collective-permute-done((bf16[256,1408]{1,0:T(8,128)(2,1)S(1)}, bf16[256,1408]{1,0:T(8,128)(2,1)S(1)}, u32[]{:S(2)}, u32[]{:S(2)}) %collective-permute-start.2) | collective-permute-done | bytes 720928 | tf_op jit(solution)/shard_map/ppermute | solution.py:611
  36.0 10.3 %collective-permute-done.1 = f32[320]{0:T(512)S(1)} collective-permute-done((f32[320]{0:T(512)S(1)}, f32[320]{0:T(512)S(1)}, u32[]{:S(2)}, u32[]{:S(2)}) %collective-permute-start.1) | collective-permute-done | bytes 1312 | tf_op jit(solution)/shard_map/ppermute | solution.py:614
  52.9 22.5 %all-gather.5.cloned.1.call-done = bf16[1024,1408]{0,1:T(8,128)(2,1)} async-done(((bf16[256,1408]{0,1:T(8,128)(2,1)}), bf16[1024,1408]{0,1:T(8,128)(2,1)}) %all-gather.5.cloned.1.call-update) | async-done | bytes 2883600 | tf_op jit(solution)/shard_map/all_gather | solution.py:620
  90.7 43.6 %all-gather.7.cloned.1.call-done.refs_2_.refs_1_ = bf16[1024,1408]{1,0:T(8,128)(2,1)} async-done(((bf16[256,1408]{1,0:T(8,128)(2,1)}), bf16[1024,1408]{1,0:T(8,128)(2,1)}) %all-gather.7.cloned.1.call-update) | async-done | bytes 2883600 | tf_op jit(solution)/shard_map/all_gather | solution.py:620
  134.4 5.7 collective-permute-done.4
  140.1 3.4 copy.39.refs_2_.refs_1_
  143.5 4.7 copy.40.refs_3_.refs_2_
  154.5 4.1 norm_far.1.refs_1_.far_rows
  158.7 4.4 joint.1.operands_1_
  163.2 19.2 %collective-permute-done.7.refs_3_.refs_2_ = bf16[512,1408]{1,0:T(8,128)(2,1)S(1)} collective-permute-done((bf16[512,1408]{1,0:T(8,128)(2,1)S(1)}, bf16[512,1408]{1,0:T(8,128)(2,1)S(1)}, u32[]{:S(2)}, u32[]{:S(2)}) %collective-permute-start.7) | collective-permute-done | bytes 1441824 | tf_op jit(solution)/shard_map/ppermute | solution.py:611
  182.4 10.0 %attend.1 = (bf16[640,512]{1,0:T(8,128)(2,1)S(1)}, bf16[640,512]{1,0:T(8,128)(2,1)S(1)}, bf16[1280,768]{1,0:T(8,128)(2,1)S(1)}) custom-call(s32[14]{0:T(128)S(1)} %concatenate.36.operands_0_, f32[1280,768]{1,0:T(8,128)S(1)} %joint.1.operands_1_, f32[1280,128]{1,0:T(8,128)S(1)} %copy-done.78, f32[1280,128]{1,0:T(8,128)S(1)} %copy-done.80), custom_call_target="tpu_custom_call" | custom-call | flops 1476395008 | bytes 1966080 | tf_op jit(solution)/shard_map/attend/pallas_call | solution.py:706
  199.9 2.7 add_convert_fusion.2.mine
  208.0 32.4 %collective-permute-done.10.refs_4_.refs_3_ = bf16[512,1408]{1,0:T(8,128)(2,1)S(1)} collective-permute-done((bf16[512,1408]{1,0:T(8,128)(2,1)S(1)}, bf16[512,1408]{1,0:T(8,128)(2,1)S(1)}, u32[]{:S(2)}, u32[]{:S(2)}) %collective-permute-start.10) | collective-permute-done | bytes 1441824 | tf_op jit(solution)/shard_map/ppermute | solution.py:611
  240.4 21.3 %collective-permute-done.9.got = bf16[640,2048]{1,0:T(8,128)(2,1)S(1)} collective-permute-done((bf16[640,2048]{1,0:T(8,128)(2,1)}, bf16[640,2048]{1,0:T(8,128)(2,1)S(1)}, u32[]{:S(2)}, u32[]{:S(2)}) %collective-permute-start.9) | collective-permute-done | bytes 2621472 | tf_op jit(solution)/shard_map/ppermute | solution.py:614
  263.4 3.9 middle.1
  269.7 10.7 %hidden_grad.1.refs_2_ = bf16[1280,1408]{1,0:T(8,128)(2,1)S(1)} custom-call(bf16[640,2048]{1,0:T(8,128)(2,1)S(1)} %copy-done.17, bf16[640,2048]{1,0:T(8,128)(2,1)} %collective-permute-done.6.refs_1_.far_rows, bf16[1024,1408]{1,0:T(8,128)(2,1)S(1)} %copy-done.13, bf16[512,1408]{1,0:T(8,128)(2,1)S(1)} %copy-done.44, ...), custom_call_target="tpu_custom_call" | custom-call | flops 1845493760 | bytes 2752512 | tf_op jit(solution)/shard_map/hidden_grad/pallas_call | solution.py:406
  282.2 19.1 %all-gather.11.cloned.1.call-done.refs_5_.refs_4_ = bf16[1024,2816]{1,0:T(8,128)(2,1)} async-done(((bf16[256,2816]{1,0:T(8,128)(2,1)}), bf16[1024,2816]{1,0:T(8,128)(2,1)}) %all-gather.11.cloned.1.call-update) | async-done | bytes 5767184 | tf_op jit(solution)/shard_map/all_gather | solution.py:620
  301.3 24.9 %gated.1 = (bf16[1280,1408]{1,0:T(8,128)(2,1)S(1)}, bf16[1280,1408]{1,0:T(8,128)(2,1)S(1)}, bf16[1280,1408]{1,0:T(8,128)(2,1)S(1)}) custom-call(bf16[640,2048]{1,0:T(8,128)(2,1)} %get-tuple-element.87.refs_0_.near_rows, bf16[640,2048]{1,0:T(8,128)(2,1)} %collective-permute-done.11.refs_1_.far_rows, bf16[1280,1408]{1,0:T(8,128)(2,1)} %copy-done.42, ...), custom_call_target="tpu_custom_call" | custom-call | flops 3690987520 | bytes 4194304 | tf_op jit(solution)/shard_map/gated/pallas_call | solution.py:463
  328.0 7.7 %grad_up_late.3 = bf16[1024,1408]{1,0:T(8,128)(2,1)S(1)} custom-call(bf16[640,2048]{1,0:T(8,128)(2,1)} %get-tuple-element.87.refs_0_.near_rows, bf16[640,2048]{1,0:T(8,128)(2,1)} %collective-permute-done.11.refs_1_.far_rows, bf16[1280,1408]{1,0:T(8,128)(2,1)S(1)} %get-tuple-element.106.refs_0_.refs_3_), custom_call_target="tpu_custom_call" | custom-call | flops 922746880 | bytes 1556480 | tf_op jit(solution)/shard_map/grad_up_late/pallas_call | solution.py:562
  335.7 6.5 grad_up_late.2
  342.3 2.8 pad_maximum_fusion
  348.9 6.7 grad_down.2
  358.3 11.0 %normed_ff_grad_far.1 = bf16[640,2048]{1,0:T(8,128)(2,1)S(1)} custom-call(bf16[1280,1408]{1,0:T(8,128)(2,1)S(1)} %copy-done.10, bf16[1024,1408]{1,0:T(8,128)(2,1)} %all-gather.9.cloned.1.call-done.refs_3_.refs_1_, bf16[1024,1408]{1,0:T(8,128)(2,1)} %collective-permute-done.12.refs_4_.refs_2_, bf16[1280,1408]{1,0:T(8,128)(2,1)S(1)} %copy-done.12, ...), custom_call_target="tpu_custom_call" | custom-call | flops 1845493760 | bytes 6127616 | tf_op jit(solution)/shard_map/normed_ff_grad_far/pallas_call | solution.py:530
  371.0 6.5 grad_gate.2
  383.2 14.2 %normed_ff_grad_near.1.mine = bf16[640,2048]{1,0:T(8,128)(2,1)S(1)} custom-call(bf16[1280,1408]{1,0:T(8,128)(2,1)S(1)} %copy-done.10, bf16[1024,1408]{1,0:T(8,128)(2,1)} %all-gather.9.cloned.1.call-done.refs_3_.refs_1_, bf16[1024,1408]{1,0:T(8,128)(2,1)} %collective-permute-done.12.refs_4_.refs_2_, bf16[1280,1408]{1,0:T(8,128)(2,1)S(1)} %copy-done.12, ...), custom_call_target="tpu_custom_call" | custom-call | flops 1845493760 | bytes 6782976 | tf_op jit(solution)/shard_map/normed_ff_grad_near/pallas_call | solution.py:530
  399.0 6.8 grad_down.3
  405.8 6.5 grad_gate.3
  413.9 20.6 %collective-permute-done.17 = bf16[1024,1408]{1,0:T(8,128)(2,1)} collective-permute-done((bf16[1024,1408]{1,0:T(8,128)(2,1)S(1)}, bf16[1024,1408]{1,0:T(8,128)(2,1)}, u32[]{:S(2)}, u32[]{:S(2)}) %collective-permute-start.17) | collective-permute-done | bytes 2883616 | tf_op jit(solution)/shard_map/ppermute | solution.py:611
  434.4 22.0 %collective-permute-done.16.got = bf16[640,2048]{1,0:T(8,128)(2,1)S(1)} collective-permute-done((bf16[640,2048]{1,0:T(8,128)(2,1)S(1)}, bf16[640,2048]{1,0:T(8,128)(2,1)S(1)}, u32[]{:S(2)}, u32[]{:S(2)}) %collective-permute-start.16) | collective-permute-done | bytes 2621472 | tf_op jit(solution)/shard_map/ppermute | solution.py:614
  458.0 4.2 add_convert_fusion.1
  470.4 3.7 middle_back.1
  476.9 4.4 collective-permute-done.18.refs_1_.far_rows
  484.6 3.3 mixed_grad.1.operands_2_
  488.0 16.0 %attend_back.1 = (bf16[640,768]{1,0:T(8,128)(2,1)S(1)}, bf16[640,768]{1,0:T(8,128)(2,1)S(1)}) custom-call(s32[14]{0:T(128)S(1)} %concatenate.36.operands_0_, bf16[1280,768]{1,0:T(8,128)(2,1)S(1)} %copy-done.88, bf16[1280,512]{1,0:T(8,128)(2,1)S(1)} %mixed_grad.1.operands_2_, f32[1280,128]{1,0:T(8,128)S(1)} %copy-done.79, f32[1280,128]{1,0:T(8,128)S(1)} %copy-done.81), custom_call_target="tpu_custom_call" | custom-call | flops 2214592512 | bytes 1966080 | tf_op jit(solution)/shard_map/attend_back/pallas_call | solution.py:826
  504.0 3.1 grad_joint.2
  508.3 33.2 %collective-permute-done.19 = bf16[1024,1408]{1,0:T(8,128)(2,1)} collective-permute-done((bf16[1024,1408]{1,0:T(8,128)(2,1)S(1)}, bf16[1024,1408]{1,0:T(8,128)(2,1)}, u32[]{:S(2)}, u32[]{:S(2)}) %collective-permute-start.19) | collective-permute-done | bytes 2883616 | tf_op jit(solution)/shard_map/ppermute | solution.py:611
  541.4 5.0 add_convert_fusion
  557.2 48.0 %collective-permute-done.22 = bf16[1024,512]{1,0:T(8,128)(2,1)S(1)} collective-permute-done((bf16[1024,512]{1,0:T(8,128)(2,1)}, bf16[1024,512]{1,0:T(8,128)(2,1)S(1)}, u32[]{:S(2)}, u32[]{:S(2)}) %collective-permute-start.22) | collective-permute-done | bytes 1048608 | tf_op jit(solution)/shard_map/ppermute | solution.py:611
  605.6 3.1 grad_joint.3
  617.7 5.1 branch_far.1
  623.0 3.1 normed_grad_far.1
  627.8 5.4 branch_near.1.mine
  635.7 9.1 %collective-permute-done.24 = bf16[256,1408]{1,0:T(8,128)(2,1)S(1)} collective-permute-done((bf16[256,1408]{1,0:T(8,128)(2,1)S(1)}, bf16[256,1408]{1,0:T(8,128)(2,1)S(1)}, u32[]{:S(2)}, u32[]{:S(2)}) %collective-permute-start.24) | collective-permute-done | bytes 720928 | tf_op jit(solution)/shard_map/ppermute | solution.py:611
  646.2 3.3 normed_grad_near.1.mine
  656.2 4.1 reduce-scatter.9.cloned.1.call-done
  673.1 20.6 %collective-permute-done.21.got = bf16[320,2048]{1,0:T(8,128)(2,1)} collective-permute-done((bf16[320,2048]{1,0:T(8,128)(2,1)}, bf16[320,2048]{1,0:T(8,128)(2,1)}, u32[]{:S(2)}, u32[]{:S(2)}) %collective-permute-start.21) | collective-permute-done | bytes 1310752 | tf_op jit(solution)/shard_map/ppermute | solution.py:614
  696.2 4.0 input_grad.1
  (306 shorter events, 142.0 us)
Async XLA Ops:
  7.2 68.2 %all-gather.5.cloned.1.call-start = ((), (), s32[]{:S(2)}) async-start(), calls=%async_computation.4 | async-start | bytes 3604480 | tf_op jit(solution)/shard_map/all_gather | solution.py:620
  13.4 121.0 %all-gather.7.cloned.1.call-start = ((), (), s32[]{:S(2)}) async-start(), calls=%async_computation.5 | async-start | bytes 3604480 | tf_op jit(solution)/shard_map/all_gather | solution.py:620
  14.2 188.4 %all-gather.9.cloned.1.call-start = ((), (), s32[]{:S(2)}) async-start(), calls=%async_computation.6 | async-start | bytes 3604480 | tf_op jit(solution)/shard_map/all_gather | solution.py:620
  14.2 32.2 %collective-permute-start = (bf16[320,2048]{1,0:T(8,128)(2,1)}, bf16[320,2048]{1,0:T(8,128)(2,1)}, u32[]{:S(2)}, u32[]{:S(2)}) collective-permute-start(bf16[320,2048]{1,0:T(8,128)(2,1)} %rows.1), channel_id=1, source_target_pairs={{0,2},{2,0},{1,3},{3,1},{4,6},{6,4},{5,7},{7,5},{8,10},{10,8},{9,1... | collective-permute-start | bytes 3932168 | tf_op jit(solution)/shard_map/ppermute | solution.py:614
  17.2 17.6 %collective-permute-start.2 = (bf16[256,1408]{1,0:T(8,128)(2,1)S(1)}, bf16[256,1408]{1,0:T(8,128)(2,1)S(1)}, u32[]{:S(2)}, u32[]{:S(2)}) collective-permute-start(bf16[256,1408]{1,0:T(8,128)(2,1)S(1)} %copy-done.89), channel_id=1, source_target_pairs={{4,0},{0,4},{5,1},{1,5},{6,2},{2,6},{7,3},{3,7},{12,8},{8,12},{13,... | collective-permute-start | bytes 2162696 | tf_op jit(solution)/shard_map/ppermute | solution.py:611
  18.7 27.6 %collective-permute-start.1 = (f32[320]{0:T(512)S(1)}, f32[320]{0:T(512)S(1)}, u32[]{:S(2)}, u32[]{:S(2)}) collective-permute-start(f32[320]{0:T(512)S(1)} %subtract_convert_fusion), channel_id=1, source_target_pairs={{0,2},{2,0},{1,3},{3,1},{4,6},{6,4},{5,7},{7,5},{8,10},{10,8},{9,1... | collective-permute-start | bytes 3848 | tf_op jit(solution)/shard_map/ppermute | solution.py:614
  47.8 31.7 %copy-start.35 = (bf16[640,2048]{1,0:T(8,128)(2,1)}, bf16[640,2048]{1,0:T(8,128)(2,1)S(1)}, u32[]{:S(2)}) copy-start(bf16[640,2048]{1,0:T(8,128)(2,1)S(1)} %constant_dynamic-update-slice_fusion.rows) | copy-start | bytes 7864324
  47.8 5.1 collective-permute-start.3
  47.9 253.4 %all-gather.11.cloned.1.call-start = ((), (), s32[]{:S(2)}) async-start(), calls=%async_computation.7 | async-start | bytes 7208960 | tf_op jit(solution)/shard_map/all_gather | solution.py:620
  48.0 31.6 %collective-permute-start.5 = (bf16[320,2048]{1,0:T(8,128)(2,1)}, bf16[320,2048]{1,0:T(8,128)(2,1)}, u32[]{:S(2)}, u32[]{:S(2)}) collective-permute-start(bf16[320,2048]{1,0:T(8,128)(2,1)} %param.25), channel_id=1, source_target_pairs={{0,2},{2,0},{1,3},{3,1},{4,6},{6,4},{5,7},{7,5},{8,10},{10,8},{9,1... | collective-permute-start | bytes 3932168 | tf_op jit(solution)/shard_map/ppermute | solution.py:614
  75.4 64.7 %collective-permute-start.4 = (bf16[1024,1408]{0,1:T(8,128)(2,1)}, bf16[1024,1408]{0,1:T(8,128)(2,1)}, u32[]{:S(2)}, u32[]{:S(2)}) collective-permute-start(bf16[1024,1408]{0,1:T(8,128)(2,1)} %all-gather.5.cloned.1.call-done), channel_id=1, source_target_pairs={{4,0},{0,4},{5,1},{1,5},{6,2},{2,6},{7,3},{3,7},{12,8},{8,12},{13,... | collective-permute-start | bytes 8650760 | tf_op jit(solution)/shard_map/ppermute | solution.py:611
  85.6 5.1 collective-permute-start.6
  89.8 451.6 %reduce-scatter.5.cloned.1.call-start = ((), (), s32[]{:S(2)}) async-start(), calls=%async_computation.8 | async-start | bytes 7208960 | tf_op jit(solution)/shard_map/reduce_scatter | solution.py:623
  149.8 32.6 %collective-permute-start.7 = (bf16[512,1408]{1,0:T(8,128)(2,1)S(1)}, bf16[512,1408]{1,0:T(8,128)(2,1)S(1)}, u32[]{:S(2)}, u32[]{:S(2)}) collective-permute-start(bf16[512,1408]{1,0:T(8,128)(2,1)S(1)} %slice.70), channel_id=1, source_target_pairs={{4,0},{0,4},{5,1},{1,5},{6,2},{2,6},{7,3},{3,7},{12,8},{8,12},{13,... | collective-permute-start | bytes 4325384 | tf_op jit(solution)/shard_map/ppermute | solution.py:611
  158.7 23.7 %copy-start.78 = (f32[1280,128]{1,0:T(8,128)S(1)}, f32[1280,128]{1,0:T(8,128)}, u32[]{:S(2)}) copy-start(f32[1280,128]{1,0:T(8,128)} %get-tuple-element.157.operands_2_.operands_3_) | copy-start | bytes 1966084
  158.7 23.7 %copy-start.80 = (f32[1280,128]{1,0:T(8,128)S(1)}, f32[1280,128]{1,0:T(8,128)}, u32[]{:S(2)}) copy-start(f32[1280,128]{1,0:T(8,128)} %get-tuple-element.158.operands_3_.operands_4_) | copy-start | bytes 1966084
  194.9 5.0 collective-permute-start.8
  202.6 59.1 %copy-start.37 = (bf16[640,2048]{1,0:T(8,128)(2,1)S(1)}, bf16[640,2048]{1,0:T(8,128)(2,1)}, u32[]{:S(2)}) copy-start(bf16[640,2048]{1,0:T(8,128)(2,1)} %copy-done.35) | copy-start | bytes 7864324
  202.6 59.1 %collective-permute-start.9 = (bf16[640,2048]{1,0:T(8,128)(2,1)}, bf16[640,2048]{1,0:T(8,128)(2,1)S(1)}, u32[]{:S(2)}, u32[]{:S(2)}) collective-permute-start(bf16[640,2048]{1,0:T(8,128)(2,1)} %add_convert_fusion.2.mine), channel_id=1, source_target_pairs={{0,2},{2,0},{1,3},{3,1},{4,6},{6,4},{5,7},{7,5},{8,10},{10,8},{9,1... | collective-permute-start | bytes 7864328 | tf_op jit(solution)/shard_map/ppermute | solution.py:614
  205.8 34.5 %collective-permute-start.10 = (bf16[512,1408]{1,0:T(8,128)(2,1)S(1)}, bf16[512,1408]{1,0:T(8,128)(2,1)S(1)}, u32[]{:S(2)}, u32[]{:S(2)}) collective-permute-start(bf16[512,1408]{1,0:T(8,128)(2,1)S(1)} %slice.71), channel_id=1, source_target_pairs={{4,0},{0,4},{5,1},{1,5},{6,2},{2,6},{7,3},{3,7},{12,8},{8,12},{13,... | collective-permute-start | bytes 4325384 | tf_op jit(solution)/shard_map/ppermute | solution.py:611
  207.3 94.0 %collective-permute-start.12 = (bf16[1024,1408]{1,0:T(8,128)(2,1)}, bf16[1024,1408]{1,0:T(8,128)(2,1)}, u32[]{:S(2)}, u32[]{:S(2)}) collective-permute-start(bf16[1024,1408]{1,0:T(8,128)(2,1)} %all-gather.9.cloned.1.call-done.refs_3_.refs_1_), channel_id=1, source_target_pairs={{4,0},{0,4},{5,1},{1,5},{6,2},{2,6},{7,3},{3,7},{12,8},{8,12},{13,... | collective-permute-start | bytes 8650760 | tf_op jit(solution)/shard_map/ppermute | solution.py:611
  207.9 61.7 %copy-start.13 = (bf16[1024,1408]{1,0:T(8,128)(2,1)S(1)}, bf16[1024,1408]{1,0:T(8,128)(2,1)}, u32[]{:S(2)}) copy-start(bf16[1024,1408]{1,0:T(8,128)(2,1)} %all-gather.7.cloned.1.call-done.refs_2_.refs_1_) | copy-start | bytes 8650756
  207.9 61.7 %copy-start.17 = (bf16[640,2048]{1,0:T(8,128)(2,1)S(1)}, bf16[640,2048]{1,0:T(8,128)(2,1)}, u32[]{:S(2)}) copy-start(bf16[640,2048]{1,0:T(8,128)(2,1)} %copy-done.16) | copy-start | bytes 7864324
  208.0 61.7 %copy-start.44 = (bf16[512,1408]{1,0:T(8,128)(2,1)S(1)}, bf16[512,1408]{1,0:T(8,128)(2,1)}, u32[]{:S(2)}) copy-start(bf16[512,1408]{1,0:T(8,128)(2,1)} %copy-done.43) | copy-start | bytes 4325380
  240.4 29.3 %copy-start.47 = (bf16[512,1408]{1,0:T(8,128)(2,1)}, bf16[512,1408]{1,0:T(8,128)(2,1)S(1)}, u32[]{:S(2)}) copy-start(bf16[512,1408]{1,0:T(8,128)(2,1)S(1)} %collective-permute-done.10.refs_4_.refs_3_) | copy-start | bytes 4325380
  269.6 31.6 %collective-permute-start.11 = (bf16[640,2048]{1,0:T(8,128)(2,1)}, bf16[640,2048]{1,0:T(8,128)(2,1)}, u32[]{:S(2)}, u32[]{:S(2)}) collective-permute-start(bf16[640,2048]{1,0:T(8,128)(2,1)} %get-tuple-element.87.refs_0_.near_rows), channel_id=1, source_target_pairs={{0,1},{1,0},{2,3},{3,2},{4,5},{5,4},{6,7},{7,6},{8,9},{9,8},{10,11... | collective-permute-start | bytes 7864328 | tf_op jit(solution)/shard_map/ppermute | solution.py:614
  345.1 265.6 %reduce-scatter.7.cloned.1.call-start = ((), (), s32[]{:S(2)}) async-start(), calls=%async_computation.9 | async-start | bytes 3604480 | tf_op jit(solution)/shard_map/reduce_scatter | solution.py:623
  369.4 9.7 %collective-permute-start.13 = (bf16[640,2048]{1,0:T(8,128)(2,1)S(1)}, bf16[640,2048]{1,0:T(8,128)(2,1)S(1)}, u32[]{:S(2)}, u32[]{:S(2)}) collective-permute-start(bf16[640,2048]{1,0:T(8,128)(2,1)S(1)} %normed_ff_grad_far.1), channel_id=1, source_target_pairs={{0,1},{1,0},{2,3},{3,2},{4,5},{5,4},{6,7},{7,6},{8,9},{9,8},{10,11... | collective-permute-start | bytes 7864328 | tf_op jit(solution)/shard_map/ppermute | solution.py:614
  369.5 65.0 %collective-permute-start.17 = (bf16[1024,1408]{1,0:T(8,128)(2,1)S(1)}, bf16[1024,1408]{1,0:T(8,128)(2,1)}, u32[]{:S(2)}, u32[]{:S(2)}) collective-permute-start(bf16[1024,1408]{1,0:T(8,128)(2,1)S(1)} %grad_down.2), channel_id=1, source_target_pairs={{4,0},{0,4},{5,1},{1,5},{6,2},{2,6},{7,3},{3,7},{12,8},{8,12},{13,... | collective-permute-start | bytes 8650760 | tf_op jit(solution)/shard_map/ppermute | solution.py:611
  397.5 59.0 %collective-permute-start.16 = (bf16[640,2048]{1,0:T(8,128)(2,1)S(1)}, bf16[640,2048]{1,0:T(8,128)(2,1)S(1)}, u32[]{:S(2)}, u32[]{:S(2)}) collective-permute-start(bf16[640,2048]{1,0:T(8,128)(2,1)S(1)} %normed_ff_grad_near.1.mine), channel_id=1, source_target_pairs={{0,2},{2,0},{1,3},{3,1},{4,6},{6,4},{5,7},{7,5},{8,10},{10,8},{9,1... | collective-permute-start | bytes 7864328 | tf_op jit(solution)/shard_map/ppermute | solution.py:614
  462.2 191.4 %reduce-scatter.11.cloned.1.call-start = ((), (), s32[]{:S(2)}) async-start(), calls=%async_computation.11 | async-start | bytes 3604480 | tf_op jit(solution)/shard_map/reduce_scatter | solution.py:623
  476.4 4.9 collective-permute-start.18
  476.4 65.0 %collective-permute-start.19 = (bf16[1024,1408]{1,0:T(8,128)(2,1)S(1)}, bf16[1024,1408]{1,0:T(8,128)(2,1)}, u32[]{:S(2)}, u32[]{:S(2)}) collective-permute-start(bf16[1024,1408]{1,0:T(8,128)(2,1)S(1)} %copy-done.69), channel_id=1, source_target_pairs={{4,0},{0,4},{5,1},{1,5},{6,2},{2,6},{7,3},{3,7},{12,8},{8,12},{13,... | collective-permute-start | bytes 8650760 | tf_op jit(solution)/shard_map/ppermute | solution.py:611
  546.5 113.8 %reduce-scatter.9.cloned.1.call-start = ((), (), s32[]{:S(2)}) async-start(), calls=%async_computation.10 | async-start | bytes 3276800 | tf_op jit(solution)/shard_map/reduce_scatter | solution.py:623
  546.5 62.1 %collective-permute-start.23 = (bf16[1024,768]{1,0:T(8,128)(2,1)}, bf16[1024,768]{1,0:T(8,128)(2,1)S(1)}, u32[]{:S(2)}, u32[]{:S(2)}) collective-permute-start(bf16[1024,768]{1,0:T(8,128)(2,1)} %copy-done.74), channel_id=1, source_target_pairs={{4,0},{0,4},{5,1},{1,5},{6,2},{2,6},{7,3},{3,7},{12,8},{8,12},{13,... | collective-permute-start | bytes 4718600 | tf_op jit(solution)/shard_map/ppermute | solution.py:611
  547.0 58.2 %collective-permute-start.22 = (bf16[1024,512]{1,0:T(8,128)(2,1)}, bf16[1024,512]{1,0:T(8,128)(2,1)S(1)}, u32[]{:S(2)}, u32[]{:S(2)}) collective-permute-start(bf16[1024,512]{1,0:T(8,128)(2,1)} %copy-done.77), channel_id=1, source_target_pairs={{4,0},{0,4},{5,1},{1,5},{6,2},{2,6},{7,3},{3,7},{12,8},{8,12},{13,... | collective-permute-start | bytes 3145736 | tf_op jit(solution)/shard_map/ppermute | solution.py:611
  554.7 50.8 %copy-start.25 = (bf16[640,2048]{1,0:T(8,128)(2,1)S(1)}, bf16[640,2048]{1,0:T(8,128)(2,1)}, u32[]{:S(2)}) copy-start(bf16[640,2048]{1,0:T(8,128)(2,1)} %copy-done.23) | copy-start | bytes 7864324
  554.7 50.8 %copy-start.55 = (bf16[640,768]{1,0:T(8,128)(2,1)S(1)}, bf16[640,768]{1,0:T(8,128)(2,1)}, u32[]{:S(2)}) copy-start(bf16[640,768]{1,0:T(8,128)(2,1)} %copy-done.54) | copy-start | bytes 2949124
  554.7 50.8 %copy-start.58 = (bf16[640,768]{1,0:T(8,128)(2,1)S(1)}, bf16[640,768]{1,0:T(8,128)(2,1)}, u32[]{:S(2)}) copy-start(bf16[640,768]{1,0:T(8,128)(2,1)} %copy-done.57) | copy-start | bytes 2949124
  557.2 48.4 %copy-start.22 = (bf16[640,2048]{1,0:T(8,128)(2,1)S(1)}, bf16[640,2048]{1,0:T(8,128)(2,1)}, u32[]{:S(2)}) copy-start(bf16[640,2048]{1,0:T(8,128)(2,1)} %copy-done.20) | copy-start | bytes 7864324
  622.8 5.0 collective-permute-start.14
  626.1 20.1 %collective-permute-start.20 = (bf16[640,2048]{1,0:T(8,128)(2,1)S(1)}, bf16[640,2048]{1,0:T(8,128)(2,1)S(1)}, u32[]{:S(2)}, u32[]{:S(2)}) collective-permute-start(bf16[640,2048]{1,0:T(8,128)(2,1)S(1)} %normed_grad_far.1), channel_id=1, source_target_pairs={{0,1},{1,0},{2,3},{3,2},{4,5},{5,4},{6,7},{7,6},{8,9},{9,8},{10,11... | collective-permute-start | bytes 7864328 | tf_op jit(solution)/shard_map/ppermute | solution.py:614
  626.7 18.1 %collective-permute-start.24 = (bf16[256,1408]{1,0:T(8,128)(2,1)S(1)}, bf16[256,1408]{1,0:T(8,128)(2,1)S(1)}, u32[]{:S(2)}, u32[]{:S(2)}) collective-permute-start(bf16[256,1408]{1,0:T(8,128)(2,1)S(1)} %slice.80), channel_id=1, source_target_pairs={{4,0},{0,4},{5,1},{1,5},{6,2},{2,6},{7,3},{3,7},{12,8},{8,12},{13,... | collective-permute-start | bytes 2162696 | tf_op jit(solution)/shard_map/ppermute | solution.py:611
  634.4 32.3 %collective-permute-start.15 = (bf16[320,2048]{1,0:T(8,128)(2,1)}, bf16[320,2048]{1,0:T(8,128)(2,1)}, u32[]{:S(2)}, u32[]{:S(2)}) collective-permute-start(bf16[320,2048]{1,0:T(8,128)(2,1)} %slice.90), channel_id=1, source_target_pairs={{0,2},{2,0},{1,3},{3,1},{4,6},{6,4},{5,7},{7,5},{8,10},{10,8},{9,1... | collective-permute-start | bytes 3932168 | tf_op jit(solution)/shard_map/ppermute | solution.py:614
  652.3 41.3 %collective-permute-start.21 = (bf16[320,2048]{1,0:T(8,128)(2,1)}, bf16[320,2048]{1,0:T(8,128)(2,1)}, u32[]{:S(2)}, u32[]{:S(2)}) collective-permute-start(bf16[320,2048]{1,0:T(8,128)(2,1)} %slice.91), channel_id=1, source_target_pairs={{0,2},{2,0},{1,3},{3,1},{4,6},{6,4},{5,7},{7,5},{8,10},{10,8},{9,1... | collective-permute-start | bytes 3932168 | tf_op jit(solution)/shard_map/ppermute | solution.py:614
  663.9 1.2 collective-permute-start.25
  665.2 35.0 %collective-permute-start.26 = (f32[2,256]{1,0:T(2,128)S(1)}, f32[2,256]{1,0:T(2,128)S(1)}, u32[]{:S(2)}, u32[]{:S(2)}) collective-permute-start(f32[2,256]{1,0:T(2,128)S(1)} %fusion.19), channel_id=1, source_target_pairs={{0,2},{2,0},{1,3},{3,1},{4,6},{6,4},{5,7},{7,5},{8,10},{10,8},{9,1... | collective-permute-start | bytes 6152 | tf_op jit(solution)/shard_map/ppermute | solution.py:614
  669.2 24.4 %copy-start.39 = (bf16[640,2048]{1,0:T(8,128)(2,1)S(1)}, bf16[640,2048]{1,0:T(8,128)(2,1)}, u32[]{:S(2)}) copy-start(bf16[640,2048]{1,0:T(8,128)(2,1)} %copy-done.38) | copy-start | bytes 7864324
  (84 other events, 429.4 us)
Sparse Core Ops, SparseCore 0:
  13.5 61.8 all-gather.4
  77.0 57.3 all-gather.6
  135.9 57.8 all-gather.8
  195.8 105.3 all-gather.10
  345.2 100.5 reduce-scatter.4
  462.3 53.4 reduce-scatter.6
  546.6 53.4 reduce-scatter.10
  610.8 49.3 reduce-scatter.8

commit v2 on v1

--- a/solution.py
+++ b/solution.py
@@ -258,6 +258,10 @@
     return jax.ShapeDtypeStruct((rows, columns), kind)
 
 
+def in_hbm(rows, columns, kind):
+    return pltpu.HBM((rows, columns), kind)
+
+
 def runs(order, width):
     run = width // order.shape[0]
     for j in range(order.shape[0]):
@@ -303,6 +307,17 @@
         at += weight.shape[1]
     rows = jnp.concatenate([gains[...], jnp.zeros((HD - gains.shape[0], gains.shape[1]), f32)])
     result[:, at:] = rows.T.astype(bf16)
+
+
+def gains_kernel(*refs):
+    slots, first, second = refs[:-2], refs[-2], refs[-1]
+    at = 0
+    for slot in slots:
+        columns = slot[...].astype(f32).T
+        here = slice(at, at + slot.shape[0])
+        first[:, here] = columns[0:1, :]
+        second[:, here] = columns[1:2, :]
+        at += slot.shape[0]
 
 
 def kept_kernel(order, rows, keep, result):
@@ -415,47 +430,72 @@
     )(near, far, *weights)
 
 
-def gated(rows, hidden_grad, gates, ups):
+def gate_product(rows, hidden_grad, gates):
+    near, far = rows
+    length, units = hidden_grad.shape
+    width = near.shape[1]
+
+    def kernel(*refs):
+        hidden_back, slots = refs[2], refs[3:-2]
+        gate_out, up_grad = refs[-2:]
+
+        def work(side):
+            for cut in column_cuts(units):
+                gate = product(refs[side], slots, cut)
+                gate_out[:, cut] = gate
+                active = gate / (1.0 + jnp.exp(-gate))
+                up_grad[:, cut] = (hidden_back[:, cut].astype(f32) * active).astype(bf16)
+
+        in_halves(4, work)
+
+    here = spec((length // 4, units), lambda i: (i, 0))
+    return pl.pallas_call(
+        kernel,
+        grid=(4,),
+        in_specs=of_group(near, far, 4) + [here] + resident(gates),
+        out_specs=[here] * 2,
+        out_shape=[in_hbm(length, units, f32), shaped(length, units, bf16)],
+        compiler_params=pltpu.CompilerParams(vmem_limit_bytes=VMEM),
+        cost_estimate=cost(2 * length * width * units, 2 * width * (length + units)),
+        name="gate",
+    )(near, far, hidden_grad, *gates)
+
+
+def up_product(rows, hidden_grad, gate, ups):
     near, far = rows
     length, units = hidden_grad.shape
     width = near.shape[1]
     up_slots = [slot for slots, _, _ in ups for slot in slots]
-    count = len(gates)
 
     def kernel(*refs):
-        hidden_back, gate_refs = refs[2], refs[3 : 3 + count]
-        up_refs = refs[3 + count : -3]
-        hidden, gate_grad, up_grad = refs[-3:]
+        hidden_back, gate_in = refs[2], refs[3]
+        up_refs = refs[4:-2]
+        hidden, gate_grad = refs[-2:]
 
         def work(side):
-            at = 0
+            rows_in, at = refs[side], 0
             for slots, first, columns in ups:
                 mine = up_refs[at : at + len(slots)]
                 at += len(slots)
                 for inside in column_cuts(columns.stop - columns.start):
                     cut = slice(first + inside.start, first + inside.stop)
                     there = slice(columns.start + inside.start, columns.start + inside.stop)
-                    gate = product(refs[side], gate_refs, cut)
-                    if len(slots) == 1 and count > 1:
+                    if len(slots) == 1 and mine[0].shape[0] < width:
+                        depth = mine[0].shape[0]
+                        count = width // depth
                         step = mine[0].shape[1] // count
-                        views = [
-                            mine[0][:, slice(there.start + s * step, there.stop + s * step)]
-                            for s in range(count)
-                        ]
-                        half = mine[0].shape[0]
-                        upward = dot_nn(refs[side][:, :half], views[0])
-                        for s in range(1, count):
-                            rows_s = refs[side][:, s * half : (s + 1) * half]
-                            upward = upward + dot_nn(rows_s, views[s])
+                        upward = None
+                        for s in range(count):
+                            view = mine[0][:, there.start + s * step : there.stop + s * step]
+                            term = dot_nn(rows_in[:, s * depth : (s + 1) * depth], view)
+                            upward = term if upward is None else upward + term
                     else:
-                        upward = product(refs[side], mine, there)
-                    back = hidden_back[:, cut].astype(f32)
-                    sigma = 1.0 / (1.0 + jnp.exp(-gate))
-                    active = gate * sigma
-                    hidden[:, cut] = (active * upward).astype(bf16)
-                    slope = sigma * (1.0 + gate * (1.0 - sigma))
-                    gate_grad[:, cut] = (back * upward * slope).astype(bf16)
-                    up_grad[:, cut] = (back * active).astype(bf16)
+                        upward = product(rows_in, mine, there)
+                    value = gate_in[:, cut]
+                    sigma = 1.0 / (1.0 + jnp.exp(-value))
+                    back = hidden_back[:, cut].astype(f32) * upward * sigma
+                    hidden[:, cut] = (value * sigma * upward).astype(bf16)
+                    gate_grad[:, cut] = (back * (1.0 + value * (1.0 - sigma))).astype(bf16)
 
         in_halves(4, work)
 
@@ -463,13 +503,13 @@
     return pl.pallas_call(
         kernel,
         grid=(4,),
-        in_specs=of_group(near, far, 4) + [here] + resident(list(gates) + up_slots),
-        out_specs=[here] * 3,
-        out_shape=[shaped(length, units, bf16)] * 3,
+        in_specs=of_group(near, far, 4) + [here, here] + resident(up_slots),
+        out_specs=[here] * 2,
+        out_shape=[shaped(length, units, bf16)] * 2,
         compiler_params=pltpu.CompilerParams(vmem_limit_bytes=VMEM),
-        cost_estimate=cost(4 * length * width * units, 2 * width * (length + 2 * units)),
-        name="gated",
-    )(near, far, hidden_grad, *gates, *up_slots)
+        cost_estimate=cost(2 * length * width * units, 2 * width * (length + units)),
+        name="up",
+    )(near, far, hidden_grad, gate, *up_slots)
 
 
 def back_rows(grads, weights, side, name, far=None):
@@ -539,36 +579,82 @@
     )(*operands)
 
 
-def weight_part(rows, grads, half, s, name, columns=None):
+def grad_terms(near, far, refs, columns, pair):
+    count = near.shape[0]
+    if pair:
+        first, second = refs[0][:, columns], refs[1][:, columns]
+    else:
+        first, second = refs[0][:count, columns], refs[0][count:, columns]
+    return (dot_tn(near[...], first) + dot_tn(far[...], second)).astype(bf16)
+
+
+def weight_part(rows, grads, half, s, name, columns=None, parts=1):
     near, far = rows
     pair = isinstance(grads, tuple)
     units = grads[0].shape[1] if pair else grads.shape[1]
     columns = slice(0, units) if columns is None else columns
     wide = columns.stop - columns.start
-    tile = 512 if half % 512 == 0 else half
+    tile = min(512, half) if parts == 1 else half // 4
     tiles = half // tile
+    edges = [0, tiles] if parts == 1 else [0, 1, tiles]
     count = near.shape[0]
     row_spec = spec((count, tile), lambda j: (0, s * tiles + j))
+    operands = grads if pair else (grads,)
 
     def kernel(near_rows, far_rows, *refs):
-        if pair:
-            first, second = refs[0][:, columns], refs[1][:, columns]
-        else:
-            first, second = refs[0][:count, columns], refs[0][count:, columns]
-        total = dot_tn(near_rows[...], first) + dot_tn(far_rows[...], second)
-        refs[-1][...] = total.astype(bf16)
-
-    operands = grads if pair else (grads,)
-    return pl.pallas_call(
+        total = grad_terms(near_rows, far_rows, refs, columns, pair)
+        for part in range(parts):
+
+            @pl.when((pl.program_id(0) >= edges[part]) & (pl.program_id(0) < edges[part + 1]))
+            def _(part=part):
+                refs[len(operands) + part][...] = total
+
+    found = pl.pallas_call(
         kernel,
         grid=(tiles,),
         in_specs=[row_spec, row_spec] + [whole(operand.shape) for operand in operands],
-        out_specs=spec((tile, wide), lambda j: (j, 0)),
-        out_shape=shaped(half, wide, bf16),
+        out_specs=[
+            spec(
+                (tile, wide),
+                lambda j, part=part: (
+                    jnp.clip(j, edges[part], edges[part + 1] - 1) - edges[part],
+                    0,
+                ),
+            )
+            for part in range(parts)
+        ],
+        out_shape=[
+            in_hbm((edges[part + 1] - edges[part]) * tile, wide, bf16) for part in range(parts)
+        ],
         compiler_params=pltpu.CompilerParams(vmem_limit_bytes=VMEM),
         cost_estimate=cost(4 * count * half * wide, 4 * count * (half + wide)),
         name=name,
     )(near, far, *operands)
+    return found if parts > 1 else found[0]
+
+
+def weight_slots(rows, grads, half, name, columns):
+    near, far = rows
+    wide = columns.stop - columns.start
+    tile = min(512, half)
+    tiles = half // tile
+    inner = near.shape[1] // half
+    count = near.shape[0]
+    row_spec = spec((count, tile), lambda j: (0, j))
+
+    def kernel(near_rows, far_rows, *refs):
+        refs[-1][...] = grad_terms(near_rows, far_rows, refs, columns, False)
+
+    return pl.pallas_call(
+        kernel,
+        grid=(inner * tiles,),
+        in_specs=[row_spec, row_spec, whole(grads.shape)],
+        out_specs=spec((tile, wide), lambda j: (j % tiles, j // tiles)),
+        out_shape=in_hbm(half, inner * wide, bf16),
+        compiler_params=pltpu.CompilerParams(vmem_limit_bytes=VMEM),
+        cost_estimate=cost(4 * count * half * inner * wide, 4 * count * (half + wide)),
+        name=name,
+    )(near, far, grads)
 
 
 def make_body(outer, inner, rows_axis, cores_axis):
@@ -677,13 +763,21 @@
         packed_slots, near_branch, far_branch, down_own = fence(
             (packed_slots, near_branch, far_branch, down_own)
         )
-        down_first = from_inner(down_own[: half // 2], 1) if inner > 1 else None
+        quarter = half // 4
+        down_got = [from_inner(down_own[:quarter], 1)] if inner > 1 else []
         gain_at = joint_width + heads * HD
         joint_columns = slice(0, joint_width)
         output_columns = slice(joint_width, gain_at)
-        gains = [values[:, gain_at:].T[:2].astype(f32) for values in packed_slots]
-        gain_one = jnp.concatenate([values[0:1] for values in gains], axis=1)
-        gain_two = jnp.concatenate([values[1:2] for values in gains], axis=1)
+        gain_one, gain_two = pl.pallas_call(
+            gains_kernel,
+            grid=(1,),
+            in_specs=[spec((half, HD), lambda i: (0, gain_at // HD))] * inner,
+            out_specs=[whole((1, width))] * 2,
+            out_shape=[shaped(1, width, f32)] * 2,
+            compiler_params=pltpu.CompilerParams(vmem_limit_bytes=VMEM),
+            cost_estimate=cost(0, width * 8),
+            name="gains",
+        )(*packed_slots)
         all_branch = (near_branch, far_branch)
 
         def norm(rows, name):
@@ -699,11 +793,15 @@
 
         attend, attend_back = attention_calls(length, blocks, heads)
         raw = through(normed, packed_slots, "joint", joint_columns, f32)
-        weight_down = [down_own]
         if inner > 1:
-            raw, down_first, down_own = fence((raw, down_first, down_own))
-            weight_down = [down_own, down_first, from_inner(down_own[half // 2 :], 1)]
+            raw, down_got, down_own = fence((raw, down_got, down_own))
+            down_got = down_got + [from_inner(down_own[quarter : 2 * quarter], 1)]
         mixed_near, mixed_far, rotated = attend(table, raw, cosine, sine)
+        if inner > 1:
+            mixed_near, mixed_far, down_got, down_own = fence(
+                (mixed_near, mixed_far, down_got, down_own)
+            )
+            down_got = down_got + [from_inner(down_own[2 * quarter : 3 * quarter], 1)]
         mixed = (mixed_near, mixed_far)
 
         def packed_plan(columns):
@@ -713,10 +811,14 @@
         attended_far = swap(back_rows([mixed], attended_plan, 1, "attended_far"), "core")
         attended = back_rows([mixed], attended_plan, 0, "attended_near")
         attended = (attended.astype(f32) + attended_far.astype(f32)).astype(bf16)
-        attended, gate_own = fence((attended, gate_own))
+        attended, gate_own, down_got = fence((attended, gate_own, down_got))
+        if inner > 1:
+            down_got = down_got + [from_inner(down_own[3 * quarter :], 1)]
+        weight_down = [down_own] + down_got
         got = swap(attended, "row")
         weight_gate = spread(gate_own)
-        got, weight_down, up_own = fence((got, weight_down, up_own))
+        hidden_grad = through(all_branch, weight_down, "hidden_grad", slice(0, units), bf16)
+        got, hidden_grad, up_own = fence((got, hidden_grad, up_own))
         weight_up = spread(up_own) if early else []
         swapped = part // tile
         middle, normed_ff = row_call(
@@ -730,14 +832,12 @@
         )
         all_ff = (normed_ff, swap(normed_ff, "core"))
 
-        hidden_grad = through(all_branch, weight_down, "hidden_grad", slice(0, units), bf16)
         up_parts = [(weight_up, 0, slice(0, early))] if early else []
         up_plan = [(weight_up, 0, [slice(0, early)] * inner)] if early else []
         if late:
             up_parts.append((up_both, early, slice(0, late)))
             up_plan.append((up_both * inner, early, [slice(s * late, (s + 1) * late) for s in slots]))
-        hidden_ff, gate_grad, up_grad = gated(all_ff, hidden_grad, weight_gate, up_parts)
-
+        gate, up_grad = gate_product(all_ff, hidden_grad, weight_gate)
         def weight_parts(rows, grads, name, columns=None):
             return [weight_part(rows, grads, half, s, name, columns) for s in slots]
 
@@ -748,18 +848,17 @@
         last = inner - 1
         up_late_sums = None
         if late:
-            up_late_parts = weight_parts(all_ff, up_grad, "grad_up_late", slice(early, units))
-            gate_grad, up_grad, hidden_ff, up_late_parts = fence(
-                (gate_grad, up_grad, hidden_ff, up_late_parts)
-            )
-            up_late_sums = scatter(jnp.concatenate(up_late_parts, axis=1))
+            up_late_parts = weight_slots(all_ff, up_grad, half, "grad_up_late", slice(early, units))
+            gate, up_grad, up_late_parts = fence((gate, up_grad, up_late_parts))
+            up_late_sums = scatter(up_late_parts)
+        hidden_ff, gate_grad = up_product(all_ff, hidden_grad, gate, up_parts)
         down_last = weight_part(all_branch, hidden_ff, half, last, "grad_down")
         gate_grad, up_grad, down_last = fence((gate_grad, up_grad, down_last))
         back_plan = ([gate_grad, up_grad], [all_of(weight_gate), up_plan])
         ff_far = back_rows(*back_plan, 1, "normed_ff_grad_far")
         ff_far, gate_grad, up_grad = fence((ff_far, gate_grad, up_grad))
         ff_far = swap(ff_far, "core")
-        gate_last = weight_part(all_ff, gate_grad, half, last, "grad_gate")
+        gate_last = weight_part(all_ff, gate_grad, half, last, "grad_gate", parts=2)
         gate_grad, up_grad, gate_last = fence((gate_grad, up_grad, gate_last))
         back_plan = ([gate_grad, up_grad], [all_of(weight_gate), up_plan])
         ff_grad = back_rows(*back_plan, 0, "normed_ff_grad_near", ff_far)
@@ -774,12 +873,13 @@
                 return values
             return (values.astype(f32) + got.astype(f32)).astype(bf16)
 
-        down_got, gate_got = to_last(down_last), to_last(gate_last)
+        down_got = to_last(down_last)
+        gate_got = [to_last(values) for values in gate_last]
         up_last = up_got = None
         if early:
             up_last = weight_part(all_ff, up_grad, half, last, "grad_up", slice(0, early))
             up_got = to_last(up_last)
-        own = [down_last, gate_last, up_last]
+        own = [down_last, jnp.concatenate(gate_last, axis=0), up_last]
         if last:
             own = [
                 weight_part(all_branch, hidden_ff, half, 0, "grad_down"),
@@ -788,8 +888,15 @@
                 if early
                 else None,
             ]
-        ff_got, down_got, own, up_last = fence((ff_got, down_got, own, up_last))
-        grad_down = scatter(plus(own[0], down_got))
+        branch_plan = ([hidden_ff], [all_of(weight_down)])
+        branch_far = back_rows(*branch_plan, 1, "branch_far")
+        branch_near = back_rows(*branch_plan, 0, "branch_near")
+        down_own, down_got, own[1], branch_far, branch_near = fence(
+            (own[0], down_got, own[1], branch_far, branch_near)
+        )
+        down_sum = plus(down_own, down_got)
+        ff_got, own, up_last, gate_got[0] = fence((ff_got, own, up_last, gate_got[0]))
+        grad_down = scatter(down_sum)
         middle_grad, attended_grad = row_call(
             middle_back_kernel,
             "middle_back",
@@ -808,7 +915,35 @@
         )
         all_attended = (attended_grad, swap(attended_grad, "core"))
 
-        branch = core_sum([hidden_ff], [all_of(weight_down)], "branch")
+        mixed_grad = through(all_attended, packed_slots, "mixed_grad", output_columns, bf16)
+        output_last = weight_part(all_attended, mixed, half, last, "grad_output")
+        mixed_grad, output_last = fence((mixed_grad, output_last))
+        packed_grad = tuple(attend_back(table, rotated, mixed_grad, cosine, sine))
+        joint_last = weight_part(normed, packed_grad, half, last, "grad_joint")
+        packed_grad, gate_got, up_late_sums, joint_last = fence(
+            (packed_grad, gate_got, up_late_sums, joint_last)
+        )
+        gate_sums = own[1]
+        if last:
+            rows = half // 4
+            gate_sums = jnp.concatenate(
+                [plus(own[1][:rows], gate_got[0]), plus(own[1][rows:], gate_got[1])], axis=0
+            )
+        grad_gate = scatter(gate_sums)
+        normed_grad = core_sum([packed_grad], [packed_plan(joint_columns)], "normed_grad")
+        normed_got = swap(normed_grad[part:], "row")
+        output_sum, joint_sum = output_last, joint_last
+        if last:
+            output_own = weight_part(all_attended, mixed, half, 0, "grad_output")
+            joint_own = weight_part(normed, packed_grad, half, 0, "grad_joint")
+            output_own, joint_own, normed_grad = fence((output_own, joint_own, normed_grad))
+            output_got, joint_got = to_last(output_last), to_last(joint_last)
+            output_got, joint_got, normed_got, branch_far = fence(
+                (output_got, joint_got, normed_got, branch_far)
+            )
+            output_sum = plus(output_own, output_got)
+            joint_sum = plus(joint_own, joint_got)
+        branch = (branch_near.astype(f32) + swap(branch_far, "core").astype(f32)).astype(bf16)
         branch_got = swap(branch[part:], "row")
         (layer_out,) = row_call(
             layer_kernel,
@@ -819,35 +954,13 @@
             [(middle, 0), (keep, 0), (branch, 0), (branch_got, 0)],
             [(width, bf16)],
         )
-
-        mixed_grad = through(all_attended, packed_slots, "mixed_grad", output_columns, bf16)
-        output_last = weight_part(all_attended, mixed, half, last, "grad_output")
-        mixed_grad, output_last = fence((mixed_grad, output_last))
-        packed_grad = tuple(attend_back(table, rotated, mixed_grad, cosine, sine))
-        joint_last = weight_part(normed, packed_grad, half, last, "grad_joint")
-        packed_grad, gate_got, up_late_sums, joint_last = fence(
-            (packed_grad, gate_got, up_late_sums, joint_last)
-        )
-        grad_gate = scatter(plus(own[1], gate_got))
-        output_sum, joint_sum = output_last, joint_last
-        if last:
-            output_sum = plus(
-                weight_part(all_attended, mixed, half, 0, "grad_output"), to_last(output_last)
-            )
-            joint_sum = plus(
-                weight_part(normed, packed_grad, half, 0, "grad_joint"), to_last(joint_last)
-            )
         attention_sum = jnp.concatenate([output_sum, joint_sum], axis=1)
         grad_up = None
         if early:
             up_got, grad_down = fence((up_got, grad_down))
             grad_up = scatter(plus(own[2], up_got)).astype(f32)
         attention_sum, grad_down = fence((attention_sum, grad_down))
-        attention_sum = scatter(attention_sum).astype(f32)
-        grad_output = attention_sum[:, : heads * HD]
-        grad_joint = attention_sum[:, heads * HD :]
-        normed_grad = core_sum([packed_grad], [packed_plan(joint_columns)], "normed_grad")
-        normed_got = swap(normed_grad[part:], "row")
+        attention_sum = scatter(attention_sum)
         (input_grad,) = pl.pallas_call(
             input_kernel,
             grid=(part // tile,),
@@ -872,6 +985,11 @@
         grad_down, grad_gate, grad_up = [
             grad.astype(f32) for grad in (grad_down, grad_gate, grad_up)
         ]
+
+        attention_sum, input_grad, layer_out = fence((attention_sum, input_grad, layer_out))
+        attention_sum = attention_sum.astype(f32)
+        grad_output = attention_sum[:, : heads * HD]
+        grad_joint = attention_sum[:, heads * HD :]
 
         def gain_terms(pairs, gain):
             total = None

time: 717 us -> 654 us (0.912)
  waiting for transfers between devices: 359 us -> 291 us
  Pallas kernels: 190 us -> 218 us
  local copies, waits for them, and re-layouts: 85.6 us -> 61.4 us
    ppermute x10 -> x13, waiting for transfers between devices: 182 us -> 156 us  [from_inner(): lax.ppermute(values, 'inner', [((i + k) % inner, i) for i in range(inner)])]
    ppermute x17, waiting for transfers between devices: 86.8 us -> 61.1 us  [swap(): return lax.ppermute(values, axis, [(0, 1), (1, 0)])]
    all_gather x4, waiting for transfers between devices: 85.2 us -> 66.7 us  [gather(): return lax.all_gather(values, 'outer', axis=0, tiled=True)]
    unnamed x196 -> x208, local copies, waits for them, and re-layouts: 64.6 us -> 48 us
    pallas_call x1 -> x4, Pallas kernels: 24.9 us -> 37.5 us  [the longest x1 12.7 us: up_product(): pl.pallas_call(kernel, grid=(4,), in_specs=of_group(near, far, 4) + [here...]
    pallas_call x8, Pallas kernels: 47 us -> 59.6 us  [back_rows(): pl.pallas_call(kernel, grid=(width // tile,), in_specs=specs, out_specs=s...]
    optimization_barrier x2 -> x0, local copies, waits for them, and re-layouts: 8.08 us -> none  [body(): fence((packed_slots, near_branch, far_branch, down_own))]
    ppermute x10 -> x13, starting transfers between devices: 11 us -> 18 us  [from_inner(): lax.ppermute(values, 'inner', [((i + k) % inner, i) for i in range(inner)])]
  transfers between devices with their start and end apart: 35 -> 38, of which waited for: 23 -> 26; matrix products, arithmetic and copies ran while one was open for 7% -> 7% of each run, Pallas kernels for 21% -> 34%
where the time goes in v2:
time: 654 us; the launch traced here: 645 us
  waiting for transfers between devices  291 us (44%)
  Pallas kernels  218 us (33%)
  local copies, waits for them, and re-layouts  61.4 us (9%)
  other arithmetic  32 us (5%)
  starting transfers between devices  28.3 us (4%)
  between operations  15.5 us (2%)
    ppermute x13, waiting for transfers between devices, from_inner(): lax.ppermute(values, 'inner', [((i + k) % inner, i) for i in range(inner)])  156 us
    all_gather x4, waiting for transfers between devices, gather(): return lax.all_gather(values, 'outer', axis=0, tiled=True)  66.7 us
    ppermute x17, waiting for transfers between devices, swap(): return lax.ppermute(values, axis, [(0, 1), (1, 0)])  61.1 us
    pallas_call x8, Pallas kernels, back_rows(): pl.pallas_call(kernel, grid=(width // tile,), in_specs=specs, out_specs=s...  59.6 us
    unnamed x208, local copies, waits for them, and re-layouts  48 us
    pallas_call x8, Pallas kernels, weight_part(): pl.pallas_call(kernel, grid=(tiles,), in_specs=[row_spec, row_spec] + [wh...  46 us
    pallas_call x3, Pallas kernels, through(): pl.pallas_call(kernel, grid=(2,), in_specs=of_group(near, far, 2) + resid...  24.1 us
    pallas_call x6, Pallas kernels, row_call(): pl.pallas_call(kernel, grid=(rows // tile,), in_specs=[pl.BlockSpec(memor...  19.7 us
  transfers between devices with their start and end apart: 38, of which 26 were waited for; matrix products, arithmetic and copies ran while one was open for 7% of the time, Pallas kernels for 34%

profile of v2, /device:TPU:0, one launch (start us, length us, event | category | flops | bytes accessed | tf_op | source)
XLA Modules:
  0.0 645.2 jit_solution(297801624478184207)
XLA Ops:
  13.2 3.0 collective-permute-start.1
  19.8 14.3 %collective-permute-done.3 = bf16[256,1408]{1,0:T(8,128)(2,1)} collective-permute-done((bf16[256,1408]{1,0:T(8,128)(2,1)}, bf16[256,1408]{1,0:T(8,128)(2,1)}, u32[]{:S(2)}, u32[]{:S(2)}) %collective-permute-start.3) | collective-permute-done | bytes 720928 | tf_op jit(solution)/shard_map/ppermute | solution.py:697
  36.7 8.7 %collective-permute-done.2 = f32[320]{0:T(512)S(1)} collective-permute-done((f32[320]{0:T(512)S(1)}, f32[320]{0:T(512)S(1)}, u32[]{:S(2)}, u32[]{:S(2)}) %collective-permute-start.2) | collective-permute-done | bytes 1312 | tf_op jit(solution)/shard_map/ppermute | solution.py:700
  51.9 23.2 %all-gather.5.cloned.1.call-done.refs_0_.refs_2_.refs_1_ = bf16[1024,1408]{1,0:T(8,128)(2,1)} async-done(((bf16[256,1408]{1,0:T(8,128)(2,1)}), bf16[1024,1408]{1,0:T(8,128)(2,1)}) %all-gather.5.cloned.1.call-update) | async-done | bytes 2883600 | tf_op jit(solution)/shard_map/all_gather | solution.py:706
  86.0 5.2 collective-permute-done.6.refs_1_.far_rows
  91.2 43.4 %all-gather.7.cloned.1.call-done.refs_2_.refs_1_ = bf16[1024,1408]{1,0:T(8,128)(2,1)} async-done(((bf16[256,1408]{1,0:T(8,128)(2,1)}), bf16[1024,1408]{1,0:T(8,128)(2,1)}) %all-gather.7.cloned.1.call-update) | async-done | bytes 2883600 | tf_op jit(solution)/shard_map/all_gather | solution.py:706
  134.6 5.0 collective-permute-done.5.refs_1_.refs_3_.refs_2_
  147.2 4.1 norm_far.1.refs_1_.far_rows
  151.3 7.2 %joint.1.operands_1_ = f32[1280,768]{1,0:T(8,128)S(1)} custom-call(bf16[640,2048]{1,0:T(8,128)(2,1)S(1)} %norm_near.1.refs_0_.near_rows, bf16[640,2048]{1,0:T(8,128)(2,1)S(1)} %norm_far.1.refs_1_.far_rows, bf16[1024,1408]{1,0:T(8,128)(2,1)S(1)} %copy-done.2, bf16[1024,1408]{1,0:T(8,128)(2,1)} %collective-permute-done.5.refs_1_.refs_3_.refs_2_), custom_call_target="tpu_custom_call" | custom-call | flops 1006632960 | bytes 2097152 | tf_op jit(solution)/shard_map/joint/pallas_call | solution.py:421
  164.5 10.0 %attend.1 = (bf16[640,512]{1,0:T(8,128)(2,1)S(1)}, bf16[640,512]{1,0:T(8,128)(2,1)S(1)}, bf16[1280,768]{1,0:T(8,128)(2,1)S(1)}) custom-call(s32[14]{0:T(128)S(1)} %concatenate.31.operands_0_, f32[1280,768]{1,0:T(8,128)S(1)} %joint.1.operands_1_, f32[1280,128]{1,0:T(8,128)S(1)} %get-tuple-element.203.operands_2_.operands_3_, ...), custom_call_target="tpu_custom_call" | custom-call | flops 1476395008 | bytes 1966080 | tf_op jit(solution)/shard_map/attend/pallas_call | solution.py:799
  176.5 5.8 attended_far.1
  186.3 4.9 attended_near.1
  191.3 4.4 add_convert_fusion.2.mine
  195.7 8.3 %collective-permute-done.10.refs_5_.refs_4_ = bf16[256,1408]{1,0:T(8,128)(2,1)} collective-permute-done((bf16[256,1408]{1,0:T(8,128)(2,1)}, bf16[256,1408]{1,0:T(8,128)(2,1)}, u32[]{:S(2)}, u32[]{:S(2)}) %collective-permute-start.10) | collective-permute-done | bytes 720928 | tf_op jit(solution)/shard_map/ppermute | solution.py:697
  207.5 17.3 %collective-permute-done.12.refs_6_.refs_5_ = bf16[256,1408]{1,0:T(8,128)(2,1)S(1)} collective-permute-done((bf16[256,1408]{1,0:T(8,128)(2,1)}, bf16[256,1408]{1,0:T(8,128)(2,1)S(1)}, u32[]{:S(2)}, u32[]{:S(2)}) %collective-permute-start.12) | collective-permute-done | bytes 720928 | tf_op jit(solution)/shard_map/ppermute | solution.py:697
  227.8 11.7 %hidden_grad.1.refs_2_ = bf16[1280,1408]{1,0:T(8,128)(2,1)S(1)} custom-call(bf16[640,2048]{1,0:T(8,128)(2,1)} %kept.1.refs_0_.near_rows, bf16[640,2048]{1,0:T(8,128)(2,1)} %collective-permute-done.6.refs_1_.far_rows, bf16[1024,1408]{1,0:T(8,128)(2,1)S(1)} %copy-done.15, bf16[256,1408]{1,0:T(8,128)(2,1)} %collective-permute-done.7.refs_3_.refs_2_, ...), custom_call_target="tpu_custom_call" | custom-call | flops 1845493760 | bytes 2752512 | tf_op jit(solution)/shard_map/hidden_grad/pallas_call | solution.py:421
  239.5 23.2 %collective-permute-done.11.got = bf16[640,2048]{1,0:T(8,128)(2,1)S(1)} collective-permute-done((bf16[640,2048]{1,0:T(8,128)(2,1)}, bf16[640,2048]{1,0:T(8,128)(2,1)S(1)}, u32[]{:S(2)}, u32[]{:S(2)}) %collective-permute-start.11) | collective-permute-done | bytes 2621472 | tf_op jit(solution)/shard_map/ppermute | solution.py:700
  267.9 17.1 %collective-permute-done.14.refs_4_.refs_2_ = bf16[1024,1408]{1,0:T(8,128)(2,1)S(1)} collective-permute-done((bf16[1024,1408]{1,0:T(8,128)(2,1)}, bf16[1024,1408]{1,0:T(8,128)(2,1)S(1)}, u32[]{:S(2)}, u32[]{:S(2)}) %collective-permute-start.14) | collective-permute-done | bytes 2883616 | tf_op jit(solution)/shard_map/ppermute | solution.py:697
  285.0 11.4 %gate.1 = (f32[1280,1408]{1,0:T(8,128)}, bf16[1280,1408]{1,0:T(8,128)(2,1)S(1)}) custom-call(bf16[640,2048]{1,0:T(8,128)(2,1)S(1)} %get-tuple-element.123.refs_0_.near_rows, bf16[640,2048]{1,0:T(8,128)(2,1)S(1)} %collective-permute-done.13.refs_1_.far_rows, bf16[1280,1408]{1,0:T(8,128)(2,1)S(1)} %hidden_grad.1.refs_2_, bf16[1024,1408]{1,0:T(8,128)(2,1)S(1)} %copy-done.27, ...), custom_call_target="tpu_custom_call" | custom-call | flops 1845493760 | bytes 2752512 | tf_op jit(solution)/shard_map/gate/pallas_call | solution.py:452
  296.4 12.1 %grad_up_late.1 = bf16[1024,2816]{1,0:T(8,128)(2,1)} custom-call(bf16[640,2048]{1,0:T(8,128)(2,1)S(1)} %get-tuple-element.123.refs_0_.near_rows, bf16[640,2048]{1,0:T(8,128)(2,1)S(1)} %collective-permute-done.13.refs_1_.far_rows, bf16[1280,1408]{1,0:T(8,128)(2,1)S(1)} %get-tuple-element.140.refs_0_.refs_3_), custom_call_target="tpu_custom_call" | custom-call | flops 1845493760 | bytes 1556480 | tf_op jit(solution)/shard_map/grad_up_late/pallas_call | solution.py:648
  319.1 12.7 %up.1 = (bf16[1280,1408]{1,0:T(8,128)(2,1)S(1)}, bf16[1280,1408]{1,0:T(8,128)(2,1)S(1)}) custom-call(bf16[640,2048]{1,0:T(8,128)(2,1)S(1)} %copy-done.4, bf16[640,2048]{1,0:T(8,128)(2,1)S(1)} %copy-done.7, bf16[1280,1408]{1,0:T(8,128)(2,1)S(1)} %copy-done.26, f32[1280,1408]{1,0:T(8,128)} %get-tuple-element.128.refs_3_, bf16[1024,2816]{1,0:T(8,128)(2,1)S(1)} %copy-done), custom_call_target="tpu_custom_call" | custom-call | flops 1845493760 | bytes 2752512 | tf_op jit(solution)/shard_map/up/pallas_call | solution.py:503
  331.8 9.1 %grad_down.2 = bf16[1024,1408]{1,0:T(8,128)(2,1)} custom-call(bf16[640,2048]{1,0:T(8,128)(2,1)} %kept.1.refs_0_.near_rows, bf16[640,2048]{1,0:T(8,128)(2,1)} %collective-permute-done.6.refs_1_.far_rows, bf16[1280,1408]{1,0:T(8,128)(2,1)S(1)} %get-tuple-element.143.refs_0_), custom_call_target="tpu_custom_call" | custom-call | flops 922746880 | bytes 1556480 | tf_op jit(solution)/shard_map/grad_down/pallas_call | solution.py:612
  344.9 9.2 %normed_ff_grad_far.1 = bf16[640,2048]{1,0:T(8,128)(2,1)S(1)} custom-call(bf16[1280,1408]{1,0:T(8,128)(2,1)S(1)} %copy-done.12, bf16[1024,1408]{1,0:T(8,128)(2,1)S(1)} %copy-done.28, bf16[1024,1408]{1,0:T(8,128)(2,1)S(1)} %copy-done.30, bf16[1280,1408]{1,0:T(8,128)(2,1)S(1)} %copy-done.24, bf16[1024,2816]{1,0:T(8,128)(2,1)S(1)} %copy-done.1, ...), custom_call_target="tpu_custom_call" | custom-call | flops 1845493760 | bytes 6127616 | tf_op jit(solution)/shard_map/normed_ff_grad_far/pallas_call | solution.py:570
  356.9 7.4 %grad_gate.2 = (bf16[256,1408]{1,0:T(8,128)(2,1)}, bf16[768,1408]{1,0:T(8,128)(2,1)}) custom-call(bf16[640,2048]{1,0:T(8,128)(2,1)S(1)} %copy-done.5, bf16[640,2048]{1,0:T(8,128)(2,1)S(1)} %copy-done.8, bf16[1280,1408]{1,0:T(8,128)(2,1)S(1)} %copy-done.12), custom_call_target="tpu_custom_call" | custom-call | flops 922746880 | bytes 1556480 | tf_op jit(solution)/shard_map/grad_gate/pallas_call | solution.py:612
  364.4 13.9 %normed_ff_grad_near.1.mine = bf16[640,2048]{1,0:T(8,128)(2,1)} custom-call(bf16[1280,1408]{1,0:T(8,128)(2,1)S(1)} %copy-done.13, bf16[1024,1408]{1,0:T(8,128)(2,1)S(1)} %copy-done.28, bf16[1024,1408]{1,0:T(8,128)(2,1)S(1)} %copy-done.31, bf16[1280,1408]{1,0:T(8,128)(2,1)S(1)} %copy-done.24, ...), custom_call_target="tpu_custom_call" | custom-call | flops 1845493760 | bytes 6782976 | tf_op jit(solution)/shard_map/normed_ff_grad_near/pallas_call | solution.py:570
  380.5 8.0 %grad_down.3 = bf16[1024,1408]{1,0:T(8,128)(2,1)} custom-call(bf16[640,2048]{1,0:T(8,128)(2,1)} %kept.1.refs_0_.near_rows, bf16[640,2048]{1,0:T(8,128)(2,1)} %collective-permute-done.6.refs_1_.far_rows, bf16[1280,1408]{1,0:T(8,128)(2,1)S(1)} %copy-done.10), custom_call_target="tpu_custom_call" | custom-call | flops 922746880 | bytes 1556480 | tf_op jit(solution)/shard_map/grad_down/pallas_call | solution.py:612
  388.6 7.5 %branch_near.1 = bf16[640,2048]{1,0:T(8,128)(2,1)S(1)} custom-call(bf16[1280,1408]{1,0:T(8,128)(2,1)S(1)} %copy-done.10, bf16[1024,1408]{1,0:T(8,128)(2,1)S(1)} %copy-done.16, bf16[256,1408]{1,0:T(8,128)(2,1)} %collective-permute-done.7.refs_3_.refs_2_, bf16[256,1408]{1,0:T(8,128)(2,1)S(1)} %copy-done.58, ...), custom_call_target="tpu_custom_call" | custom-call | flops 922746880 | bytes 2342912 | tf_op jit(solution)/shard_map/branch_near/pallas_call | solution.py:570
  397.6 7.6 %branch_far.1 = bf16[640,2048]{1,0:T(8,128)(2,1)S(1)} custom-call(bf16[1280,1408]{1,0:T(8,128)(2,1)S(1)} %copy-done.10, bf16[1024,1408]{1,0:T(8,128)(2,1)S(1)} %copy-done.16, bf16[256,1408]{1,0:T(8,128)(2,1)} %collective-permute-done.7.refs_3_.refs_2_, bf16[256,1408]{1,0:T(8,128)(2,1)S(1)} %copy-done.58, ...), custom_call_target="tpu_custom_call" | custom-call | flops 922746880 | bytes 2342912 | tf_op jit(solution)/shard_map/branch_far/pallas_call | solution.py:570
  405.3 6.8 %grad_gate.3 = bf16[1024,1408]{1,0:T(8,128)(2,1)} custom-call(bf16[640,2048]{1,0:T(8,128)(2,1)S(1)} %copy-done.5, bf16[640,2048]{1,0:T(8,128)(2,1)S(1)} %copy-done.8, bf16[1280,1408]{1,0:T(8,128)(2,1)S(1)} %copy-done.14), custom_call_target="tpu_custom_call" | custom-call | flops 922746880 | bytes 1556480 | tf_op jit(solution)/shard_map/grad_gate/pallas_call | solution.py:612
  412.1 8.5 %collective-permute-done.17 = bf16[1024,1408]{1,0:T(8,128)(2,1)S(1)} collective-permute-done((bf16[1024,1408]{1,0:T(8,128)(2,1)}, bf16[1024,1408]{1,0:T(8,128)(2,1)S(1)}, u32[]{:S(2)}, u32[]{:S(2)}) %collective-permute-start.17) | collective-permute-done | bytes 2883616 | tf_op jit(solution)/shard_map/ppermute | solution.py:697
  424.5 16.7 %collective-permute-done.18 = bf16[256,1408]{1,0:T(8,128)(2,1)S(1)} collective-permute-done((bf16[256,1408]{1,0:T(8,128)(2,1)}, bf16[256,1408]{1,0:T(8,128)(2,1)S(1)}, u32[]{:S(2)}, u32[]{:S(2)}) %collective-permute-start.18) | collective-permute-done | bytes 720928 | tf_op jit(solution)/shard_map/ppermute | solution.py:697
  446.3 5.3 middle_back.1
  455.4 3.4 collective-permute-done.19.far_rows.refs_1_
  458.8 3.2 grad_output.3
  462.0 5.2 mixed_grad.1.operands_2_
  467.3 16.2 %attend_back.1 = (bf16[640,768]{1,0:T(8,128)(2,1)S(1)}, bf16[640,768]{1,0:T(8,128)(2,1)S(1)}) custom-call(s32[14]{0:T(128)S(1)} %concatenate.31.operands_0_, bf16[1280,768]{1,0:T(8,128)(2,1)S(1)} %copy-done.86, bf16[1280,512]{1,0:T(8,128)(2,1)S(1)} %mixed_grad.1.operands_2_, f32[1280,128]{1,0:T(8,128)S(1)} %copy-done.77, f32[1280,128]{1,0:T(8,128)S(1)} %copy-done.79), custom_call_target="tpu_custom_call" | custom-call | flops 2214592512 | bytes 1966080 | tf_op jit(solution)/shard_map/attend_back/pallas_call | solution.py:921
  483.6 4.2 grad_joint.2
  487.7 15.7 %collective-permute-done.20 = bf16[768,1408]{1,0:T(8,128)(2,1)} collective-permute-done((bf16[768,1408]{1,0:T(8,128)(2,1)S(1)}, bf16[768,1408]{1,0:T(8,128)(2,1)}, u32[]{:S(2)}, u32[]{:S(2)}) %collective-permute-start.20) | collective-permute-done | bytes 2162720 | tf_op jit(solution)/shard_map/ppermute | solution.py:697
  510.8 5.4 normed_grad_far.1
  517.9 3.2 collective-permute-done.21.refs_3_
  521.2 5.3 normed_grad_near.1.mine
  529.8 3.2 grad_output.2
  533.0 4.1 grad_joint.3
  537.1 38.4 %collective-permute-done.22 = bf16[1024,512]{1,0:T(8,128)(2,1)S(1)} collective-permute-done((bf16[1024,512]{1,0:T(8,128)(2,1)S(1)}, bf16[1024,512]{1,0:T(8,128)(2,1)S(1)}, u32[]{:S(2)}, u32[]{:S(2)}) %collective-permute-start.22) | collective-permute-done | bytes 1048608 | tf_op jit(solution)/shard_map/ppermute | solution.py:697
  586.2 12.1 %collective-permute-done.27 = bf16[256,1408]{1,0:T(8,128)(2,1)S(1)} collective-permute-done((bf16[256,1408]{1,0:T(8,128)(2,1)S(1)}, bf16[256,1408]{1,0:T(8,128)(2,1)S(1)}, u32[]{:S(2)}, u32[]{:S(2)}) %collective-permute-start.27) | collective-permute-done | bytes 720928 | tf_op jit(solution)/shard_map/ppermute | solution.py:697
  599.8 3.3 input_grad.1
  605.8 11.1 %collective-permute-done.26.got = bf16[320,2048]{1,0:T(8,128)(2,1)} collective-permute-done((bf16[320,2048]{1,0:T(8,128)(2,1)}, bf16[320,2048]{1,0:T(8,128)(2,1)}, u32[]{:S(2)}, u32[]{:S(2)}) %collective-permute-start.26) | collective-permute-done | bytes 1310752 | tf_op jit(solution)/shard_map/ppermute | solution.py:700
  622.1 6.8 %reduce-scatter.9.cloned.1.call-done = bf16[256,1280]{1,0:T(8,128)(2,1)} async-done(((bf16[1024,1280]{1,0:T(8,128)(2,1)}), bf16[256,1280]{1,0:T(8,128)(2,1)}) %reduce-scatter.9.cloned.1.call-update) | async-done | bytes 655376 | tf_op jit(solution)/shard_map/reduce_scatter | solution.py:709
  (319 shorter events, 135.7 us)
Async XLA Ops:
  7.2 68.0 %all-gather.5.cloned.1.call-start = ((), (), s32[]{:S(2)}) async-start(), calls=%async_computation.4 | async-start | bytes 3604480 | tf_op jit(solution)/shard_map/all_gather | solution.py:706
  13.1 121.5 %all-gather.7.cloned.1.call-start = ((), (), s32[]{:S(2)}) async-start(), calls=%async_computation.5 | async-start | bytes 3604480 | tf_op jit(solution)/shard_map/all_gather | solution.py:706
  13.2 32.2 %collective-permute-start.1 = (bf16[320,2048]{1,0:T(8,128)(2,1)}, bf16[320,2048]{1,0:T(8,128)(2,1)}, u32[]{:S(2)}, u32[]{:S(2)}) collective-permute-start(bf16[320,2048]{1,0:T(8,128)(2,1)} %rows.1), channel_id=1, source_target_pairs={{0,2},{2,0},{1,3},{3,1},{4,6},{6,4},{5,7},{7,5},{8,10},{10,8},{9,1... | collective-permute-start | bytes 3932168 | tf_op jit(solution)/shard_map/ppermute | solution.py:700
  16.2 17.9 %collective-permute-start.3 = (bf16[256,1408]{1,0:T(8,128)(2,1)}, bf16[256,1408]{1,0:T(8,128)(2,1)}, u32[]{:S(2)}, u32[]{:S(2)}) collective-permute-start(bf16[256,1408]{1,0:T(8,128)(2,1)} %param.23), channel_id=1, source_target_pairs={{4,0},{0,4},{5,1},{1,5},{6,2},{2,6},{7,3},{3,7},{12,8},{8,12},{13,... | collective-permute-start | bytes 2162696 | tf_op jit(solution)/shard_map/ppermute | solution.py:697
  17.7 178.0 %all-gather.9.cloned.1.call-start = ((), (), s32[]{:S(2)}) async-start(), calls=%async_computation.6 | async-start | bytes 3604480 | tf_op jit(solution)/shard_map/all_gather | solution.py:706
  17.8 27.5 %collective-permute-start.2 = (f32[320]{0:T(512)S(1)}, f32[320]{0:T(512)S(1)}, u32[]{:S(2)}, u32[]{:S(2)}) collective-permute-start(f32[320]{0:T(512)S(1)} %subtract_convert_fusion), channel_id=1, source_target_pairs={{0,2},{2,0},{1,3},{3,1},{4,6},{6,4},{5,7},{7,5},{8,10},{10,8},{9,1... | collective-permute-start | bytes 3848 | tf_op jit(solution)/shard_map/ppermute | solution.py:700
  46.8 31.6 %copy-start.39 = (bf16[640,2048]{1,0:T(8,128)(2,1)}, bf16[640,2048]{1,0:T(8,128)(2,1)S(1)}, u32[]{:S(2)}) copy-start(bf16[640,2048]{1,0:T(8,128)(2,1)S(1)} %constant_dynamic-update-slice_fusion.2.rows) | copy-start | bytes 7864324
  46.8 5.1 collective-permute-start.4
  46.9 31.5 %collective-permute-start = (bf16[320,2048]{1,0:T(8,128)(2,1)}, bf16[320,2048]{1,0:T(8,128)(2,1)}, u32[]{:S(2)}, u32[]{:S(2)}) collective-permute-start(bf16[320,2048]{1,0:T(8,128)(2,1)} %param.25), channel_id=1, source_target_pairs={{0,2},{2,0},{1,3},{3,1},{4,6},{6,4},{5,7},{7,5},{8,10},{10,8},{9,1... | collective-permute-start | bytes 3932168 | tf_op jit(solution)/shard_map/ppermute | solution.py:700
  75.2 64.5 %collective-permute-start.5 = (bf16[1024,1408]{1,0:T(8,128)(2,1)}, bf16[1024,1408]{1,0:T(8,128)(2,1)}, u32[]{:S(2)}, u32[]{:S(2)}) collective-permute-start(bf16[1024,1408]{1,0:T(8,128)(2,1)} %all-gather.5.cloned.1.call-done.refs_0_.refs_2_.refs_1_), channel_id=1, source_target_pairs={{4,0},{0,4},{5,1},{1,5},{6,2},{2,6},{7,3},{3,7},{12,8},{8,12},{13,... | collective-permute-start | bytes 8650760 | tf_op jit(solution)/shard_map/ppermute | solution.py:697
  82.9 60.3 %copy-start.99 = (s32[1,10]{1,0:T(1,128)S(1)}, s32[1,10]{1,0:T(1,128)}, u32[]{:S(2)}) copy-start(s32[1,10]{1,0:T(1,128)} %param.15) | copy-start | bytes 124
  82.9 60.4 %copy-start.2 = (bf16[1024,1408]{1,0:T(8,128)(2,1)S(1)}, bf16[1024,1408]{1,0:T(8,128)(2,1)}, u32[]{:S(2)}) copy-start(bf16[1024,1408]{1,0:T(8,128)(2,1)} %all-gather.5.cloned.1.call-done.refs_0_.refs_2_.refs_1_) | copy-start | bytes 8650756
  85.9 5.3 collective-permute-start.6
  86.0 224.4 %all-gather.11.cloned.1.call-start = ((), (), s32[]{:S(2)}) async-start(), calls=%async_computation.7 | async-start | bytes 7208960 | tf_op jit(solution)/shard_map/all_gather | solution.py:706
  141.7 17.3 %collective-permute-start.7 = (bf16[256,1408]{1,0:T(8,128)(2,1)}, bf16[256,1408]{1,0:T(8,128)(2,1)}, u32[]{:S(2)}, u32[]{:S(2)}) collective-permute-start(bf16[256,1408]{1,0:T(8,128)(2,1)} %slice.52), channel_id=1, source_target_pairs={{4,0},{0,4},{5,1},{1,5},{6,2},{2,6},{7,3},{3,7},{12,8},{8,12},{13,... | collective-permute-start | bytes 2162696 | tf_op jit(solution)/shard_map/ppermute | solution.py:697
  160.1 16.4 %collective-permute-start.8 = (bf16[256,1408]{1,0:T(8,128)(2,1)S(1)}, bf16[256,1408]{1,0:T(8,128)(2,1)S(1)}, u32[]{:S(2)}, u32[]{:S(2)}) collective-permute-start(bf16[256,1408]{1,0:T(8,128)(2,1)S(1)} %slice.53), channel_id=1, source_target_pairs={{4,0},{0,4},{5,1},{1,5},{6,2},{2,6},{7,3},{3,7},{12,8},{8,12},{13,... | collective-permute-start | bytes 2162696 | tf_op jit(solution)/shard_map/ppermute | solution.py:697
  182.4 8.9 %collective-permute-start.9 = (bf16[640,2048]{1,0:T(8,128)(2,1)}, bf16[640,2048]{1,0:T(8,128)(2,1)}, u32[]{:S(2)}, u32[]{:S(2)}) collective-permute-start(bf16[640,2048]{1,0:T(8,128)(2,1)} %attended_far.1), channel_id=1, source_target_pairs={{0,1},{1,0},{2,3},{3,2},{4,5},{5,4},{6,7},{7,6},{8,9},{9,8},{10,11... | collective-permute-start | bytes 7864328 | tf_op jit(solution)/shard_map/ppermute | solution.py:700
  182.5 321.0 %reduce-scatter.5.cloned.1.call-start = ((), (), s32[]{:S(2)}) async-start(), calls=%async_computation.8 | async-start | bytes 7208960 | tf_op jit(solution)/shard_map/reduce_scatter | solution.py:709
  185.1 18.9 %collective-permute-start.10 = (bf16[256,1408]{1,0:T(8,128)(2,1)}, bf16[256,1408]{1,0:T(8,128)(2,1)}, u32[]{:S(2)}, u32[]{:S(2)}) collective-permute-start(bf16[256,1408]{1,0:T(8,128)(2,1)} %get-tuple-element.194), channel_id=1, source_target_pairs={{4,0},{0,4},{5,1},{1,5},{6,2},{2,6},{7,3},{3,7},{12,8},{8,12},{13,... | collective-permute-start | bytes 2162696 | tf_op jit(solution)/shard_map/ppermute | solution.py:697
  204.0 58.7 %collective-permute-start.11 = (bf16[640,2048]{1,0:T(8,128)(2,1)}, bf16[640,2048]{1,0:T(8,128)(2,1)S(1)}, u32[]{:S(2)}, u32[]{:S(2)}) collective-permute-start(bf16[640,2048]{1,0:T(8,128)(2,1)} %add_convert_fusion.2.mine), channel_id=1, source_target_pairs={{0,2},{2,0},{1,3},{3,1},{4,6},{6,4},{5,7},{7,5},{8,10},{10,8},{9,1... | collective-permute-start | bytes 7864328 | tf_op jit(solution)/shard_map/ppermute | solution.py:700
  205.5 19.3 %collective-permute-start.12 = (bf16[256,1408]{1,0:T(8,128)(2,1)}, bf16[256,1408]{1,0:T(8,128)(2,1)S(1)}, u32[]{:S(2)}, u32[]{:S(2)}) collective-permute-start(bf16[256,1408]{1,0:T(8,128)(2,1)} %get-tuple-element.193), channel_id=1, source_target_pairs={{4,0},{0,4},{5,1},{1,5},{6,2},{2,6},{7,3},{3,7},{12,8},{8,12},{13,... | collective-permute-start | bytes 2162696 | tf_op jit(solution)/shard_map/ppermute | solution.py:697
  206.7 78.3 %collective-permute-start.14 = (bf16[1024,1408]{1,0:T(8,128)(2,1)}, bf16[1024,1408]{1,0:T(8,128)(2,1)S(1)}, u32[]{:S(2)}, u32[]{:S(2)}) collective-permute-start(bf16[1024,1408]{1,0:T(8,128)(2,1)} %all-gather.9.cloned.1.call-done.refs_3_.refs_1_), channel_id=1, source_target_pairs={{4,0},{0,4},{5,1},{1,5},{6,2},{2,6},{7,3},{3,7},{12,8},{8,12},{13,... | collective-permute-start | bytes 8650760 | tf_op jit(solution)/shard_map/ppermute | solution.py:697
  227.7 35.0 %copy-start.41 = (bf16[640,2048]{1,0:T(8,128)(2,1)S(1)}, bf16[640,2048]{1,0:T(8,128)(2,1)}, u32[]{:S(2)}) copy-start(bf16[640,2048]{1,0:T(8,128)(2,1)} %copy-done.39) | copy-start | bytes 7864324
  227.8 35.0 %copy-start.48 = (bf16[640,2048]{1,0:T(8,128)(2,1)S(1)}, bf16[640,2048]{1,0:T(8,128)(2,1)}, u32[]{:S(2)}) copy-start(bf16[640,2048]{1,0:T(8,128)(2,1)} %add_convert_fusion.2.mine) | copy-start | bytes 7864324
  239.5 45.5 %copy-start.25 = (bf16[1280,1408]{1,0:T(8,128)(2,1)}, bf16[1280,1408]{1,0:T(8,128)(2,1)S(1)}, u32[]{:S(2)}) copy-start(bf16[1280,1408]{1,0:T(8,128)(2,1)S(1)} %hidden_grad.1.refs_2_) | copy-start | bytes 10813444
  262.7 22.3 %copy-start.27 = (bf16[1024,1408]{1,0:T(8,128)(2,1)S(1)}, bf16[1024,1408]{1,0:T(8,128)(2,1)}, u32[]{:S(2)}) copy-start(bf16[1024,1408]{1,0:T(8,128)(2,1)} %all-gather.9.cloned.1.call-done.refs_3_.refs_1_) | copy-start | bytes 8650756
  267.8 28.6 %copy-start.3 = (bf16[640,2048]{1,0:T(8,128)(2,1)}, bf16[640,2048]{1,0:T(8,128)(2,1)S(1)}, u32[]{:S(2)}) copy-start(bf16[640,2048]{1,0:T(8,128)(2,1)S(1)} %get-tuple-element.123.refs_0_.near_rows) | copy-start | bytes 7864324
  267.8 17.1 %collective-permute-start.13 = (bf16[640,2048]{1,0:T(8,128)(2,1)S(1)}, bf16[640,2048]{1,0:T(8,128)(2,1)S(1)}, u32[]{:S(2)}, u32[]{:S(2)}) collective-permute-start(bf16[640,2048]{1,0:T(8,128)(2,1)S(1)} %get-tuple-element.123.refs_0_.near_rows), channel_id=1, source_target_pairs={{0,1},{1,0},{2,3},{3,2},{4,5},{5,4},{6,7},{7,6},{8,9},{9,8},{10,11... | collective-permute-start | bytes 7864328 | tf_op jit(solution)/shard_map/ppermute | solution.py:700
  310.3 268.0 %reduce-scatter.7.cloned.1.call-start = ((), (), s32[]{:S(2)}) async-start(), calls=%async_computation.9 | async-start | bytes 3604480 | tf_op jit(solution)/shard_map/reduce_scatter | solution.py:709
  355.5 8.8 %collective-permute-start.15 = (bf16[640,2048]{1,0:T(8,128)(2,1)}, bf16[640,2048]{1,0:T(8,128)(2,1)S(1)}, u32[]{:S(2)}, u32[]{:S(2)}) collective-permute-start(bf16[640,2048]{1,0:T(8,128)(2,1)} %copy-done.70), channel_id=1, source_target_pairs={{0,1},{1,0},{2,3},{3,2},{4,5},{5,4},{6,7},{7,6},{8,9},{9,8},{10,11... | collective-permute-start | bytes 7864328 | tf_op jit(solution)/shard_map/ppermute | solution.py:700
  355.5 65.1 %collective-permute-start.17 = (bf16[1024,1408]{1,0:T(8,128)(2,1)}, bf16[1024,1408]{1,0:T(8,128)(2,1)S(1)}, u32[]{:S(2)}, u32[]{:S(2)}) collective-permute-start(bf16[1024,1408]{1,0:T(8,128)(2,1)} %grad_down.2), channel_id=1, source_target_pairs={{4,0},{0,4},{5,1},{1,5},{6,2},{2,6},{7,3},{3,7},{12,8},{8,12},{13,... | collective-permute-start | bytes 8650760 | tf_op jit(solution)/shard_map/ppermute | solution.py:697
  378.2 62.9 %collective-permute-start.16 = (bf16[640,2048]{1,0:T(8,128)(2,1)}, bf16[640,2048]{1,0:T(8,128)(2,1)}, u32[]{:S(2)}, u32[]{:S(2)}) collective-permute-start(bf16[640,2048]{1,0:T(8,128)(2,1)} %normed_ff_grad_near.1.mine), channel_id=1, source_target_pairs={{0,2},{2,0},{1,3},{3,1},{4,6},{6,4},{5,7},{7,5},{8,10},{10,8},{9,1... | collective-permute-start | bytes 7864328 | tf_op jit(solution)/shard_map/ppermute | solution.py:700
  422.9 180.1 %reduce-scatter.11.cloned.1.call-start = ((), (), s32[]{:S(2)}) async-start(), calls=%async_computation.11 | async-start | bytes 3604480 | tf_op jit(solution)/shard_map/reduce_scatter | solution.py:709
  423.0 18.1 %collective-permute-start.18 = (bf16[256,1408]{1,0:T(8,128)(2,1)}, bf16[256,1408]{1,0:T(8,128)(2,1)S(1)}, u32[]{:S(2)}, u32[]{:S(2)}) collective-permute-start(bf16[256,1408]{1,0:T(8,128)(2,1)} %get-tuple-element.147), channel_id=1, source_target_pairs={{4,0},{0,4},{5,1},{1,5},{6,2},{2,6},{7,3},{3,7},{12,8},{8,12},{13,... | collective-permute-start | bytes 2162696 | tf_op jit(solution)/shard_map/ppermute | solution.py:697
  453.9 4.9 collective-permute-start.19
  453.9 49.6 %collective-permute-start.20 = (bf16[768,1408]{1,0:T(8,128)(2,1)S(1)}, bf16[768,1408]{1,0:T(8,128)(2,1)}, u32[]{:S(2)}, u32[]{:S(2)}) collective-permute-start(bf16[768,1408]{1,0:T(8,128)(2,1)S(1)} %copy-done.100), channel_id=1, source_target_pairs={{4,0},{0,4},{5,1},{1,5},{6,2},{2,6},{7,3},{3,7},{12,8},{8,12},{13,... | collective-permute-start | bytes 6488072 | tf_op jit(solution)/shard_map/ppermute | solution.py:697
  509.5 119.3 %reduce-scatter.9.cloned.1.call-start = ((), (), s32[]{:S(2)}) async-start(), calls=%async_computation.10 | async-start | bytes 3276800 | tf_op jit(solution)/shard_map/reduce_scatter | solution.py:709
  516.2 5.0 collective-permute-start.21
  516.3 59.3 %collective-permute-start.23 = (bf16[1024,768]{1,0:T(8,128)(2,1)S(1)}, bf16[1024,768]{1,0:T(8,128)(2,1)S(1)}, u32[]{:S(2)}, u32[]{:S(2)}) collective-permute-start(bf16[1024,768]{1,0:T(8,128)(2,1)S(1)} %copy-done.91), channel_id=1, source_target_pairs={{4,0},{0,4},{5,1},{1,5},{6,2},{2,6},{7,3},{3,7},{12,8},{8,12},{13,... | collective-permute-start | bytes 4718600 | tf_op jit(solution)/shard_map/ppermute | solution.py:697
  528.1 47.4 %collective-permute-start.24 = (bf16[320,2048]{1,0:T(8,128)(2,1)S(1)}, bf16[320,2048]{1,0:T(8,128)(2,1)S(1)}, u32[]{:S(2)}, u32[]{:S(2)}) collective-permute-start(bf16[320,2048]{1,0:T(8,128)(2,1)S(1)} %slice.68), channel_id=1, source_target_pairs={{0,2},{2,0},{1,3},{3,1},{4,6},{6,4},{5,7},{7,5},{8,10},{10,8},{9,1... | collective-permute-start | bytes 3932168 | tf_op jit(solution)/shard_map/ppermute | solution.py:700
  528.5 47.0 %collective-permute-start.22 = (bf16[1024,512]{1,0:T(8,128)(2,1)S(1)}, bf16[1024,512]{1,0:T(8,128)(2,1)S(1)}, u32[]{:S(2)}, u32[]{:S(2)}) collective-permute-start(bf16[1024,512]{1,0:T(8,128)(2,1)S(1)} %copy-done.93), channel_id=1, source_target_pairs={{4,0},{0,4},{5,1},{1,5},{6,2},{2,6},{7,3},{3,7},{12,8},{8,12},{13,... | collective-permute-start | bytes 3145736 | tf_op jit(solution)/shard_map/ppermute | solution.py:697
  533.0 42.6 %copy-start.89 = (bf16[1024,512]{1,0:T(8,128)(2,1)S(1)}, bf16[1024,512]{1,0:T(8,128)(2,1)}, u32[]{:S(2)}) copy-start(bf16[1024,512]{1,0:T(8,128)(2,1)} %grad_output.2) | copy-start | bytes 3145732
  537.1 38.7 %copy-start.88 = (bf16[1024,768]{1,0:T(8,128)(2,1)S(1)}, bf16[1024,768]{1,0:T(8,128)(2,1)}, u32[]{:S(2)}) copy-start(bf16[1024,768]{1,0:T(8,128)(2,1)} %grad_joint.3) | copy-start | bytes 4718596
  578.3 5.2 collective-permute-start.25
  579.7 18.6 %collective-permute-start.27 = (bf16[256,1408]{1,0:T(8,128)(2,1)S(1)}, bf16[256,1408]{1,0:T(8,128)(2,1)S(1)}, u32[]{:S(2)}, u32[]{:S(2)}) collective-permute-start(bf16[256,1408]{1,0:T(8,128)(2,1)S(1)} %slice.64), channel_id=1, source_target_pairs={{4,0},{0,4},{5,1},{1,5},{6,2},{2,6},{7,3},{3,7},{12,8},{8,12},{13,... | collective-permute-start | bytes 2162696 | tf_op jit(solution)/shard_map/ppermute | solution.py:697
  585.8 31.1 %collective-permute-start.26 = (bf16[320,2048]{1,0:T(8,128)(2,1)}, bf16[320,2048]{1,0:T(8,128)(2,1)}, u32[]{:S(2)}, u32[]{:S(2)}) collective-permute-start(bf16[320,2048]{1,0:T(8,128)(2,1)} %slice.69), channel_id=1, source_target_pairs={{0,2},{2,0},{1,3},{3,1},{4,6},{6,4},{5,7},{7,5},{8,10},{10,8},{9,1... | collective-permute-start | bytes 3932168 | tf_op jit(solution)/shard_map/ppermute | solution.py:700
  632.5 1.2 collective-permute-start.28
  633.8 3.7 collective-permute-start.29
  (93 other events, 684.2 us)
Sparse Core Ops, SparseCore 0:
  13.2 61.8 all-gather.4
  76.7 57.8 all-gather.6
  136.2 57.8 all-gather.8
  196.1 105.3 all-gather.10
  310.4 100.4 reduce-scatter.4
  423.1 54.6 reduce-scatter.6
  509.7 54.6 reduce-scatter.10
  578.4 50.3 reduce-scatter.8

commit v3 on v2

--- a/solution.py
+++ b/solution.py
@@ -512,7 +512,7 @@
     )(near, far, hidden_grad, gate, *up_slots)
 
 
-def back_rows(grads, weights, side, name, far=None):
+def back_rows(grads, weights, side, name, far=None, shape=shaped):
     width = sum(array.shape[0] for array in weights[0][0][0])
     tile = min(512, min(array.shape[0] for parts in weights for w in parts for array in w[0]))
     first = grads[0]
@@ -572,7 +572,7 @@
         grid=(width // tile,),
         in_specs=specs,
         out_specs=spec((count, tile), lambda j: (0, j)),
-        out_shape=shaped(count, width, bf16),
+        out_shape=shape(count, width, bf16),
         compiler_params=pltpu.CompilerParams(vmem_limit_bytes=VMEM),
         cost_estimate=cost(work, 2 * sum(operand.size for operand in operands)),
         name=name,
@@ -858,12 +858,19 @@
         ff_far = back_rows(*back_plan, 1, "normed_ff_grad_far")
         ff_far, gate_grad, up_grad = fence((ff_far, gate_grad, up_grad))
         ff_far = swap(ff_far, "core")
-        gate_last = weight_part(all_ff, gate_grad, half, last, "grad_gate", parts=2)
+        first = units // HD * 4 // 11 * HD if last else 0
+        gate_columns = slice(first, units)
+        gate_last = weight_part(all_ff, gate_grad, half, last, "grad_gate", gate_columns)
         gate_grad, up_grad, gate_last = fence((gate_grad, up_grad, gate_last))
         back_plan = ([gate_grad, up_grad], [all_of(weight_gate), up_plan])
-        ff_grad = back_rows(*back_plan, 0, "normed_ff_grad_near", ff_far)
+        ff_grad = back_rows(*back_plan, 0, "normed_ff_grad_near", ff_far, in_hbm)
         ff_grad, gate_grad, up_grad, hidden_ff = fence((ff_grad, gate_grad, up_grad, hidden_ff))
         ff_got = swap(ff_grad, "row")
+        gate_first_sums = None
+        if first:
+            gate_first = weight_slots(all_ff, gate_grad, half, "grad_gate_first", slice(0, first))
+            gate_grad, hidden_ff, gate_first = fence((gate_grad, hidden_ff, gate_first))
+            gate_first_sums = scatter(gate_first)
 
         def to_last(values):
             return from_inner(values, inner - last) if last else None
@@ -874,16 +881,16 @@
             return (values.astype(f32) + got.astype(f32)).astype(bf16)
 
         down_got = to_last(down_last)
-        gate_got = [to_last(values) for values in gate_last]
+        gate_got = to_last(gate_last)
         up_last = up_got = None
         if early:
             up_last = weight_part(all_ff, up_grad, half, last, "grad_up", slice(0, early))
             up_got = to_last(up_last)
-        own = [down_last, jnp.concatenate(gate_last, axis=0), up_last]
+        own = [down_last, gate_last, up_last]
         if last:
             own = [
                 weight_part(all_branch, hidden_ff, half, 0, "grad_down"),
-                weight_part(all_ff, gate_grad, half, 0, "grad_gate"),
+                weight_part(all_ff, gate_grad, half, 0, "grad_gate", gate_columns),
                 weight_part(all_ff, up_grad, half, 0, "grad_up", slice(0, early))
                 if early
                 else None,
@@ -895,7 +902,7 @@
             (own[0], down_got, own[1], branch_far, branch_near)
         )
         down_sum = plus(down_own, down_got)
-        ff_got, own, up_last, gate_got[0] = fence((ff_got, own, up_last, gate_got[0]))
+        ff_got, own, up_last, gate_last = fence((ff_got, own, up_last, gate_last))
         grad_down = scatter(down_sum)
         middle_grad, attended_grad = row_call(
             middle_back_kernel,
@@ -920,30 +927,26 @@
         mixed_grad, output_last = fence((mixed_grad, output_last))
         packed_grad = tuple(attend_back(table, rotated, mixed_grad, cosine, sine))
         joint_last = weight_part(normed, packed_grad, half, last, "grad_joint")
-        packed_grad, gate_got, up_late_sums, joint_last = fence(
-            (packed_grad, gate_got, up_late_sums, joint_last)
-        )
-        gate_sums = own[1]
-        if last:
-            rows = half // 4
-            gate_sums = jnp.concatenate(
-                [plus(own[1][:rows], gate_got[0]), plus(own[1][rows:], gate_got[1])], axis=0
-            )
-        grad_gate = scatter(gate_sums)
-        normed_grad = core_sum([packed_grad], [packed_plan(joint_columns)], "normed_grad")
+        normed_plan = ([packed_grad], [packed_plan(joint_columns)])
+        normed_far = back_rows(*normed_plan, 1, "normed_grad_far")
+        normed_near = back_rows(*normed_plan, 0, "normed_grad_near")
+        packed_grad, gate_got, up_late_sums, joint_last, normed_far, normed_near = fence(
+            (packed_grad, gate_got, up_late_sums, joint_last, normed_far, normed_near)
+        )
+        grad_gate = scatter(plus(own[1], gate_got))
+        normed_grad = (normed_near.astype(f32) + swap(normed_far, "core").astype(f32)).astype(bf16)
         normed_got = swap(normed_grad[part:], "row")
+        branch = (branch_near.astype(f32) + swap(branch_far, "core").astype(f32)).astype(bf16)
         output_sum, joint_sum = output_last, joint_last
         if last:
             output_own = weight_part(all_attended, mixed, half, 0, "grad_output")
             joint_own = weight_part(normed, packed_grad, half, 0, "grad_joint")
-            output_own, joint_own, normed_grad = fence((output_own, joint_own, normed_grad))
             output_got, joint_got = to_last(output_last), to_last(joint_last)
-            output_got, joint_got, normed_got, branch_far = fence(
-                (output_got, joint_got, normed_got, branch_far)
+            output_got, joint_got, normed_got, branch = fence(
+                (output_got, joint_got, normed_got, branch)
             )
             output_sum = plus(output_own, output_got)
             joint_sum = plus(joint_own, joint_got)
-        branch = (branch_near.astype(f32) + swap(branch_far, "core").astype(f32)).astype(bf16)
         branch_got = swap(branch[part:], "row")
         (layer_out,) = row_call(
             layer_kernel,
@@ -959,7 +962,10 @@
         if early:
             up_got, grad_down = fence((up_got, grad_down))
             grad_up = scatter(plus(own[2], up_got)).astype(f32)
-        attention_sum, grad_down = fence((attention_sum, grad_down))
+        attention_sum, grad_down, gate_first_sums = fence(
+            (attention_sum, grad_down, gate_first_sums)
+        )
+        attention_terms = attention_sum
         attention_sum = scatter(attention_sum)
         (input_grad,) = pl.pallas_call(
             input_kernel,
@@ -980,52 +986,59 @@
             name="input_grad",
         )(order, hidden_in, normed_grad, normed_got, gain_one, middle_grad)
         if late:
-            grad_late = collect([up_late_sums[:, s * late : (s + 1) * late] for s in slots])
+            sums = [(up_late_sums, late)] + ([(gate_first_sums, first)] if first else [])
+            grad_late = collect(
+                [
+                    jnp.concatenate([rows[:, s * wide : (s + 1) * wide] for rows, wide in sums], axis=1)
+                    for s in slots
+                ]
+            )
+            if first:
+                grad_gate = jnp.concatenate([grad_late[:, late:], grad_gate.astype(f32)], axis=1)
+                grad_late = grad_late[:, :late]
             grad_up = grad_late if grad_up is None else jnp.concatenate([grad_up, grad_late], axis=1)
         grad_down, grad_gate, grad_up = [
             grad.astype(f32) for grad in (grad_down, grad_gate, grad_up)
         ]
 
-        attention_sum, input_grad, layer_out = fence((attention_sum, input_grad, layer_out))
+        def over_tensor(values):
+            values = values + swap(values, "core")
+            return values + swap(values, "row")
+
+        own_weights = packed_slots[0][:, :joint_width].astype(f32)
+        terms = jnp.sum(own_weights * attention_terms[:, heads * HD :].astype(f32), axis=1)
+        terms = over_tensor(terms[None, :])
+        step = 1
+        while step < outer:
+            pairs = [(z ^ step, z) for z in range(outer)]
+            terms = terms + lax.ppermute(terms, "outer", pairs)
+            step *= 2
+        at = lax.axis_index("outer") * shard
+        attention_gain_grad = lax.dynamic_slice_in_dim(terms[0], at, shard, 0)
+        attention_gain_grad = attention_gain_grad / attention_gain.astype(f32)
+        terms = jnp.sum(gate_weight.astype(f32) * grad_gate, axis=1)
+        terms = terms + jnp.sum(up_weight.astype(f32) * grad_up, axis=1)
+        feedforward_gain_grad = over_tensor(terms[None, :])[0] / feedforward_gain.astype(f32)
+
+        attention_sum, input_grad, layer_out, attention_gain_grad, feedforward_gain_grad = fence(
+            (attention_sum, input_grad, layer_out, attention_gain_grad, feedforward_gain_grad)
+        )
         attention_sum = attention_sum.astype(f32)
         grad_output = attention_sum[:, : heads * HD]
         grad_joint = attention_sum[:, heads * HD :]
-
-        def gain_terms(pairs, gain):
-            total = None
-            for weight, grad in pairs:
-                term = jnp.sum(weight.astype(f32) * grad, axis=1)
-                total = term if total is None else total + term
-            return total / gain.astype(f32)
-
         query_width = heads * HD
         grad_query = grad_joint[:, :query_width]
         grad_key = grad_joint[:, query_width : query_width + HD]
         grad_value = grad_joint[:, query_width + HD :]
-        gain_grads = jnp.stack(
-            [
-                gain_terms(
-                    [
-                        (query_weight, grad_query),
-                        (key_weight, grad_key),
-                        (value_weight, grad_value),
-                    ],
-                    attention_gain,
-                ),
-                gain_terms([(gate_weight, grad_gate), (up_weight, grad_up)], feedforward_gain),
-            ]
-        )
-        gain_grads = gain_grads + swap(gain_grads, "core")
-        gain_grads = gain_grads + swap(gain_grads, "row")
         return (
             layer_out,
             input_grad,
-            gain_grads[0],
+            attention_gain_grad,
             grad_query,
             grad_key,
             grad_value,
             grad_output,
-            gain_grads[1],
+            feedforward_gain_grad,
             grad_gate,
             grad_up,
             grad_down,

time: 654 us -> 640 us (0.979)
  waiting for transfers between devices: 291 us -> 260 us
  local copies, waits for them, and re-layouts: 61.4 us -> 73.8 us
    ppermute x13 -> x12, waiting for transfers between devices: 156 us -> 132 us  [from_inner(): lax.ppermute(values, 'inner', [((i + k) % inner, i) for i in range(inner)])]
    unnamed x208 -> x202, local copies, waits for them, and re-layouts: 48 us -> 54.7 us
    pallas_call x1 -> x2, Pallas kernels: 12.1 us -> 17.4 us  [weight_slots(): pl.pallas_call(kernel, grid=(inner * tiles,), in_specs=[row_spec, row_spe...]
    ppermute x17 -> x19, waiting for transfers between devices: 61.1 us -> 57.6 us  [swap(): return lax.ppermute(values, axis, [(0, 1), (1, 0)])]
    ppermute x13 -> x12, starting transfers between devices: 18 us -> 16 us  [from_inner(): lax.ppermute(values, 'inner', [((i + k) % inner, i) for i in range(inner)])]
  transfers between devices with their start and end apart: 38 -> 42, of which waited for: 26 -> 23; matrix products, arithmetic and copies ran while one was open for 7% -> 9% of each run, Pallas kernels for 34% -> 34%
where the time goes in v3:
time: 640 us; the launch traced here: 632 us
  waiting for transfers between devices  260 us (41%)
  Pallas kernels  214 us (33%)
  local copies, waits for them, and re-layouts  73.8 us (12%)
  other arithmetic  38.3 us (6%)
  starting transfers between devices  29.8 us (5%)
  between operations  15.3 us (2%)
    ppermute x12, waiting for transfers between devices, from_inner(): lax.ppermute(values, 'inner', [((i + k) % inner, i) for i in range(inner)])  132 us
    all_gather x4, waiting for transfers between devices, gather(): return lax.all_gather(values, 'outer', axis=0, tiled=True)  66.7 us
    ppermute x19, waiting for transfers between devices, swap(): return lax.ppermute(values, axis, [(0, 1), (1, 0)])  57.6 us
    pallas_call x8, Pallas kernels, back_rows(): pl.pallas_call(kernel, grid=(width // tile,), in_specs=specs, out_specs=s...  56.4 us
    unnamed x202, local copies, waits for them, and re-layouts  54.7 us
    pallas_call x8, Pallas kernels, weight_part(): pl.pallas_call(kernel, grid=(tiles,), in_specs=[row_spec, row_spec] + [wh...  42 us
    pallas_call x3, Pallas kernels, through(): pl.pallas_call(kernel, grid=(2,), in_specs=of_group(near, far, 2) + resid...  24.2 us
    pallas_call x6, Pallas kernels, row_call(): pl.pallas_call(kernel, grid=(rows // tile,), in_specs=[pl.BlockSpec(memor...  18.7 us
  transfers between devices with their start and end apart: 42, of which 23 were waited for; matrix products, arithmetic and copies ran while one was open for 9% of the time, Pallas kernels for 34%

profile of v3, /device:TPU:0, one launch (start us, length us, event | category | flops | bytes accessed | tf_op | source)
XLA Modules:
  0.0 631.6 jit_solution(3792291994927132515)
XLA Ops:
  19.8 14.3 %collective-permute-done.3 = bf16[256,1408]{1,0:T(8,128)(2,1)} collective-permute-done((bf16[256,1408]{1,0:T(8,128)(2,1)}, bf16[256,1408]{1,0:T(8,128)(2,1)}, u32[]{:S(2)}, u32[]{:S(2)}) %collective-permute-start.3) | collective-permute-done | bytes 720928 | tf_op jit(solution)/shard_map/ppermute | solution.py:697
  36.7 8.7 %collective-permute-done.2 = f32[320]{0:T(512)S(1)} collective-permute-done((f32[320]{0:T(512)S(1)}, f32[320]{0:T(512)S(1)}, u32[]{:S(2)}, u32[]{:S(2)}) %collective-permute-start.2) | collective-permute-done | bytes 1312 | tf_op jit(solution)/shard_map/ppermute | solution.py:700
  51.9 23.2 %all-gather.5.cloned.1.call-done.refs_0_.refs_2_.refs_1_ = bf16[1024,1408]{1,0:T(8,128)(2,1)} async-done(((bf16[256,1408]{1,0:T(8,128)(2,1)}), bf16[1024,1408]{1,0:T(8,128)(2,1)}) %all-gather.5.cloned.1.call-update) | async-done | bytes 2883600 | tf_op jit(solution)/shard_map/all_gather | solution.py:706
  82.9 3.0 kept.1.refs_0_.near_rows
  86.0 5.2 collective-permute-done.6.refs_1_.far_rows
  91.2 43.4 %all-gather.7.cloned.1.call-done.refs_2_.refs_1_ = bf16[1024,1408]{1,0:T(8,128)(2,1)} async-done(((bf16[256,1408]{1,0:T(8,128)(2,1)}), bf16[1024,1408]{1,0:T(8,128)(2,1)}) %all-gather.7.cloned.1.call-update) | async-done | bytes 2883600 | tf_op jit(solution)/shard_map/all_gather | solution.py:706
  134.6 5.0 collective-permute-done.5.refs_1_.refs_3_.refs_2_
  147.2 4.1 norm_far.1.refs_1_.far_rows
  151.3 7.2 %joint.1.operands_1_ = f32[1280,768]{1,0:T(8,128)S(1)} custom-call(bf16[640,2048]{1,0:T(8,128)(2,1)S(1)} %norm_near.1.refs_0_.near_rows, bf16[640,2048]{1,0:T(8,128)(2,1)S(1)} %norm_far.1.refs_1_.far_rows, bf16[1024,1408]{1,0:T(8,128)(2,1)S(1)} %copy-done, bf16[1024,1408]{1,0:T(8,128)(2,1)} %collective-permute-done.5.refs_1_.refs_3_.refs_2_), custom_call_target="tpu_custom_call" | custom-call | flops 1006632960 | bytes 2097152 | tf_op jit(solution)/shard_map/joint/pallas_call | solution.py:421
  164.5 10.0 %attend.1 = (bf16[640,512]{1,0:T(8,128)(2,1)S(1)}, bf16[640,512]{1,0:T(8,128)(2,1)S(1)}, bf16[1280,768]{1,0:T(8,128)(2,1)S(1)}) custom-call(s32[14]{0:T(128)S(1)} %concatenate.37.operands_0_, f32[1280,768]{1,0:T(8,128)S(1)} %joint.1.operands_1_, f32[1280,128]{1,0:T(8,128)S(1)} %get-tuple-element.200.operands_2_.operands_3_, ...), custom_call_target="tpu_custom_call" | custom-call | flops 1476395008 | bytes 1966080 | tf_op jit(solution)/shard_map/attend/pallas_call | solution.py:799
  176.5 5.8 attended_far.1
  186.3 4.9 attended_near.1
  191.3 4.4 add_convert_fusion.3.mine
  195.7 8.3 %collective-permute-done.10.refs_5_.refs_4_ = bf16[256,1408]{1,0:T(8,128)(2,1)} collective-permute-done((bf16[256,1408]{1,0:T(8,128)(2,1)}, bf16[256,1408]{1,0:T(8,128)(2,1)}, u32[]{:S(2)}, u32[]{:S(2)}) %collective-permute-start.10) | collective-permute-done | bytes 720928 | tf_op jit(solution)/shard_map/ppermute | solution.py:697
  207.5 17.3 %collective-permute-done.12.refs_6_.refs_5_ = bf16[256,1408]{1,0:T(8,128)(2,1)S(1)} collective-permute-done((bf16[256,1408]{1,0:T(8,128)(2,1)}, bf16[256,1408]{1,0:T(8,128)(2,1)S(1)}, u32[]{:S(2)}, u32[]{:S(2)}) %collective-permute-start.12) | collective-permute-done | bytes 720928 | tf_op jit(solution)/shard_map/ppermute | solution.py:697
  227.8 11.7 %hidden_grad.1.refs_2_ = bf16[1280,1408]{1,0:T(8,128)(2,1)S(1)} custom-call(bf16[640,2048]{1,0:T(8,128)(2,1)} %kept.1.refs_0_.near_rows, bf16[640,2048]{1,0:T(8,128)(2,1)} %collective-permute-done.6.refs_1_.far_rows, bf16[1024,1408]{1,0:T(8,128)(2,1)S(1)} %copy-done.17, bf16[256,1408]{1,0:T(8,128)(2,1)} %collective-permute-done.7.refs_3_.refs_2_, ...), custom_call_target="tpu_custom_call" | custom-call | flops 1845493760 | bytes 2752512 | tf_op jit(solution)/shard_map/hidden_grad/pallas_call | solution.py:421
  239.5 23.2 %collective-permute-done.11.got = bf16[640,2048]{1,0:T(8,128)(2,1)S(1)} collective-permute-done((bf16[640,2048]{1,0:T(8,128)(2,1)}, bf16[640,2048]{1,0:T(8,128)(2,1)S(1)}, u32[]{:S(2)}, u32[]{:S(2)}) %collective-permute-start.11) | collective-permute-done | bytes 2621472 | tf_op jit(solution)/shard_map/ppermute | solution.py:700
  267.8 17.1 %collective-permute-done.14.refs_4_.refs_2_ = bf16[1024,1408]{1,0:T(8,128)(2,1)S(1)} collective-permute-done((bf16[1024,1408]{1,0:T(8,128)(2,1)}, bf16[1024,1408]{1,0:T(8,128)(2,1)S(1)}, u32[]{:S(2)}, u32[]{:S(2)}) %collective-permute-start.14) | collective-permute-done | bytes 2883616 | tf_op jit(solution)/shard_map/ppermute | solution.py:697
  285.0 11.4 %gate.1 = (f32[1280,1408]{1,0:T(8,128)}, bf16[1280,1408]{1,0:T(8,128)(2,1)S(1)}) custom-call(bf16[640,2048]{1,0:T(8,128)(2,1)S(1)} %get-tuple-element.123.refs_0_.near_rows, bf16[640,2048]{1,0:T(8,128)(2,1)S(1)} %collective-permute-done.13.refs_1_.far_rows, bf16[1280,1408]{1,0:T(8,128)(2,1)S(1)} %hidden_grad.1.refs_2_, bf16[1024,1408]{1,0:T(8,128)(2,1)S(1)} %copy-done.29, ...), custom_call_target="tpu_custom_call" | custom-call | flops 1845493760 | bytes 2752512 | tf_op jit(solution)/shard_map/gate/pallas_call | solution.py:452
  296.4 12.1 %grad_up_late.1 = bf16[1024,2816]{1,0:T(8,128)(2,1)} custom-call(bf16[640,2048]{1,0:T(8,128)(2,1)S(1)} %get-tuple-element.123.refs_0_.near_rows, bf16[640,2048]{1,0:T(8,128)(2,1)S(1)} %collective-permute-done.13.refs_1_.far_rows, bf16[1280,1408]{1,0:T(8,128)(2,1)S(1)} %get-tuple-element.138.refs_0_.refs_3_), custom_call_target="tpu_custom_call" | custom-call | flops 1845493760 | bytes 1556480 | tf_op jit(solution)/shard_map/grad_up_late/pallas_call | solution.py:648
  319.1 12.7 %up.1 = (bf16[1280,1408]{1,0:T(8,128)(2,1)S(1)}, bf16[1280,1408]{1,0:T(8,128)(2,1)S(1)}) custom-call(bf16[640,2048]{1,0:T(8,128)(2,1)S(1)} %copy-done.4, bf16[640,2048]{1,0:T(8,128)(2,1)S(1)} %copy-done.8, bf16[1280,1408]{1,0:T(8,128)(2,1)S(1)} %copy-done.28, f32[1280,1408]{1,0:T(8,128)} %get-tuple-element.128.refs_3_, bf16[1024,2816]{1,0:T(8,128)(2,1)S(1)} %copy-done.1), custom_call_target="tpu_custom_call" | custom-call | flops 1845493760 | bytes 2752512 | tf_op jit(solution)/shard_map/up/pallas_call | solution.py:503
  331.9 9.2 %grad_down.2 = bf16[1024,1408]{1,0:T(8,128)(2,1)} custom-call(bf16[640,2048]{1,0:T(8,128)(2,1)} %kept.1.refs_0_.near_rows, bf16[640,2048]{1,0:T(8,128)(2,1)} %collective-permute-done.6.refs_1_.far_rows, bf16[1280,1408]{1,0:T(8,128)(2,1)S(1)} %get-tuple-element.143.refs_0_), custom_call_target="tpu_custom_call" | custom-call | flops 922746880 | bytes 1556480 | tf_op jit(solution)/shard_map/grad_down/pallas_call | solution.py:612
  343.2 9.2 %normed_ff_grad_far.1 = bf16[640,2048]{1,0:T(8,128)(2,1)S(1)} custom-call(bf16[1280,1408]{1,0:T(8,128)(2,1)S(1)} %copy-done.13, bf16[1024,1408]{1,0:T(8,128)(2,1)S(1)} %copy-done.30, bf16[1024,1408]{1,0:T(8,128)(2,1)S(1)} %copy-done.32, bf16[1280,1408]{1,0:T(8,128)(2,1)S(1)} %copy-done.26, bf16[1024,2816]{1,0:T(8,128)(2,1)S(1)} %copy-done.2, ...), custom_call_target="tpu_custom_call" | custom-call | flops 1845493760 | bytes 6127616 | tf_op jit(solution)/shard_map/normed_ff_grad_far/pallas_call | solution.py:570
  354.2 4.9 grad_gate.2
  359.1 10.5 %normed_ff_grad_near.1.mine = bf16[640,2048]{1,0:T(8,128)(2,1)} custom-call(bf16[1280,1408]{1,0:T(8,128)(2,1)S(1)} %copy-done.13, bf16[1024,1408]{1,0:T(8,128)(2,1)S(1)} %copy-done.30, bf16[1024,1408]{1,0:T(8,128)(2,1)S(1)} %copy-done.32, bf16[1280,1408]{1,0:T(8,128)(2,1)S(1)} %copy-done.26, bf16[1024,2816]{1,0:T(8,128)(2,1)S(1)} %copy-done.2, ...), custom_call_target="tpu_custom_call" | custom-call | flops 1845493760 | bytes 6782976 | tf_op jit(solution)/shard_map/normed_ff_grad_near/pallas_call | solution.py:570
  371.4 5.4 grad_gate_first.1
  384.0 5.0 grad_gate.3
  389.0 8.1 %grad_down.3 = bf16[1024,1408]{1,0:T(8,128)(2,1)} custom-call(bf16[640,2048]{1,0:T(8,128)(2,1)} %kept.1.refs_0_.near_rows, bf16[640,2048]{1,0:T(8,128)(2,1)} %collective-permute-done.6.refs_1_.far_rows, bf16[1280,1408]{1,0:T(8,128)(2,1)S(1)} %copy-done.16), custom_call_target="tpu_custom_call" | custom-call | flops 922746880 | bytes 1556480 | tf_op jit(solution)/shard_map/grad_down/pallas_call | solution.py:612
  397.0 7.5 %branch_near.1 = bf16[640,2048]{1,0:T(8,128)(2,1)S(1)} custom-call(bf16[1280,1408]{1,0:T(8,128)(2,1)S(1)} %copy-done.16, bf16[1024,1408]{1,0:T(8,128)(2,1)S(1)} %copy-done.18, bf16[256,1408]{1,0:T(8,128)(2,1)} %collective-permute-done.7.refs_3_.refs_2_, bf16[256,1408]{1,0:T(8,128)(2,1)S(1)} %copy-done.58, ...), custom_call_target="tpu_custom_call" | custom-call | flops 922746880 | bytes 2342912 | tf_op jit(solution)/shard_map/branch_near/pallas_call | solution.py:570
  406.0 7.6 %branch_far.1 = bf16[640,2048]{1,0:T(8,128)(2,1)S(1)} custom-call(bf16[1280,1408]{1,0:T(8,128)(2,1)S(1)} %copy-done.16, bf16[1024,1408]{1,0:T(8,128)(2,1)S(1)} %copy-done.18, bf16[256,1408]{1,0:T(8,128)(2,1)} %collective-permute-done.7.refs_3_.refs_2_, bf16[256,1408]{1,0:T(8,128)(2,1)S(1)} %copy-done.58, ...), custom_call_target="tpu_custom_call" | custom-call | flops 922746880 | bytes 2342912 | tf_op jit(solution)/shard_map/branch_far/pallas_call | solution.py:570
  415.2 26.8 %collective-permute-done.17 = bf16[1024,1408]{1,0:T(8,128)(2,1)S(1)} collective-permute-done((bf16[1024,1408]{1,0:T(8,128)(2,1)}, bf16[1024,1408]{1,0:T(8,128)(2,1)S(1)}, u32[]{:S(2)}, u32[]{:S(2)}) %collective-permute-start.17) | collective-permute-done | bytes 2883616 | tf_op jit(solution)/shard_map/ppermute | solution.py:697
  450.3 4.9 middle_back.1
  458.9 3.5 collective-permute-done.18.far_rows.refs_1_
  462.4 3.2 grad_output.3
  465.6 5.2 mixed_grad.1.operands_2_
  470.9 16.1 %attend_back.1 = (bf16[640,768]{1,0:T(8,128)(2,1)S(1)}, bf16[640,768]{1,0:T(8,128)(2,1)S(1)}) custom-call(s32[14]{0:T(128)S(1)} %concatenate.37.operands_0_, bf16[1280,768]{1,0:T(8,128)(2,1)S(1)} %copy-done.84, bf16[1280,512]{1,0:T(8,128)(2,1)S(1)} %mixed_grad.1.operands_2_, f32[1280,128]{1,0:T(8,128)S(1)} %copy-done.76, f32[1280,128]{1,0:T(8,128)S(1)} %copy-done.78), custom_call_target="tpu_custom_call" | custom-call | flops 2214592512 | bytes 1966080 | tf_op jit(solution)/shard_map/attend_back/pallas_call | solution.py:928
  487.0 5.8 normed_grad_near.1
  492.8 4.1 grad_joint.2
  497.0 5.1 normed_grad_far.1
  504.1 3.8 add_convert_fusion.4
  509.5 3.7 add_convert_fusion.2.mine
  516.5 4.8 add_convert_fusion.1.mine
  521.4 3.4 grad_output.2
  524.8 4.1 grad_joint.3
  529.0 38.1 %collective-permute-done.19 = bf16[1024,512]{1,0:T(8,128)(2,1)S(1)} collective-permute-done((bf16[1024,512]{1,0:T(8,128)(2,1)S(1)}, bf16[1024,512]{1,0:T(8,128)(2,1)S(1)}, u32[]{:S(2)}, u32[]{:S(2)}) %collective-permute-start.19) | collective-permute-done | bytes 1048608 | tf_op jit(solution)/shard_map/ppermute | solution.py:697
  590.0 3.2 input_grad.1
  604.6 9.8 %collective-permute-done.32 = f32[1,256]{1,0:T(1,128)S(1)} collective-permute-done((f32[1,256]{1,0:T(1,128)S(1)}, f32[1,256]{1,0:T(1,128)S(1)}, u32[]{:S(2)}, u32[]{:S(2)}) %collective-permute-start.32) | collective-permute-done | bytes 1056 | tf_op jit(solution)/shard_map/ppermute | solution.py:700
  617.0 3.9 reduce-scatter.12.cloned.1.call-done
  (331 shorter events, 146.4 us)
Async XLA Ops:
  7.2 68.0 %all-gather.5.cloned.1.call-start = ((), (), s32[]{:S(2)}) async-start(), calls=%async_computation.5 | async-start | bytes 3604480 | tf_op jit(solution)/shard_map/all_gather | solution.py:706
  13.1 121.5 %all-gather.7.cloned.1.call-start = ((), (), s32[]{:S(2)}) async-start(), calls=%async_computation.6 | async-start | bytes 3604480 | tf_op jit(solution)/shard_map/all_gather | solution.py:706
  13.2 32.2 %collective-permute-start.1 = (bf16[320,2048]{1,0:T(8,128)(2,1)}, bf16[320,2048]{1,0:T(8,128)(2,1)}, u32[]{:S(2)}, u32[]{:S(2)}) collective-permute-start(bf16[320,2048]{1,0:T(8,128)(2,1)} %rows.1), channel_id=1, source_target_pairs={{0,2},{2,0},{1,3},{3,1},{4,6},{6,4},{5,7},{7,5},{8,10},{10,8},{9,1... | collective-permute-start | bytes 3932168 | tf_op jit(solution)/shard_map/ppermute | solution.py:700
  16.2 17.9 %collective-permute-start.3 = (bf16[256,1408]{1,0:T(8,128)(2,1)}, bf16[256,1408]{1,0:T(8,128)(2,1)}, u32[]{:S(2)}, u32[]{:S(2)}) collective-permute-start(bf16[256,1408]{1,0:T(8,128)(2,1)} %param.23), channel_id=1, source_target_pairs={{4,0},{0,4},{5,1},{1,5},{6,2},{2,6},{7,3},{3,7},{12,8},{8,12},{13,... | collective-permute-start | bytes 2162696 | tf_op jit(solution)/shard_map/ppermute | solution.py:697
  17.7 178.0 %all-gather.9.cloned.1.call-start = ((), (), s32[]{:S(2)}) async-start(), calls=%async_computation.7 | async-start | bytes 3604480 | tf_op jit(solution)/shard_map/all_gather | solution.py:706
  17.8 27.5 %collective-permute-start.2 = (f32[320]{0:T(512)S(1)}, f32[320]{0:T(512)S(1)}, u32[]{:S(2)}, u32[]{:S(2)}) collective-permute-start(f32[320]{0:T(512)S(1)} %subtract_convert_fusion), channel_id=1, source_target_pairs={{0,2},{2,0},{1,3},{3,1},{4,6},{6,4},{5,7},{7,5},{8,10},{10,8},{9,1... | collective-permute-start | bytes 3848 | tf_op jit(solution)/shard_map/ppermute | solution.py:700
  46.8 5.1 collective-permute-start.4
  46.9 31.5 %collective-permute-start = (bf16[320,2048]{1,0:T(8,128)(2,1)}, bf16[320,2048]{1,0:T(8,128)(2,1)}, u32[]{:S(2)}, u32[]{:S(2)}) collective-permute-start(bf16[320,2048]{1,0:T(8,128)(2,1)} %param.25), channel_id=1, source_target_pairs={{0,2},{2,0},{1,3},{3,1},{4,6},{6,4},{5,7},{7,5},{8,10},{10,8},{9,1... | collective-permute-start | bytes 3932168 | tf_op jit(solution)/shard_map/ppermute | solution.py:700
  75.2 64.5 %collective-permute-start.5 = (bf16[1024,1408]{1,0:T(8,128)(2,1)}, bf16[1024,1408]{1,0:T(8,128)(2,1)}, u32[]{:S(2)}, u32[]{:S(2)}) collective-permute-start(bf16[1024,1408]{1,0:T(8,128)(2,1)} %all-gather.5.cloned.1.call-done.refs_0_.refs_2_.refs_1_), channel_id=1, source_target_pairs={{4,0},{0,4},{5,1},{1,5},{6,2},{2,6},{7,3},{3,7},{12,8},{8,12},{13,... | collective-permute-start | bytes 8650760 | tf_op jit(solution)/shard_map/ppermute | solution.py:697
  82.9 60.2 %copy-start.97 = (s32[1,10]{1,0:T(1,128)S(1)}, s32[1,10]{1,0:T(1,128)}, u32[]{:S(2)}) copy-start(s32[1,10]{1,0:T(1,128)} %param.15) | copy-start | bytes 124
  82.9 60.3 %copy-start = (bf16[1024,1408]{1,0:T(8,128)(2,1)S(1)}, bf16[1024,1408]{1,0:T(8,128)(2,1)}, u32[]{:S(2)}) copy-start(bf16[1024,1408]{1,0:T(8,128)(2,1)} %all-gather.5.cloned.1.call-done.refs_0_.refs_2_.refs_1_) | copy-start | bytes 8650756
  86.0 5.3 collective-permute-start.6
  86.0 224.4 %all-gather.11.cloned.1.call-start = ((), (), s32[]{:S(2)}) async-start(), calls=%async_computation.8 | async-start | bytes 7208960 | tf_op jit(solution)/shard_map/all_gather | solution.py:706
  141.7 17.3 %collective-permute-start.7 = (bf16[256,1408]{1,0:T(8,128)(2,1)}, bf16[256,1408]{1,0:T(8,128)(2,1)}, u32[]{:S(2)}, u32[]{:S(2)}) collective-permute-start(bf16[256,1408]{1,0:T(8,128)(2,1)} %slice.58), channel_id=1, source_target_pairs={{4,0},{0,4},{5,1},{1,5},{6,2},{2,6},{7,3},{3,7},{12,8},{8,12},{13,... | collective-permute-start | bytes 2162696 | tf_op jit(solution)/shard_map/ppermute | solution.py:697
  160.1 16.4 %collective-permute-start.8 = (bf16[256,1408]{1,0:T(8,128)(2,1)S(1)}, bf16[256,1408]{1,0:T(8,128)(2,1)S(1)}, u32[]{:S(2)}, u32[]{:S(2)}) collective-permute-start(bf16[256,1408]{1,0:T(8,128)(2,1)S(1)} %slice.59), channel_id=1, source_target_pairs={{4,0},{0,4},{5,1},{1,5},{6,2},{2,6},{7,3},{3,7},{12,8},{8,12},{13,... | collective-permute-start | bytes 2162696 | tf_op jit(solution)/shard_map/ppermute | solution.py:697
  182.4 8.9 %collective-permute-start.9 = (bf16[640,2048]{1,0:T(8,128)(2,1)}, bf16[640,2048]{1,0:T(8,128)(2,1)}, u32[]{:S(2)}, u32[]{:S(2)}) collective-permute-start(bf16[640,2048]{1,0:T(8,128)(2,1)} %attended_far.1), channel_id=1, source_target_pairs={{0,1},{1,0},{2,3},{3,2},{4,5},{5,4},{6,7},{7,6},{8,9},{9,8},{10,11... | collective-permute-start | bytes 7864328 | tf_op jit(solution)/shard_map/ppermute | solution.py:700
  182.5 321.1 %reduce-scatter.6.cloned.1.call-start = ((), (), s32[]{:S(2)}) async-start(), calls=%async_computation.9 | async-start | bytes 7208960 | tf_op jit(solution)/shard_map/reduce_scatter | solution.py:709
  185.1 18.9 %collective-permute-start.10 = (bf16[256,1408]{1,0:T(8,128)(2,1)}, bf16[256,1408]{1,0:T(8,128)(2,1)}, u32[]{:S(2)}, u32[]{:S(2)}) collective-permute-start(bf16[256,1408]{1,0:T(8,128)(2,1)} %get-tuple-element.188), channel_id=1, source_target_pairs={{4,0},{0,4},{5,1},{1,5},{6,2},{2,6},{7,3},{3,7},{12,8},{8,12},{13,... | collective-permute-start | bytes 2162696 | tf_op jit(solution)/shard_map/ppermute | solution.py:697
  204.0 58.7 %collective-permute-start.11 = (bf16[640,2048]{1,0:T(8,128)(2,1)}, bf16[640,2048]{1,0:T(8,128)(2,1)S(1)}, u32[]{:S(2)}, u32[]{:S(2)}) collective-permute-start(bf16[640,2048]{1,0:T(8,128)(2,1)} %add_convert_fusion.3.mine), channel_id=1, source_target_pairs={{0,2},{2,0},{1,3},{3,1},{4,6},{6,4},{5,7},{7,5},{8,10},{10,8},{9,1... | collective-permute-start | bytes 7864328 | tf_op jit(solution)/shard_map/ppermute | solution.py:700
  205.5 19.3 %collective-permute-start.12 = (bf16[256,1408]{1,0:T(8,128)(2,1)}, bf16[256,1408]{1,0:T(8,128)(2,1)S(1)}, u32[]{:S(2)}, u32[]{:S(2)}) collective-permute-start(bf16[256,1408]{1,0:T(8,128)(2,1)} %get-tuple-element.187), channel_id=1, source_target_pairs={{4,0},{0,4},{5,1},{1,5},{6,2},{2,6},{7,3},{3,7},{12,8},{8,12},{13,... | collective-permute-start | bytes 2162696 | tf_op jit(solution)/shard_map/ppermute | solution.py:697
  206.7 78.3 %collective-permute-start.14 = (bf16[1024,1408]{1,0:T(8,128)(2,1)}, bf16[1024,1408]{1,0:T(8,128)(2,1)S(1)}, u32[]{:S(2)}, u32[]{:S(2)}) collective-permute-start(bf16[1024,1408]{1,0:T(8,128)(2,1)} %all-gather.9.cloned.1.call-done.refs_3_.refs_1_), channel_id=1, source_target_pairs={{4,0},{0,4},{5,1},{1,5},{6,2},{2,6},{7,3},{3,7},{12,8},{8,12},{13,... | collective-permute-start | bytes 8650760 | tf_op jit(solution)/shard_map/ppermute | solution.py:697
  239.5 45.5 %copy-start.27 = (bf16[1280,1408]{1,0:T(8,128)(2,1)}, bf16[1280,1408]{1,0:T(8,128)(2,1)S(1)}, u32[]{:S(2)}) copy-start(bf16[1280,1408]{1,0:T(8,128)(2,1)S(1)} %hidden_grad.1.refs_2_) | copy-start | bytes 10813444
  267.8 17.2 %collective-permute-start.13 = (bf16[640,2048]{1,0:T(8,128)(2,1)S(1)}, bf16[640,2048]{1,0:T(8,128)(2,1)S(1)}, u32[]{:S(2)}, u32[]{:S(2)}) collective-permute-start(bf16[640,2048]{1,0:T(8,128)(2,1)S(1)} %get-tuple-element.123.refs_0_.near_rows), channel_id=1, source_target_pairs={{0,1},{1,0},{2,3},{3,2},{4,5},{5,4},{6,7},{7,6},{8,9},{9,8},{10,11... | collective-permute-start | bytes 7864328 | tf_op jit(solution)/shard_map/ppermute | solution.py:700
  310.4 259.5 %reduce-scatter.10.cloned.1.call-start = ((), (), s32[]{:S(2)}) async-start(), calls=%async_computation.11 | async-start | bytes 2621440 | tf_op jit(solution)/shard_map/reduce_scatter | solution.py:709
  352.4 6.7 %collective-permute-start.15 = (bf16[640,2048]{1,0:T(8,128)(2,1)S(1)}, bf16[640,2048]{1,0:T(8,128)(2,1)S(1)}, u32[]{:S(2)}, u32[]{:S(2)}) collective-permute-start(bf16[640,2048]{1,0:T(8,128)(2,1)S(1)} %normed_ff_grad_far.1), channel_id=1, source_target_pairs={{0,1},{1,0},{2,3},{3,2},{4,5},{5,4},{6,7},{7,6},{8,9},{9,8},{10,11... | collective-permute-start | bytes 7864328 | tf_op jit(solution)/shard_map/ppermute | solution.py:700
  376.8 193.1 %reduce-scatter.8.cloned.1.call-start = ((), (), s32[]{:S(2)}) async-start(), calls=%async_computation.10 | async-start | bytes 3604480 | tf_op jit(solution)/shard_map/reduce_scatter | solution.py:709
  376.8 65.1 %collective-permute-start.17 = (bf16[1024,1408]{1,0:T(8,128)(2,1)}, bf16[1024,1408]{1,0:T(8,128)(2,1)S(1)}, u32[]{:S(2)}, u32[]{:S(2)}) collective-permute-start(bf16[1024,1408]{1,0:T(8,128)(2,1)} %grad_down.2), channel_id=1, source_target_pairs={{4,0},{0,4},{5,1},{1,5},{6,2},{2,6},{7,3},{3,7},{12,8},{8,12},{13,... | collective-permute-start | bytes 8650760 | tf_op jit(solution)/shard_map/ppermute | solution.py:697
  378.3 66.0 %collective-permute-start.16 = (bf16[640,2048]{1,0:T(8,128)(2,1)}, bf16[640,2048]{1,0:T(8,128)(2,1)}, u32[]{:S(2)}, u32[]{:S(2)}) collective-permute-start(bf16[640,2048]{1,0:T(8,128)(2,1)} %normed_ff_grad_near.1.mine), channel_id=1, source_target_pairs={{0,2},{2,0},{1,3},{3,1},{4,6},{6,4},{5,7},{7,5},{8,10},{10,8},{9,1... | collective-permute-start | bytes 7864328 | tf_op jit(solution)/shard_map/ppermute | solution.py:700
  406.0 36.0 %copy-start.86 = (bf16[1024,1408]{1,0:T(8,128)(2,1)S(1)}, bf16[1024,1408]{1,0:T(8,128)(2,1)}, u32[]{:S(2)}) copy-start(bf16[1024,1408]{1,0:T(8,128)(2,1)} %grad_down.3) | copy-start | bytes 8650756
  444.3 137.1 %reduce-scatter.14.cloned.1.call-start = ((), (), s32[]{:S(2)}) async-start(), calls=%async_computation.13 | async-start | bytes 2293760 | tf_op jit(solution)/shard_map/reduce_scatter | solution.py:709
  457.5 4.9 collective-permute-start.18
  457.5 46.1 %collective-permute-start.20 = (bf16[1024,896]{1,0:T(8,128)(2,1)S(1)}, bf16[1024,896]{1,0:T(8,128)(2,1)}, u32[]{:S(2)}, u32[]{:S(2)}) collective-permute-start(bf16[1024,896]{1,0:T(8,128)(2,1)S(1)} %copy-done.92), channel_id=1, source_target_pairs={{4,0},{0,4},{5,1},{1,5},{6,2},{2,6},{7,3},{3,7},{12,8},{8,12},{13,... | collective-permute-start | bytes 5505032 | tf_op jit(solution)/shard_map/ppermute | solution.py:697
  503.6 5.9 collective-permute-start.22
  503.7 12.8 %collective-permute-start.24 = (bf16[640,2048]{1,0:T(8,128)(2,1)}, bf16[640,2048]{1,0:T(8,128)(2,1)}, u32[]{:S(2)}, u32[]{:S(2)}) collective-permute-start(bf16[640,2048]{1,0:T(8,128)(2,1)} %copy-done.71), channel_id=1, source_target_pairs={{0,1},{1,0},{2,3},{3,2},{4,5},{5,4},{6,7},{7,6},{8,9},{9,8},{10,11... | collective-permute-start | bytes 7864328 | tf_op jit(solution)/shard_map/ppermute | solution.py:700
  507.9 113.1 %reduce-scatter.12.cloned.1.call-start = ((), (), s32[]{:S(2)}) async-start(), calls=%async_computation.12 | async-start | bytes 3276800 | tf_op jit(solution)/shard_map/reduce_scatter | solution.py:709
  507.9 59.2 %collective-permute-start.21 = (bf16[1024,768]{1,0:T(8,128)(2,1)}, bf16[1024,768]{1,0:T(8,128)(2,1)S(1)}, u32[]{:S(2)}, u32[]{:S(2)}) collective-permute-start(bf16[1024,768]{1,0:T(8,128)(2,1)} %grad_joint.2), channel_id=1, source_target_pairs={{4,0},{0,4},{5,1},{1,5},{6,2},{2,6},{7,3},{3,7},{12,8},{8,12},{13,... | collective-permute-start | bytes 4718600 | tf_op jit(solution)/shard_map/ppermute | solution.py:697
  514.9 52.2 %collective-permute-start.23 = (bf16[320,2048]{1,0:T(8,128)(2,1)S(1)}, bf16[320,2048]{1,0:T(8,128)(2,1)S(1)}, u32[]{:S(2)}, u32[]{:S(2)}) collective-permute-start(bf16[320,2048]{1,0:T(8,128)(2,1)S(1)} %slice.76), channel_id=1, source_target_pairs={{0,2},{2,0},{1,3},{3,1},{4,6},{6,4},{5,7},{7,5},{8,10},{10,8},{9,1... | collective-permute-start | bytes 3932168 | tf_op jit(solution)/shard_map/ppermute | solution.py:700
  515.6 51.4 %collective-permute-start.19 = (bf16[1024,512]{1,0:T(8,128)(2,1)S(1)}, bf16[1024,512]{1,0:T(8,128)(2,1)S(1)}, u32[]{:S(2)}, u32[]{:S(2)}) collective-permute-start(bf16[1024,512]{1,0:T(8,128)(2,1)S(1)} %copy-done.93), channel_id=1, source_target_pairs={{4,0},{0,4},{5,1},{1,5},{6,2},{2,6},{7,3},{3,7},{12,8},{8,12},{13,... | collective-permute-start | bytes 3145736 | tf_op jit(solution)/shard_map/ppermute | solution.py:697
  524.8 42.3 %copy-start.88 = (bf16[1024,512]{1,0:T(8,128)(2,1)S(1)}, bf16[1024,512]{1,0:T(8,128)(2,1)}, u32[]{:S(2)}) copy-start(bf16[1024,512]{1,0:T(8,128)(2,1)} %grad_output.2) | copy-start | bytes 3145732
  529.0 38.5 %copy-start.87 = (bf16[1024,768]{1,0:T(8,128)(2,1)S(1)}, bf16[1024,768]{1,0:T(8,128)(2,1)}, u32[]{:S(2)}) copy-start(bf16[1024,768]{1,0:T(8,128)(2,1)} %grad_joint.3) | copy-start | bytes 4718596
  574.5 23.3 %collective-permute-start.30 = (bf16[256,1920]{1,0:T(8,128)(2,1)}, bf16[256,1920]{1,0:T(8,128)(2,1)}, u32[]{:S(2)}, u32[]{:S(2)}) collective-permute-start(bf16[256,1920]{1,0:T(8,128)(2,1)} %pad_maximum_fusion.3), channel_id=1, source_target_pairs={{4,0},{0,4},{5,1},{1,5},{6,2},{2,6},{7,3},{3,7},{12,8},{8,12},{13,... | collective-permute-start | bytes 2949128 | tf_op jit(solution)/shard_map/ppermute | solution.py:697
  576.5 1.2 collective-permute-start.26
  577.7 3.6 collective-permute-start.27
  581.3 11.9 %collective-permute-start.28 = (f32[1,1024]{1,0:T(1,128)S(1)}, f32[1,1024]{1,0:T(1,128)S(1)}, u32[]{:S(2)}, u32[]{:S(2)}) collective-permute-start(f32[1,1024]{1,0:T(1,128)S(1)} %add.203), channel_id=1, source_target_pairs={{8,0},{0,8},{24,16},{16,24},{9,1},{1,9},{25,17},{17,25},{10,2},{2,... | collective-permute-start | bytes 12296 | tf_op jit(solution)/shard_map/ppermute | solution.py:1014
  584.2 30.8 %collective-permute-start.25 = (bf16[320,2048]{1,0:T(8,128)(2,1)S(1)}, bf16[320,2048]{1,0:T(8,128)(2,1)S(1)}, u32[]{:S(2)}, u32[]{:S(2)}) collective-permute-start(bf16[320,2048]{1,0:T(8,128)(2,1)S(1)} %slice.63), channel_id=1, source_target_pairs={{0,2},{2,0},{1,3},{3,1},{4,6},{6,4},{5,7},{7,5},{8,10},{10,8},{9,1... | collective-permute-start | bytes 3932168 | tf_op jit(solution)/shard_map/ppermute | solution.py:700
  593.3 8.5 %collective-permute-start.29 = (f32[1,1024]{1,0:T(1,128)S(1)}, f32[1,1024]{1,0:T(1,128)S(1)}, u32[]{:S(2)}, u32[]{:S(2)}) collective-permute-start(f32[1,1024]{1,0:T(1,128)S(1)} %add.204), channel_id=1, source_target_pairs={{16,0},{24,8},{0,16},{8,24},{17,1},{25,9},{1,17},{9,25},{18,2},{26... | collective-permute-start | bytes 12296 | tf_op jit(solution)/shard_map/ppermute | solution.py:1014
  601.8 1.1 collective-permute-start.31
  602.9 11.5 %collective-permute-start.32 = (f32[1,256]{1,0:T(1,128)S(1)}, f32[1,256]{1,0:T(1,128)S(1)}, u32[]{:S(2)}, u32[]{:S(2)}) collective-permute-start(f32[1,256]{1,0:T(1,128)S(1)} %add.211), channel_id=1, source_target_pairs={{0,2},{2,0},{1,3},{3,1},{4,6},{6,4},{5,7},{7,5},{8,10},{10,8},{9,1... | collective-permute-start | bytes 3080 | tf_op jit(solution)/shard_map/ppermute | solution.py:700
  (94 other events, 694.2 us)
Sparse Core Ops, SparseCore 0:
  13.2 61.8 all-gather.4
  76.7 57.8 all-gather.6
  136.2 57.8 all-gather.8
  196.1 105.3 all-gather.10
  310.5 100.4 reduce-scatter.5
  413.1 44.3 reduce-scatter.9
  459.9 55.4 reduce-scatter.7
  517.9 39.2 reduce-scatter.13
  570.0 50.8 reduce-scatter.11

commit v4 on v3

--- a/solution.py
+++ b/solution.py
@@ -854,11 +854,16 @@
         hidden_ff, gate_grad = up_product(all_ff, hidden_grad, gate, up_parts)
         down_last = weight_part(all_branch, hidden_ff, half, last, "grad_down")
         gate_grad, up_grad, down_last = fence((gate_grad, up_grad, down_last))
+        first = units // HD * 4 // 11 * HD if last else 0
+        gate_first_sums = None
+        if first:
+            gate_first = weight_slots(all_ff, gate_grad, half, "grad_gate_first", slice(0, first))
+            gate_grad, up_grad, gate_first = fence((gate_grad, up_grad, gate_first))
+            gate_first_sums = scatter(gate_first)
         back_plan = ([gate_grad, up_grad], [all_of(weight_gate), up_plan])
         ff_far = back_rows(*back_plan, 1, "normed_ff_grad_far")
         ff_far, gate_grad, up_grad = fence((ff_far, gate_grad, up_grad))
         ff_far = swap(ff_far, "core")
-        first = units // HD * 4 // 11 * HD if last else 0
         gate_columns = slice(first, units)
         gate_last = weight_part(all_ff, gate_grad, half, last, "grad_gate", gate_columns)
         gate_grad, up_grad, gate_last = fence((gate_grad, up_grad, gate_last))
@@ -866,11 +871,6 @@
         ff_grad = back_rows(*back_plan, 0, "normed_ff_grad_near", ff_far, in_hbm)
         ff_grad, gate_grad, up_grad, hidden_ff = fence((ff_grad, gate_grad, up_grad, hidden_ff))
         ff_got = swap(ff_grad, "row")
-        gate_first_sums = None
-        if first:
-            gate_first = weight_slots(all_ff, gate_grad, half, "grad_gate_first", slice(0, first))
-            gate_grad, hidden_ff, gate_first = fence((gate_grad, hidden_ff, gate_first))
-            gate_first_sums = scatter(gate_first)
 
         def to_last(values):
             return from_inner(values, inner - last) if last else None

time: 640 us -> 649 us (1.014)
  local copies, waits for them, and re-layouts: 73.8 us -> 83 us
    ppermute x19, waiting for transfers between devices: 57.6 us -> 78.2 us  [swap(): return lax.ppermute(values, axis, [(0, 1), (1, 0)])]
    ppermute x12, waiting for transfers between devices: 132 us -> 112 us  [from_inner(): lax.ppermute(values, 'inner', [((i + k) % inner, i) for i in range(inner)])]
    unnamed x202 -> x210, local copies, waits for them, and re-layouts: 54.7 us -> 63.9 us
  transfers between devices with their start and end apart: 42 -> 42, of which waited for: 23 -> 25; matrix products, arithmetic and copies ran while one was open for 9% -> 9% of each run, Pallas kernels for 34% -> 34%
where the time goes in v4:
time: 649 us; the launch traced here: 640 us
  waiting for transfers between devices  261 us (40%)
  Pallas kernels  216 us (33%)
  local copies, waits for them, and re-layouts  83 us (13%)
  other arithmetic  38.4 us (6%)
  starting transfers between devices  26.4 us (4%)
  between operations  15.3 us (2%)
    ppermute x12, waiting for transfers between devices, from_inner(): lax.ppermute(values, 'inner', [((i + k) % inner, i) for i in range(inner)])  112 us
    ppermute x19, waiting for transfers between devices, swap(): return lax.ppermute(values, axis, [(0, 1), (1, 0)])  78.2 us
    all_gather x4, waiting for transfers between devices, gather(): return lax.all_gather(values, 'outer', axis=0, tiled=True)  66.7 us
    unnamed x210, local copies, waits for them, and re-layouts  63.9 us
    pallas_call x8, Pallas kernels, back_rows(): pl.pallas_call(kernel, grid=(width // tile,), in_specs=specs, out_specs=s...  57.8 us
    pallas_call x8, Pallas kernels, weight_part(): pl.pallas_call(kernel, grid=(tiles,), in_specs=[row_spec, row_spec] + [wh...  42.1 us
    pallas_call x3, Pallas kernels, through(): pl.pallas_call(kernel, grid=(2,), in_specs=of_group(near, far, 2) + resid...  24.1 us
    pallas_call x6, Pallas kernels, row_call(): pl.pallas_call(kernel, grid=(rows // tile,), in_specs=[pl.BlockSpec(memor...  18.6 us
  transfers between devices with their start and end apart: 42, of which 25 were waited for; matrix products, arithmetic and copies ran while one was open for 9% of the time, Pallas kernels for 34%

profile of v4, /device:TPU:0, one launch (start us, length us, event | category | flops | bytes accessed | tf_op | source)
XLA Modules:
  0.0 640.3 jit_solution(4666226447069814685)
XLA Ops:
  19.8 14.3 %collective-permute-done.3 = bf16[256,1408]{1,0:T(8,128)(2,1)} collective-permute-done((bf16[256,1408]{1,0:T(8,128)(2,1)}, bf16[256,1408]{1,0:T(8,128)(2,1)}, u32[]{:S(2)}, u32[]{:S(2)}) %collective-permute-start.3) | collective-permute-done | bytes 720928 | tf_op jit(solution)/shard_map/ppermute | solution.py:697
  36.7 8.7 %collective-permute-done.2 = f32[320]{0:T(512)S(1)} collective-permute-done((f32[320]{0:T(512)S(1)}, f32[320]{0:T(512)S(1)}, u32[]{:S(2)}, u32[]{:S(2)}) %collective-permute-start.2) | collective-permute-done | bytes 1312 | tf_op jit(solution)/shard_map/ppermute | solution.py:700
  51.9 23.2 %all-gather.5.cloned.1.call-done.refs_0_.refs_2_.refs_1_ = bf16[1024,1408]{1,0:T(8,128)(2,1)} async-done(((bf16[256,1408]{1,0:T(8,128)(2,1)}), bf16[1024,1408]{1,0:T(8,128)(2,1)}) %all-gather.5.cloned.1.call-update) | async-done | bytes 2883600 | tf_op jit(solution)/shard_map/all_gather | solution.py:706
  86.0 5.2 collective-permute-done.6.refs_1_.far_rows
  91.1 43.5 %all-gather.7.cloned.1.call-done.refs_2_.refs_1_ = bf16[1024,1408]{1,0:T(8,128)(2,1)} async-done(((bf16[256,1408]{1,0:T(8,128)(2,1)}), bf16[1024,1408]{1,0:T(8,128)(2,1)}) %all-gather.7.cloned.1.call-update) | async-done | bytes 2883600 | tf_op jit(solution)/shard_map/all_gather | solution.py:706
  134.6 5.0 collective-permute-done.5.refs_1_.refs_3_.refs_2_
  147.2 4.1 norm_far.1.refs_1_.far_rows
  151.3 7.2 %joint.1.operands_1_ = f32[1280,768]{1,0:T(8,128)S(1)} custom-call(bf16[640,2048]{1,0:T(8,128)(2,1)S(1)} %norm_near.1.refs_0_.near_rows, bf16[640,2048]{1,0:T(8,128)(2,1)S(1)} %norm_far.1.refs_1_.far_rows, bf16[1024,1408]{1,0:T(8,128)(2,1)S(1)} %copy-done, bf16[1024,1408]{1,0:T(8,128)(2,1)} %collective-permute-done.5.refs_1_.refs_3_.refs_2_), custom_call_target="tpu_custom_call" | custom-call | flops 1006632960 | bytes 2097152 | tf_op jit(solution)/shard_map/joint/pallas_call | solution.py:421
  164.5 10.0 %attend.1 = (bf16[640,512]{1,0:T(8,128)(2,1)S(1)}, bf16[640,512]{1,0:T(8,128)(2,1)S(1)}, bf16[1280,768]{1,0:T(8,128)(2,1)S(1)}) custom-call(s32[14]{0:T(128)S(1)} %concatenate.37.operands_0_, f32[1280,768]{1,0:T(8,128)S(1)} %joint.1.operands_1_, f32[1280,128]{1,0:T(8,128)S(1)} %get-tuple-element.200.operands_2_.operands_3_, ...), custom_call_target="tpu_custom_call" | custom-call | flops 1476395008 | bytes 1966080 | tf_op jit(solution)/shard_map/attend/pallas_call | solution.py:799
  176.5 5.9 attended_far.1
  186.4 4.9 attended_near.1
  191.3 4.4 add_convert_fusion.3.mine
  195.7 8.3 %collective-permute-done.10.refs_5_.refs_4_ = bf16[256,1408]{1,0:T(8,128)(2,1)} collective-permute-done((bf16[256,1408]{1,0:T(8,128)(2,1)}, bf16[256,1408]{1,0:T(8,128)(2,1)}, u32[]{:S(2)}, u32[]{:S(2)}) %collective-permute-start.10) | collective-permute-done | bytes 720928 | tf_op jit(solution)/shard_map/ppermute | solution.py:697
  207.5 17.3 %collective-permute-done.12.refs_6_.refs_5_ = bf16[256,1408]{1,0:T(8,128)(2,1)S(1)} collective-permute-done((bf16[256,1408]{1,0:T(8,128)(2,1)}, bf16[256,1408]{1,0:T(8,128)(2,1)S(1)}, u32[]{:S(2)}, u32[]{:S(2)}) %collective-permute-start.12) | collective-permute-done | bytes 720928 | tf_op jit(solution)/shard_map/ppermute | solution.py:697
  227.8 11.7 %hidden_grad.1.refs_2_ = bf16[1280,1408]{1,0:T(8,128)(2,1)S(1)} custom-call(bf16[640,2048]{1,0:T(8,128)(2,1)} %kept.1.refs_0_.near_rows, bf16[640,2048]{1,0:T(8,128)(2,1)} %collective-permute-done.6.refs_1_.far_rows, bf16[1024,1408]{1,0:T(8,128)(2,1)S(1)} %copy-done.18, bf16[256,1408]{1,0:T(8,128)(2,1)} %collective-permute-done.7.refs_3_.refs_2_, ...), custom_call_target="tpu_custom_call" | custom-call | flops 1845493760 | bytes 2752512 | tf_op jit(solution)/shard_map/hidden_grad/pallas_call | solution.py:421
  239.5 23.2 %collective-permute-done.11.got = bf16[640,2048]{1,0:T(8,128)(2,1)S(1)} collective-permute-done((bf16[640,2048]{1,0:T(8,128)(2,1)}, bf16[640,2048]{1,0:T(8,128)(2,1)S(1)}, u32[]{:S(2)}, u32[]{:S(2)}) %collective-permute-start.11) | collective-permute-done | bytes 2621472 | tf_op jit(solution)/shard_map/ppermute | solution.py:700
  267.9 17.1 %collective-permute-done.14.refs_4_.refs_2_ = bf16[1024,1408]{1,0:T(8,128)(2,1)S(1)} collective-permute-done((bf16[1024,1408]{1,0:T(8,128)(2,1)}, bf16[1024,1408]{1,0:T(8,128)(2,1)S(1)}, u32[]{:S(2)}, u32[]{:S(2)}) %collective-permute-start.14) | collective-permute-done | bytes 2883616 | tf_op jit(solution)/shard_map/ppermute | solution.py:697
  285.0 11.4 %gate.1 = (f32[1280,1408]{1,0:T(8,128)}, bf16[1280,1408]{1,0:T(8,128)(2,1)S(1)}) custom-call(bf16[640,2048]{1,0:T(8,128)(2,1)S(1)} %get-tuple-element.123.refs_0_.near_rows, bf16[640,2048]{1,0:T(8,128)(2,1)S(1)} %collective-permute-done.13.refs_1_.far_rows, bf16[1280,1408]{1,0:T(8,128)(2,1)S(1)} %hidden_grad.1.refs_2_, bf16[1024,1408]{1,0:T(8,128)(2,1)S(1)} %copy-done.31, ...), custom_call_target="tpu_custom_call" | custom-call | flops 1845493760 | bytes 2752512 | tf_op jit(solution)/shard_map/gate/pallas_call | solution.py:452
  296.4 12.3 %grad_up_late.1 = bf16[1024,2816]{1,0:T(8,128)(2,1)} custom-call(bf16[640,2048]{1,0:T(8,128)(2,1)S(1)} %get-tuple-element.123.refs_0_.near_rows, bf16[640,2048]{1,0:T(8,128)(2,1)S(1)} %collective-permute-done.13.refs_1_.far_rows, bf16[1280,1408]{1,0:T(8,128)(2,1)S(1)} %get-tuple-element.140.refs_0_.refs_3_), custom_call_target="tpu_custom_call" | custom-call | flops 1845493760 | bytes 1556480 | tf_op jit(solution)/shard_map/grad_up_late/pallas_call | solution.py:648
  319.4 12.4 %up.1 = (bf16[1280,1408]{1,0:T(8,128)(2,1)S(1)}, bf16[1280,1408]{1,0:T(8,128)(2,1)S(1)}) custom-call(bf16[640,2048]{1,0:T(8,128)(2,1)S(1)} %copy-done.5, bf16[640,2048]{1,0:T(8,128)(2,1)S(1)} %copy-done.9, bf16[1280,1408]{1,0:T(8,128)(2,1)S(1)} %copy-done.30, f32[1280,1408]{1,0:T(8,128)} %get-tuple-element.128.refs_3_, bf16[1024,2816]{1,0:T(8,128)(2,1)S(1)} %copy-done.1), custom_call_target="tpu_custom_call" | custom-call | flops 1845493760 | bytes 2752512 | tf_op jit(solution)/shard_map/up/pallas_call | solution.py:503
  331.8 8.9 %grad_down.2 = bf16[1024,1408]{1,0:T(8,128)(2,1)} custom-call(bf16[640,2048]{1,0:T(8,128)(2,1)} %kept.1.refs_0_.near_rows, bf16[640,2048]{1,0:T(8,128)(2,1)} %collective-permute-done.6.refs_1_.far_rows, bf16[1280,1408]{1,0:T(8,128)(2,1)S(1)} %get-tuple-element.143.refs_0_), custom_call_target="tpu_custom_call" | custom-call | flops 922746880 | bytes 1556480 | tf_op jit(solution)/shard_map/grad_down/pallas_call | solution.py:612
  340.8 5.4 grad_gate_first.1
  356.5 9.9 %normed_ff_grad_far.1 = bf16[640,2048]{1,0:T(8,128)(2,1)} custom-call(bf16[1280,1408]{1,0:T(8,128)(2,1)S(1)} %copy-done.13, bf16[1024,1408]{1,0:T(8,128)(2,1)S(1)} %copy-done.32, bf16[1024,1408]{1,0:T(8,128)(2,1)S(1)} %copy-done.35, bf16[1280,1408]{1,0:T(8,128)(2,1)S(1)} %copy-done.27, bf16[1024,2816]{1,0:T(8,128)(2,1)S(1)} %copy-done.2, ...), custom_call_target="tpu_custom_call" | custom-call | flops 1845493760 | bytes 6127616 | tf_op jit(solution)/shard_map/normed_ff_grad_far/pallas_call | solution.py:570
  373.5 5.3 grad_gate.2
  383.3 11.1 %normed_ff_grad_near.1.mine = bf16[640,2048]{1,0:T(8,128)(2,1)} custom-call(bf16[1280,1408]{1,0:T(8,128)(2,1)S(1)} %copy-done.15, bf16[1024,1408]{1,0:T(8,128)(2,1)S(1)} %copy-done.33, bf16[1024,1408]{1,0:T(8,128)(2,1)S(1)} %copy-done.36, bf16[1280,1408]{1,0:T(8,128)(2,1)S(1)} %copy-done.28, bf16[1024,2816]{1,0:T(8,128)(2,1)S(1)} %copy-done.3, ...), custom_call_target="tpu_custom_call" | custom-call | flops 1845493760 | bytes 6782976 | tf_op jit(solution)/shard_map/normed_ff_grad_near/pallas_call | solution.py:570
  394.9 4.9 grad_gate.3
  399.8 8.1 %grad_down.3 = bf16[1024,1408]{1,0:T(8,128)(2,1)} custom-call(bf16[640,2048]{1,0:T(8,128)(2,1)} %kept.1.refs_0_.near_rows, bf16[640,2048]{1,0:T(8,128)(2,1)} %collective-permute-done.6.refs_1_.far_rows, bf16[1280,1408]{1,0:T(8,128)(2,1)S(1)} %copy-done.17), custom_call_target="tpu_custom_call" | custom-call | flops 922746880 | bytes 1556480 | tf_op jit(solution)/shard_map/grad_down/pallas_call | solution.py:612
  407.9 7.5 %branch_near.1 = bf16[640,2048]{1,0:T(8,128)(2,1)S(1)} custom-call(bf16[1280,1408]{1,0:T(8,128)(2,1)S(1)} %copy-done.17, bf16[1024,1408]{1,0:T(8,128)(2,1)S(1)} %copy-done.19, bf16[256,1408]{1,0:T(8,128)(2,1)} %collective-permute-done.7.refs_3_.refs_2_, bf16[256,1408]{1,0:T(8,128)(2,1)S(1)} %copy-done.62, ...), custom_call_target="tpu_custom_call" | custom-call | flops 922746880 | bytes 2342912 | tf_op jit(solution)/shard_map/branch_near/pallas_call | solution.py:570
  416.9 7.6 %branch_far.1 = bf16[640,2048]{1,0:T(8,128)(2,1)S(1)} custom-call(bf16[1280,1408]{1,0:T(8,128)(2,1)S(1)} %copy-done.17, bf16[1024,1408]{1,0:T(8,128)(2,1)S(1)} %copy-done.19, bf16[256,1408]{1,0:T(8,128)(2,1)} %collective-permute-done.7.refs_3_.refs_2_, bf16[256,1408]{1,0:T(8,128)(2,1)S(1)} %copy-done.62, ...), custom_call_target="tpu_custom_call" | custom-call | flops 922746880 | bytes 2342912 | tf_op jit(solution)/shard_map/branch_far/pallas_call | solution.py:570
  426.0 5.6 collective-permute-done.17
  434.0 19.7 %collective-permute-done.16.got = bf16[640,2048]{1,0:T(8,128)(2,1)} collective-permute-done((bf16[640,2048]{1,0:T(8,128)(2,1)}, bf16[640,2048]{1,0:T(8,128)(2,1)}, u32[]{:S(2)}, u32[]{:S(2)}) %collective-permute-start.16) | collective-permute-done | bytes 2621472 | tf_op jit(solution)/shard_map/ppermute | solution.py:700
  459.8 4.9 middle_back.1
  467.6 4.2 collective-permute-done.18.far_rows.refs_1_
  475.0 5.2 mixed_grad.1.operands_2_
  480.3 16.1 %attend_back.1 = (bf16[640,768]{1,0:T(8,128)(2,1)S(1)}, bf16[640,768]{1,0:T(8,128)(2,1)S(1)}) custom-call(s32[14]{0:T(128)S(1)} %concatenate.37.operands_0_, bf16[1280,768]{1,0:T(8,128)(2,1)S(1)} %copy-done.88, bf16[1280,512]{1,0:T(8,128)(2,1)S(1)} %mixed_grad.1.operands_2_, f32[1280,128]{1,0:T(8,128)S(1)} %copy-done.80, f32[1280,128]{1,0:T(8,128)S(1)} %copy-done.82), custom_call_target="tpu_custom_call" | custom-call | flops 2214592512 | bytes 1966080 | tf_op jit(solution)/shard_map/attend_back/pallas_call | solution.py:928
  496.4 5.8 normed_grad_near.1
  502.3 4.1 grad_joint.2
  506.4 5.1 normed_grad_far.1
  513.4 3.8 add_convert_fusion.4
  518.2 3.7 add_convert_fusion.2.mine
  525.2 5.0 add_convert_fusion.1.mine
  530.2 3.4 grad_output.2
  533.7 4.1 grad_joint.3
  537.8 38.8 %collective-permute-done.19 = bf16[1024,512]{1,0:T(8,128)(2,1)S(1)} collective-permute-done((bf16[1024,512]{1,0:T(8,128)(2,1)S(1)}, bf16[1024,512]{1,0:T(8,128)(2,1)S(1)}, u32[]{:S(2)}, u32[]{:S(2)}) %collective-permute-start.19) | collective-permute-done | bytes 1048608 | tf_op jit(solution)/shard_map/ppermute | solution.py:697
  598.6 3.2 input_grad.1
  604.0 3.4 collective-permute-done.30
  613.2 9.8 %collective-permute-done.32 = f32[1,256]{1,0:T(1,128)S(1)} collective-permute-done((f32[1,256]{1,0:T(1,128)S(1)}, f32[1,256]{1,0:T(1,128)S(1)}, u32[]{:S(2)}, u32[]{:S(2)}) %collective-permute-start.32) | collective-permute-done | bytes 1056 | tf_op jit(solution)/shard_map/ppermute | solution.py:700
  625.6 4.0 reduce-scatter.12.cloned.1.call-done
  (339 shorter events, 156.3 us)
Async XLA Ops:
  7.2 68.0 %all-gather.5.cloned.1.call-start = ((), (), s32[]{:S(2)}) async-start(), calls=%async_computation.5 | async-start | bytes 3604480 | tf_op jit(solution)/shard_map/all_gather | solution.py:706
  13.1 121.5 %all-gather.7.cloned.1.call-start = ((), (), s32[]{:S(2)}) async-start(), calls=%async_computation.6 | async-start | bytes 3604480 | tf_op jit(solution)/shard_map/all_gather | solution.py:706
  13.2 32.2 %collective-permute-start.1 = (bf16[320,2048]{1,0:T(8,128)(2,1)}, bf16[320,2048]{1,0:T(8,128)(2,1)}, u32[]{:S(2)}, u32[]{:S(2)}) collective-permute-start(bf16[320,2048]{1,0:T(8,128)(2,1)} %rows.1), channel_id=1, source_target_pairs={{0,2},{2,0},{1,3},{3,1},{4,6},{6,4},{5,7},{7,5},{8,10},{10,8},{9,1... | collective-permute-start | bytes 3932168 | tf_op jit(solution)/shard_map/ppermute | solution.py:700
  16.2 17.9 %collective-permute-start.3 = (bf16[256,1408]{1,0:T(8,128)(2,1)}, bf16[256,1408]{1,0:T(8,128)(2,1)}, u32[]{:S(2)}, u32[]{:S(2)}) collective-permute-start(bf16[256,1408]{1,0:T(8,128)(2,1)} %param.23), channel_id=1, source_target_pairs={{4,0},{0,4},{5,1},{1,5},{6,2},{2,6},{7,3},{3,7},{12,8},{8,12},{13,... | collective-permute-start | bytes 2162696 | tf_op jit(solution)/shard_map/ppermute | solution.py:697
  17.7 178.0 %all-gather.9.cloned.1.call-start = ((), (), s32[]{:S(2)}) async-start(), calls=%async_computation.7 | async-start | bytes 3604480 | tf_op jit(solution)/shard_map/all_gather | solution.py:706
  17.8 27.5 %collective-permute-start.2 = (f32[320]{0:T(512)S(1)}, f32[320]{0:T(512)S(1)}, u32[]{:S(2)}, u32[]{:S(2)}) collective-permute-start(f32[320]{0:T(512)S(1)} %subtract_convert_fusion), channel_id=1, source_target_pairs={{0,2},{2,0},{1,3},{3,1},{4,6},{6,4},{5,7},{7,5},{8,10},{10,8},{9,1... | collective-permute-start | bytes 3848 | tf_op jit(solution)/shard_map/ppermute | solution.py:700
  46.8 5.1 collective-permute-start.4
  46.9 31.5 %collective-permute-start = (bf16[320,2048]{1,0:T(8,128)(2,1)}, bf16[320,2048]{1,0:T(8,128)(2,1)}, u32[]{:S(2)}, u32[]{:S(2)}) collective-permute-start(bf16[320,2048]{1,0:T(8,128)(2,1)} %param.25), channel_id=1, source_target_pairs={{0,2},{2,0},{1,3},{3,1},{4,6},{6,4},{5,7},{7,5},{8,10},{10,8},{9,1... | collective-permute-start | bytes 3932168 | tf_op jit(solution)/shard_map/ppermute | solution.py:700
  75.2 64.5 %collective-permute-start.5 = (bf16[1024,1408]{1,0:T(8,128)(2,1)}, bf16[1024,1408]{1,0:T(8,128)(2,1)}, u32[]{:S(2)}, u32[]{:S(2)}) collective-permute-start(bf16[1024,1408]{1,0:T(8,128)(2,1)} %all-gather.5.cloned.1.call-done.refs_0_.refs_2_.refs_1_), channel_id=1, source_target_pairs={{4,0},{0,4},{5,1},{1,5},{6,2},{2,6},{7,3},{3,7},{12,8},{8,12},{13,... | collective-permute-start | bytes 8650760 | tf_op jit(solution)/shard_map/ppermute | solution.py:697
  82.9 60.3 %copy-start.101 = (s32[1,10]{1,0:T(1,128)S(1)}, s32[1,10]{1,0:T(1,128)}, u32[]{:S(2)}) copy-start(s32[1,10]{1,0:T(1,128)} %param.15) | copy-start | bytes 124
  82.9 60.4 %copy-start = (bf16[1024,1408]{1,0:T(8,128)(2,1)S(1)}, bf16[1024,1408]{1,0:T(8,128)(2,1)}, u32[]{:S(2)}) copy-start(bf16[1024,1408]{1,0:T(8,128)(2,1)} %all-gather.5.cloned.1.call-done.refs_0_.refs_2_.refs_1_) | copy-start | bytes 8650756
  85.9 5.3 collective-permute-start.6
  85.9 224.8 %all-gather.11.cloned.1.call-start = ((), (), s32[]{:S(2)}) async-start(), calls=%async_computation.8 | async-start | bytes 7208960 | tf_op jit(solution)/shard_map/all_gather | solution.py:706
  141.7 17.3 %collective-permute-start.7 = (bf16[256,1408]{1,0:T(8,128)(2,1)}, bf16[256,1408]{1,0:T(8,128)(2,1)}, u32[]{:S(2)}, u32[]{:S(2)}) collective-permute-start(bf16[256,1408]{1,0:T(8,128)(2,1)} %slice.58), channel_id=1, source_target_pairs={{4,0},{0,4},{5,1},{1,5},{6,2},{2,6},{7,3},{3,7},{12,8},{8,12},{13,... | collective-permute-start | bytes 2162696 | tf_op jit(solution)/shard_map/ppermute | solution.py:697
  160.1 16.4 %collective-permute-start.8 = (bf16[256,1408]{1,0:T(8,128)(2,1)S(1)}, bf16[256,1408]{1,0:T(8,128)(2,1)S(1)}, u32[]{:S(2)}, u32[]{:S(2)}) collective-permute-start(bf16[256,1408]{1,0:T(8,128)(2,1)S(1)} %slice.59), channel_id=1, source_target_pairs={{4,0},{0,4},{5,1},{1,5},{6,2},{2,6},{7,3},{3,7},{12,8},{8,12},{13,... | collective-permute-start | bytes 2162696 | tf_op jit(solution)/shard_map/ppermute | solution.py:697
  182.4 8.9 %collective-permute-start.9 = (bf16[640,2048]{1,0:T(8,128)(2,1)}, bf16[640,2048]{1,0:T(8,128)(2,1)}, u32[]{:S(2)}, u32[]{:S(2)}) collective-permute-start(bf16[640,2048]{1,0:T(8,128)(2,1)} %attended_far.1), channel_id=1, source_target_pairs={{0,1},{1,0},{2,3},{3,2},{4,5},{5,4},{6,7},{7,6},{8,9},{9,8},{10,11... | collective-permute-start | bytes 7864328 | tf_op jit(solution)/shard_map/ppermute | solution.py:700
  182.5 330.4 %reduce-scatter.6.cloned.1.call-start = ((), (), s32[]{:S(2)}) async-start(), calls=%async_computation.9 | async-start | bytes 7208960 | tf_op jit(solution)/shard_map/reduce_scatter | solution.py:709
  185.2 18.9 %collective-permute-start.10 = (bf16[256,1408]{1,0:T(8,128)(2,1)}, bf16[256,1408]{1,0:T(8,128)(2,1)}, u32[]{:S(2)}, u32[]{:S(2)}) collective-permute-start(bf16[256,1408]{1,0:T(8,128)(2,1)} %get-tuple-element.188), channel_id=1, source_target_pairs={{4,0},{0,4},{5,1},{1,5},{6,2},{2,6},{7,3},{3,7},{12,8},{8,12},{13,... | collective-permute-start | bytes 2162696 | tf_op jit(solution)/shard_map/ppermute | solution.py:697
  204.0 58.7 %collective-permute-start.11 = (bf16[640,2048]{1,0:T(8,128)(2,1)}, bf16[640,2048]{1,0:T(8,128)(2,1)S(1)}, u32[]{:S(2)}, u32[]{:S(2)}) collective-permute-start(bf16[640,2048]{1,0:T(8,128)(2,1)} %add_convert_fusion.3.mine), channel_id=1, source_target_pairs={{0,2},{2,0},{1,3},{3,1},{4,6},{6,4},{5,7},{7,5},{8,10},{10,8},{9,1... | collective-permute-start | bytes 7864328 | tf_op jit(solution)/shard_map/ppermute | solution.py:700
  205.5 19.3 %collective-permute-start.12 = (bf16[256,1408]{1,0:T(8,128)(2,1)}, bf16[256,1408]{1,0:T(8,128)(2,1)S(1)}, u32[]{:S(2)}, u32[]{:S(2)}) collective-permute-start(bf16[256,1408]{1,0:T(8,128)(2,1)} %get-tuple-element.187), channel_id=1, source_target_pairs={{4,0},{0,4},{5,1},{1,5},{6,2},{2,6},{7,3},{3,7},{12,8},{8,12},{13,... | collective-permute-start | bytes 2162696 | tf_op jit(solution)/shard_map/ppermute | solution.py:697
  206.7 78.3 %collective-permute-start.14 = (bf16[1024,1408]{1,0:T(8,128)(2,1)}, bf16[1024,1408]{1,0:T(8,128)(2,1)S(1)}, u32[]{:S(2)}, u32[]{:S(2)}) collective-permute-start(bf16[1024,1408]{1,0:T(8,128)(2,1)} %all-gather.9.cloned.1.call-done.refs_3_.refs_1_), channel_id=1, source_target_pairs={{4,0},{0,4},{5,1},{1,5},{6,2},{2,6},{7,3},{3,7},{12,8},{8,12},{13,... | collective-permute-start | bytes 8650760 | tf_op jit(solution)/shard_map/ppermute | solution.py:697
  227.8 35.0 %copy-start.52 = (bf16[640,2048]{1,0:T(8,128)(2,1)S(1)}, bf16[640,2048]{1,0:T(8,128)(2,1)}, u32[]{:S(2)}) copy-start(bf16[640,2048]{1,0:T(8,128)(2,1)} %add_convert_fusion.3.mine) | copy-start | bytes 7864324
  239.5 45.5 %copy-start.29 = (bf16[1280,1408]{1,0:T(8,128)(2,1)}, bf16[1280,1408]{1,0:T(8,128)(2,1)S(1)}, u32[]{:S(2)}) copy-start(bf16[1280,1408]{1,0:T(8,128)(2,1)S(1)} %hidden_grad.1.refs_2_) | copy-start | bytes 10813444
  267.9 17.1 %collective-permute-start.13 = (bf16[640,2048]{1,0:T(8,128)(2,1)S(1)}, bf16[640,2048]{1,0:T(8,128)(2,1)S(1)}, u32[]{:S(2)}, u32[]{:S(2)}) collective-permute-start(bf16[640,2048]{1,0:T(8,128)(2,1)S(1)} %get-tuple-element.123.refs_0_.near_rows), channel_id=1, source_target_pairs={{0,1},{1,0},{2,3},{3,2},{4,5},{5,4},{6,7},{7,6},{8,9},{9,8},{10,11... | collective-permute-start | bytes 7864328 | tf_op jit(solution)/shard_map/ppermute | solution.py:700
  310.6 268.7 %reduce-scatter.10.cloned.1.call-start = ((), (), s32[]{:S(2)}) async-start(), calls=%async_computation.11 | async-start | bytes 2621440 | tf_op jit(solution)/shard_map/reduce_scatter | solution.py:709
  366.4 12.4 %collective-permute-start.15 = (bf16[640,2048]{1,0:T(8,128)(2,1)}, bf16[640,2048]{1,0:T(8,128)(2,1)}, u32[]{:S(2)}, u32[]{:S(2)}) collective-permute-start(bf16[640,2048]{1,0:T(8,128)(2,1)} %normed_ff_grad_far.1), channel_id=1, source_target_pairs={{0,1},{1,0},{2,3},{3,2},{4,5},{5,4},{6,7},{7,6},{8,9},{9,8},{10,11... | collective-permute-start | bytes 7864328 | tf_op jit(solution)/shard_map/ppermute | solution.py:700
  366.4 213.0 %reduce-scatter.8.cloned.1.call-start = ((), (), s32[]{:S(2)}) async-start(), calls=%async_computation.10 | async-start | bytes 3604480 | tf_op jit(solution)/shard_map/reduce_scatter | solution.py:709
  366.5 65.2 %collective-permute-start.17 = (bf16[1024,1408]{1,0:T(8,128)(2,1)}, bf16[1024,1408]{1,0:T(8,128)(2,1)S(1)}, u32[]{:S(2)}, u32[]{:S(2)}) collective-permute-start(bf16[1024,1408]{1,0:T(8,128)(2,1)} %grad_down.2), channel_id=1, source_target_pairs={{4,0},{0,4},{5,1},{1,5},{6,2},{2,6},{7,3},{3,7},{12,8},{8,12},{13,... | collective-permute-start | bytes 8650760 | tf_op jit(solution)/shard_map/ppermute | solution.py:697
  394.4 59.3 %collective-permute-start.16 = (bf16[640,2048]{1,0:T(8,128)(2,1)}, bf16[640,2048]{1,0:T(8,128)(2,1)}, u32[]{:S(2)}, u32[]{:S(2)}) collective-permute-start(bf16[640,2048]{1,0:T(8,128)(2,1)} %normed_ff_grad_near.1.mine), channel_id=1, source_target_pairs={{0,2},{2,0},{1,3},{3,1},{4,6},{6,4},{5,7},{7,5},{8,10},{10,8},{9,1... | collective-permute-start | bytes 7864328 | tf_op jit(solution)/shard_map/ppermute | solution.py:700
  434.0 155.9 %reduce-scatter.14.cloned.1.call-start = ((), (), s32[]{:S(2)}) async-start(), calls=%async_computation.13 | async-start | bytes 2293760 | tf_op jit(solution)/shard_map/reduce_scatter | solution.py:709
  466.9 4.9 collective-permute-start.18
  466.9 46.0 %collective-permute-start.20 = (bf16[1024,896]{1,0:T(8,128)(2,1)S(1)}, bf16[1024,896]{1,0:T(8,128)(2,1)}, u32[]{:S(2)}, u32[]{:S(2)}) collective-permute-start(bf16[1024,896]{1,0:T(8,128)(2,1)S(1)} %copy-done.96), channel_id=1, source_target_pairs={{4,0},{0,4},{5,1},{1,5},{6,2},{2,6},{7,3},{3,7},{12,8},{8,12},{13,... | collective-permute-start | bytes 5505032 | tf_op jit(solution)/shard_map/ppermute | solution.py:697
  512.9 5.3 collective-permute-start.22
  513.1 12.1 %collective-permute-start.24 = (bf16[640,2048]{1,0:T(8,128)(2,1)}, bf16[640,2048]{1,0:T(8,128)(2,1)}, u32[]{:S(2)}, u32[]{:S(2)}) collective-permute-start(bf16[640,2048]{1,0:T(8,128)(2,1)} %copy-done.75), channel_id=1, source_target_pairs={{0,1},{1,0},{2,3},{3,2},{4,5},{5,4},{6,7},{7,6},{8,9},{9,8},{10,11... | collective-permute-start | bytes 7864328 | tf_op jit(solution)/shard_map/ppermute | solution.py:700
  517.2 112.4 %reduce-scatter.12.cloned.1.call-start = ((), (), s32[]{:S(2)}) async-start(), calls=%async_computation.12 | async-start | bytes 3276800 | tf_op jit(solution)/shard_map/reduce_scatter | solution.py:709
  517.3 59.3 %collective-permute-start.21 = (bf16[1024,768]{1,0:T(8,128)(2,1)}, bf16[1024,768]{1,0:T(8,128)(2,1)S(1)}, u32[]{:S(2)}, u32[]{:S(2)}) collective-permute-start(bf16[1024,768]{1,0:T(8,128)(2,1)} %grad_joint.2), channel_id=1, source_target_pairs={{4,0},{0,4},{5,1},{1,5},{6,2},{2,6},{7,3},{3,7},{12,8},{8,12},{13,... | collective-permute-start | bytes 4718600 | tf_op jit(solution)/shard_map/ppermute | solution.py:697
  523.6 53.0 %collective-permute-start.23 = (bf16[320,2048]{1,0:T(8,128)(2,1)S(1)}, bf16[320,2048]{1,0:T(8,128)(2,1)S(1)}, u32[]{:S(2)}, u32[]{:S(2)}) collective-permute-start(bf16[320,2048]{1,0:T(8,128)(2,1)S(1)} %slice.76), channel_id=1, source_target_pairs={{0,2},{2,0},{1,3},{3,1},{4,6},{6,4},{5,7},{7,5},{8,10},{10,8},{9,1... | collective-permute-start | bytes 3932168 | tf_op jit(solution)/shard_map/ppermute | solution.py:700
  524.2 52.3 %collective-permute-start.19 = (bf16[1024,512]{1,0:T(8,128)(2,1)S(1)}, bf16[1024,512]{1,0:T(8,128)(2,1)S(1)}, u32[]{:S(2)}, u32[]{:S(2)}) collective-permute-start(bf16[1024,512]{1,0:T(8,128)(2,1)S(1)} %copy-done.97), channel_id=1, source_target_pairs={{4,0},{0,4},{5,1},{1,5},{6,2},{2,6},{7,3},{3,7},{12,8},{8,12},{13,... | collective-permute-start | bytes 3145736 | tf_op jit(solution)/shard_map/ppermute | solution.py:697
  533.7 42.9 %copy-start.92 = (bf16[1024,512]{1,0:T(8,128)(2,1)S(1)}, bf16[1024,512]{1,0:T(8,128)(2,1)}, u32[]{:S(2)}) copy-start(bf16[1024,512]{1,0:T(8,128)(2,1)} %grad_output.2) | copy-start | bytes 3145732
  537.8 39.1 %copy-start.91 = (bf16[1024,768]{1,0:T(8,128)(2,1)S(1)}, bf16[1024,768]{1,0:T(8,128)(2,1)}, u32[]{:S(2)}) copy-start(bf16[1024,768]{1,0:T(8,128)(2,1)} %grad_joint.3) | copy-start | bytes 4718596
  583.9 23.4 %collective-permute-start.30 = (bf16[256,1920]{1,0:T(8,128)(2,1)}, bf16[256,1920]{1,0:T(8,128)(2,1)}, u32[]{:S(2)}, u32[]{:S(2)}) collective-permute-start(bf16[256,1920]{1,0:T(8,128)(2,1)} %pad_maximum_fusion.3), channel_id=1, source_target_pairs={{4,0},{0,4},{5,1},{1,5},{6,2},{2,6},{7,3},{3,7},{12,8},{8,12},{13,... | collective-permute-start | bytes 2949128 | tf_op jit(solution)/shard_map/ppermute | solution.py:697
  585.0 1.2 collective-permute-start.26
  586.3 3.6 collective-permute-start.27
  589.9 11.9 %collective-permute-start.28 = (f32[1,1024]{1,0:T(1,128)S(1)}, f32[1,1024]{1,0:T(1,128)S(1)}, u32[]{:S(2)}, u32[]{:S(2)}) collective-permute-start(f32[1,1024]{1,0:T(1,128)S(1)} %add.203), channel_id=1, source_target_pairs={{8,0},{0,8},{24,16},{16,24},{9,1},{1,9},{25,17},{17,25},{10,2},{2,... | collective-permute-start | bytes 12296 | tf_op jit(solution)/shard_map/ppermute | solution.py:1014
  592.8 30.8 %collective-permute-start.25 = (bf16[320,2048]{1,0:T(8,128)(2,1)S(1)}, bf16[320,2048]{1,0:T(8,128)(2,1)S(1)}, u32[]{:S(2)}, u32[]{:S(2)}) collective-permute-start(bf16[320,2048]{1,0:T(8,128)(2,1)S(1)} %slice.63), channel_id=1, source_target_pairs={{0,2},{2,0},{1,3},{3,1},{4,6},{6,4},{5,7},{7,5},{8,10},{10,8},{9,1... | collective-permute-start | bytes 3932168 | tf_op jit(solution)/shard_map/ppermute | solution.py:700
  601.8 9.5 %collective-permute-start.29 = (f32[1,1024]{1,0:T(1,128)S(1)}, f32[1,1024]{1,0:T(1,128)S(1)}, u32[]{:S(2)}, u32[]{:S(2)}) collective-permute-start(f32[1,1024]{1,0:T(1,128)S(1)} %add.204), channel_id=1, source_target_pairs={{16,0},{24,8},{0,16},{8,24},{17,1},{25,9},{1,17},{9,25},{18,2},{26... | collective-permute-start | bytes 12296 | tf_op jit(solution)/shard_map/ppermute | solution.py:1014
  611.4 1.1 collective-permute-start.31
  612.5 10.5 %collective-permute-start.32 = (f32[1,256]{1,0:T(1,128)S(1)}, f32[1,256]{1,0:T(1,128)S(1)}, u32[]{:S(2)}, u32[]{:S(2)}) collective-permute-start(f32[1,256]{1,0:T(1,128)S(1)} %add.211), channel_id=1, source_target_pairs={{0,2},{2,0},{1,3},{3,1},{4,6},{6,4},{5,7},{7,5},{8,10},{10,8},{9,1... | collective-permute-start | bytes 3080 | tf_op jit(solution)/shard_map/ppermute | solution.py:700
  (98 other events, 649.4 us)
Sparse Core Ops, SparseCore 0:
  13.2 61.8 all-gather.4
  76.7 57.8 all-gather.6
  136.2 57.8 all-gather.8
  196.1 105.3 all-gather.10
  310.8 100.4 reduce-scatter.5
  413.4 44.3 reduce-scatter.9
  460.2 55.4 reduce-scatter.7
  518.1 39.2 reduce-scatter.13
  579.5 50.0 reduce-scatter.11

commit v5 on v3

--- a/solution.py
+++ b/solution.py
@@ -929,10 +929,11 @@
         joint_last = weight_part(normed, packed_grad, half, last, "grad_joint")
         normed_plan = ([packed_grad], [packed_plan(joint_columns)])
         normed_far = back_rows(*normed_plan, 1, "normed_grad_far")
+        packed_grad, gate_got, up_late_sums, joint_last, normed_far = fence(
+            (packed_grad, gate_got, up_late_sums, joint_last, normed_far)
+        )
+        normed_plan = ([packed_grad], [packed_plan(joint_columns)])
         normed_near = back_rows(*normed_plan, 0, "normed_grad_near")
-        packed_grad, gate_got, up_late_sums, joint_last, normed_far, normed_near = fence(
-            (packed_grad, gate_got, up_late_sums, joint_last, normed_far, normed_near)
-        )
         grad_gate = scatter(plus(own[1], gate_got))
         normed_grad = (normed_near.astype(f32) + swap(normed_far, "core").astype(f32)).astype(bf16)
         normed_got = swap(normed_grad[part:], "row")

time: 640 us -> 636 us (level)
  transfers between devices with their start and end apart: 42 -> 42, of which waited for: 23 -> 24; matrix products, arithmetic and copies ran while one was open for 9% -> 9% of each run, Pallas kernels for 34% -> 34%
where the time goes in v5:
time: 636 us; the launch traced here: 628 us
  waiting for transfers between devices  258 us (41%)
  Pallas kernels  214 us (34%)
  local copies, waits for them, and re-layouts  73.9 us (12%)
  other arithmetic  37.6 us (6%)
  starting transfers between devices  28.6 us (4%)
  between operations  15.3 us (2%)
    ppermute x12, waiting for transfers between devices, from_inner(): lax.ppermute(values, 'inner', [((i + k) % inner, i) for i in range(inner)])  129 us
    all_gather x4, waiting for transfers between devices, gather(): return lax.all_gather(values, 'outer', axis=0, tiled=True)  66.7 us
    ppermute x19, waiting for transfers between devices, swap(): return lax.ppermute(values, axis, [(0, 1), (1, 0)])  58.5 us
    pallas_call x8, Pallas kernels, back_rows(): pl.pallas_call(kernel, grid=(width // tile,), in_specs=specs, out_specs=s...  56.4 us
    unnamed x202, local copies, waits for them, and re-layouts  54.8 us
    pallas_call x8, Pallas kernels, weight_part(): pl.pallas_call(kernel, grid=(tiles,), in_specs=[row_spec, row_spec] + [wh...  41.7 us
    pallas_call x3, Pallas kernels, through(): pl.pallas_call(kernel, grid=(2,), in_specs=of_group(near, far, 2) + resid...  24.2 us
    pallas_call x6, Pallas kernels, row_call(): pl.pallas_call(kernel, grid=(rows // tile,), in_specs=[pl.BlockSpec(memor...  18.7 us
  transfers between devices with their start and end apart: 42, of which 24 were waited for; matrix products, arithmetic and copies ran while one was open for 9% of the time, Pallas kernels for 34%

profile of v5, /device:TPU:0, one launch (start us, length us, event | category | flops | bytes accessed | tf_op | source)
XLA Modules:
  0.0 627.7 jit_solution(17228117166866253334)
XLA Ops:
  19.8 14.3 %collective-permute-done.3 = bf16[256,1408]{1,0:T(8,128)(2,1)} collective-permute-done((bf16[256,1408]{1,0:T(8,128)(2,1)}, bf16[256,1408]{1,0:T(8,128)(2,1)}, u32[]{:S(2)}, u32[]{:S(2)}) %collective-permute-start.3) | collective-permute-done | bytes 720928 | tf_op jit(solution)/shard_map/ppermute | solution.py:697
  36.7 8.7 %collective-permute-done.2 = f32[320]{0:T(512)S(1)} collective-permute-done((f32[320]{0:T(512)S(1)}, f32[320]{0:T(512)S(1)}, u32[]{:S(2)}, u32[]{:S(2)}) %collective-permute-start.2) | collective-permute-done | bytes 1312 | tf_op jit(solution)/shard_map/ppermute | solution.py:700
  51.9 23.2 %all-gather.5.cloned.1.call-done.refs_0_.refs_2_.refs_1_ = bf16[1024,1408]{1,0:T(8,128)(2,1)} async-done(((bf16[256,1408]{1,0:T(8,128)(2,1)}), bf16[1024,1408]{1,0:T(8,128)(2,1)}) %all-gather.5.cloned.1.call-update) | async-done | bytes 2883600 | tf_op jit(solution)/shard_map/all_gather | solution.py:706
  82.9 3.0 kept.1.refs_0_.near_rows
  86.0 5.2 collective-permute-done.6.refs_1_.far_rows
  91.2 43.4 %all-gather.7.cloned.1.call-done.refs_2_.refs_1_ = bf16[1024,1408]{1,0:T(8,128)(2,1)} async-done(((bf16[256,1408]{1,0:T(8,128)(2,1)}), bf16[1024,1408]{1,0:T(8,128)(2,1)}) %all-gather.7.cloned.1.call-update) | async-done | bytes 2883600 | tf_op jit(solution)/shard_map/all_gather | solution.py:706
  134.6 5.0 collective-permute-done.5.refs_1_.refs_3_.refs_2_
  147.2 4.1 norm_far.1.refs_1_.far_rows
  151.3 7.2 %joint.1.operands_1_ = f32[1280,768]{1,0:T(8,128)S(1)} custom-call(bf16[640,2048]{1,0:T(8,128)(2,1)S(1)} %norm_near.1.refs_0_.near_rows, bf16[640,2048]{1,0:T(8,128)(2,1)S(1)} %norm_far.1.refs_1_.far_rows, bf16[1024,1408]{1,0:T(8,128)(2,1)S(1)} %copy-done, bf16[1024,1408]{1,0:T(8,128)(2,1)} %collective-permute-done.5.refs_1_.refs_3_.refs_2_), custom_call_target="tpu_custom_call" | custom-call | flops 1006632960 | bytes 2097152 | tf_op jit(solution)/shard_map/joint/pallas_call | solution.py:421
  164.5 10.0 %attend.1 = (bf16[640,512]{1,0:T(8,128)(2,1)S(1)}, bf16[640,512]{1,0:T(8,128)(2,1)S(1)}, bf16[1280,768]{1,0:T(8,128)(2,1)S(1)}) custom-call(s32[14]{0:T(128)S(1)} %concatenate.37.operands_0_, f32[1280,768]{1,0:T(8,128)S(1)} %joint.1.operands_1_, f32[1280,128]{1,0:T(8,128)S(1)} %get-tuple-element.198.operands_2_.operands_3_, ...), custom_call_target="tpu_custom_call" | custom-call | flops 1476395008 | bytes 1966080 | tf_op jit(solution)/shard_map/attend/pallas_call | solution.py:799
  176.5 5.8 attended_far.1
  186.3 4.9 attended_near.1
  191.3 4.4 add_convert_fusion.3.mine
  195.7 8.3 %collective-permute-done.10.refs_5_.refs_4_ = bf16[256,1408]{1,0:T(8,128)(2,1)} collective-permute-done((bf16[256,1408]{1,0:T(8,128)(2,1)}, bf16[256,1408]{1,0:T(8,128)(2,1)}, u32[]{:S(2)}, u32[]{:S(2)}) %collective-permute-start.10) | collective-permute-done | bytes 720928 | tf_op jit(solution)/shard_map/ppermute | solution.py:697
  207.5 17.3 %collective-permute-done.12.refs_6_.refs_5_ = bf16[256,1408]{1,0:T(8,128)(2,1)S(1)} collective-permute-done((bf16[256,1408]{1,0:T(8,128)(2,1)}, bf16[256,1408]{1,0:T(8,128)(2,1)S(1)}, u32[]{:S(2)}, u32[]{:S(2)}) %collective-permute-start.12) | collective-permute-done | bytes 720928 | tf_op jit(solution)/shard_map/ppermute | solution.py:697
  227.8 11.7 %hidden_grad.1.refs_2_ = bf16[1280,1408]{1,0:T(8,128)(2,1)S(1)} custom-call(bf16[640,2048]{1,0:T(8,128)(2,1)} %kept.1.refs_0_.near_rows, bf16[640,2048]{1,0:T(8,128)(2,1)} %collective-permute-done.6.refs_1_.far_rows, bf16[1024,1408]{1,0:T(8,128)(2,1)S(1)} %copy-done.17, bf16[256,1408]{1,0:T(8,128)(2,1)} %collective-permute-done.7.refs_3_.refs_2_, ...), custom_call_target="tpu_custom_call" | custom-call | flops 1845493760 | bytes 2752512 | tf_op jit(solution)/shard_map/hidden_grad/pallas_call | solution.py:421
  239.5 23.2 %collective-permute-done.11.got = bf16[640,2048]{1,0:T(8,128)(2,1)S(1)} collective-permute-done((bf16[640,2048]{1,0:T(8,128)(2,1)}, bf16[640,2048]{1,0:T(8,128)(2,1)S(1)}, u32[]{:S(2)}, u32[]{:S(2)}) %collective-permute-start.11) | collective-permute-done | bytes 2621472 | tf_op jit(solution)/shard_map/ppermute | solution.py:700
  267.8 17.1 %collective-permute-done.14.refs_4_.refs_2_ = bf16[1024,1408]{1,0:T(8,128)(2,1)S(1)} collective-permute-done((bf16[1024,1408]{1,0:T(8,128)(2,1)}, bf16[1024,1408]{1,0:T(8,128)(2,1)S(1)}, u32[]{:S(2)}, u32[]{:S(2)}) %collective-permute-start.14) | collective-permute-done | bytes 2883616 | tf_op jit(solution)/shard_map/ppermute | solution.py:697
  285.0 11.4 %gate.1 = (f32[1280,1408]{1,0:T(8,128)}, bf16[1280,1408]{1,0:T(8,128)(2,1)S(1)}) custom-call(bf16[640,2048]{1,0:T(8,128)(2,1)S(1)} %get-tuple-element.122.refs_0_.near_rows, bf16[640,2048]{1,0:T(8,128)(2,1)S(1)} %collective-permute-done.13.refs_1_.far_rows, bf16[1280,1408]{1,0:T(8,128)(2,1)S(1)} %hidden_grad.1.refs_2_, bf16[1024,1408]{1,0:T(8,128)(2,1)S(1)} %copy-done.29, ...), custom_call_target="tpu_custom_call" | custom-call | flops 1845493760 | bytes 2752512 | tf_op jit(solution)/shard_map/gate/pallas_call | solution.py:452
  296.4 12.1 %grad_up_late.1 = bf16[1024,2816]{1,0:T(8,128)(2,1)} custom-call(bf16[640,2048]{1,0:T(8,128)(2,1)S(1)} %get-tuple-element.122.refs_0_.near_rows, bf16[640,2048]{1,0:T(8,128)(2,1)S(1)} %collective-permute-done.13.refs_1_.far_rows, bf16[1280,1408]{1,0:T(8,128)(2,1)S(1)} %get-tuple-element.137.refs_0_.refs_3_), custom_call_target="tpu_custom_call" | custom-call | flops 1845493760 | bytes 1556480 | tf_op jit(solution)/shard_map/grad_up_late/pallas_call | solution.py:648
  319.1 12.7 %up.1 = (bf16[1280,1408]{1,0:T(8,128)(2,1)S(1)}, bf16[1280,1408]{1,0:T(8,128)(2,1)S(1)}) custom-call(bf16[640,2048]{1,0:T(8,128)(2,1)S(1)} %copy-done.4, bf16[640,2048]{1,0:T(8,128)(2,1)S(1)} %copy-done.8, bf16[1280,1408]{1,0:T(8,128)(2,1)S(1)} %copy-done.28, f32[1280,1408]{1,0:T(8,128)} %get-tuple-element.127.refs_3_, bf16[1024,2816]{1,0:T(8,128)(2,1)S(1)} %copy-done.1), custom_call_target="tpu_custom_call" | custom-call | flops 1845493760 | bytes 2752512 | tf_op jit(solution)/shard_map/up/pallas_call | solution.py:503
  331.9 9.2 %grad_down.2 = bf16[1024,1408]{1,0:T(8,128)(2,1)} custom-call(bf16[640,2048]{1,0:T(8,128)(2,1)} %kept.1.refs_0_.near_rows, bf16[640,2048]{1,0:T(8,128)(2,1)} %collective-permute-done.6.refs_1_.far_rows, bf16[1280,1408]{1,0:T(8,128)(2,1)S(1)} %get-tuple-element.142.refs_0_), custom_call_target="tpu_custom_call" | custom-call | flops 922746880 | bytes 1556480 | tf_op jit(solution)/shard_map/grad_down/pallas_call | solution.py:612
  343.2 9.2 %normed_ff_grad_far.1 = bf16[640,2048]{1,0:T(8,128)(2,1)S(1)} custom-call(bf16[1280,1408]{1,0:T(8,128)(2,1)S(1)} %copy-done.13, bf16[1024,1408]{1,0:T(8,128)(2,1)S(1)} %copy-done.30, bf16[1024,1408]{1,0:T(8,128)(2,1)S(1)} %copy-done.32, bf16[1280,1408]{1,0:T(8,128)(2,1)S(1)} %copy-done.26, bf16[1024,2816]{1,0:T(8,128)(2,1)S(1)} %copy-done.2, ...), custom_call_target="tpu_custom_call" | custom-call | flops 1845493760 | bytes 6127616 | tf_op jit(solution)/shard_map/normed_ff_grad_far/pallas_call | solution.py:570
  354.2 4.9 grad_gate.2
  359.1 10.5 %normed_ff_grad_near.1.mine = bf16[640,2048]{1,0:T(8,128)(2,1)} custom-call(bf16[1280,1408]{1,0:T(8,128)(2,1)S(1)} %copy-done.13, bf16[1024,1408]{1,0:T(8,128)(2,1)S(1)} %copy-done.30, bf16[1024,1408]{1,0:T(8,128)(2,1)S(1)} %copy-done.32, bf16[1280,1408]{1,0:T(8,128)(2,1)S(1)} %copy-done.26, bf16[1024,2816]{1,0:T(8,128)(2,1)S(1)} %copy-done.2, ...), custom_call_target="tpu_custom_call" | custom-call | flops 1845493760 | bytes 6782976 | tf_op jit(solution)/shard_map/normed_ff_grad_near/pallas_call | solution.py:570
  371.4 5.4 grad_gate_first.1
  384.0 5.0 grad_gate.3
  389.0 8.1 %grad_down.3 = bf16[1024,1408]{1,0:T(8,128)(2,1)} custom-call(bf16[640,2048]{1,0:T(8,128)(2,1)} %kept.1.refs_0_.near_rows, bf16[640,2048]{1,0:T(8,128)(2,1)} %collective-permute-done.6.refs_1_.far_rows, bf16[1280,1408]{1,0:T(8,128)(2,1)S(1)} %copy-done.16), custom_call_target="tpu_custom_call" | custom-call | flops 922746880 | bytes 1556480 | tf_op jit(solution)/shard_map/grad_down/pallas_call | solution.py:612
  397.0 7.5 %branch_near.1 = bf16[640,2048]{1,0:T(8,128)(2,1)S(1)} custom-call(bf16[1280,1408]{1,0:T(8,128)(2,1)S(1)} %copy-done.16, bf16[1024,1408]{1,0:T(8,128)(2,1)S(1)} %copy-done.18, bf16[256,1408]{1,0:T(8,128)(2,1)} %collective-permute-done.7.refs_3_.refs_2_, bf16[256,1408]{1,0:T(8,128)(2,1)S(1)} %copy-done.58, ...), custom_call_target="tpu_custom_call" | custom-call | flops 922746880 | bytes 2342912 | tf_op jit(solution)/shard_map/branch_near/pallas_call | solution.py:570
  406.0 7.6 %branch_far.1 = bf16[640,2048]{1,0:T(8,128)(2,1)S(1)} custom-call(bf16[1280,1408]{1,0:T(8,128)(2,1)S(1)} %copy-done.16, bf16[1024,1408]{1,0:T(8,128)(2,1)S(1)} %copy-done.18, bf16[256,1408]{1,0:T(8,128)(2,1)} %collective-permute-done.7.refs_3_.refs_2_, bf16[256,1408]{1,0:T(8,128)(2,1)S(1)} %copy-done.58, ...), custom_call_target="tpu_custom_call" | custom-call | flops 922746880 | bytes 2342912 | tf_op jit(solution)/shard_map/branch_far/pallas_call | solution.py:570
  415.2 26.8 %collective-permute-done.17 = bf16[1024,1408]{1,0:T(8,128)(2,1)S(1)} collective-permute-done((bf16[1024,1408]{1,0:T(8,128)(2,1)}, bf16[1024,1408]{1,0:T(8,128)(2,1)S(1)}, u32[]{:S(2)}, u32[]{:S(2)}) %collective-permute-start.17) | collective-permute-done | bytes 2883616 | tf_op jit(solution)/shard_map/ppermute | solution.py:697
  450.3 4.9 middle_back.1
  458.9 3.5 collective-permute-done.18.far_rows.refs_1_
  462.4 3.2 grad_output.3
  465.6 5.2 mixed_grad.1.operands_2_
  470.9 16.1 %attend_back.1 = (bf16[640,768]{1,0:T(8,128)(2,1)S(1)}, bf16[640,768]{1,0:T(8,128)(2,1)S(1)}) custom-call(s32[14]{0:T(128)S(1)} %concatenate.37.operands_0_, bf16[1280,768]{1,0:T(8,128)(2,1)S(1)} %copy-done.84, bf16[1280,512]{1,0:T(8,128)(2,1)S(1)} %mixed_grad.1.operands_2_, f32[1280,128]{1,0:T(8,128)S(1)} %copy-done.76, f32[1280,128]{1,0:T(8,128)S(1)} %copy-done.78), custom_call_target="tpu_custom_call" | custom-call | flops 2214592512 | bytes 1966080 | tf_op jit(solution)/shard_map/attend_back/pallas_call | solution.py:928
  487.0 5.8 normed_grad_far.1
  492.8 4.2 grad_joint.2
  500.5 3.8 add_convert_fusion.4
  507.0 5.1 normed_grad_near.1
  518.1 5.0 add_convert_fusion.1.mine
  523.2 3.2 grad_output.2
  526.8 4.1 grad_joint.3
  530.9 32.5 %collective-permute-done.19 = bf16[1024,512]{1,0:T(8,128)(2,1)S(1)} collective-permute-done((bf16[1024,512]{1,0:T(8,128)(2,1)S(1)}, bf16[1024,512]{1,0:T(8,128)(2,1)S(1)}, u32[]{:S(2)}, u32[]{:S(2)}) %collective-permute-start.19) | collective-permute-done | bytes 1048608 | tf_op jit(solution)/shard_map/ppermute | solution.py:697
  574.2 3.3 collective-permute-done.27
  585.8 3.2 input_grad.1
  600.3 10.3 %collective-permute-done.32 = f32[1,256]{1,0:T(1,128)S(1)} collective-permute-done((f32[1,256]{1,0:T(1,128)S(1)}, f32[1,256]{1,0:T(1,128)S(1)}, u32[]{:S(2)}, u32[]{:S(2)}) %collective-permute-start.32) | collective-permute-done | bytes 1056 | tf_op jit(solution)/shard_map/ppermute | solution.py:700
  613.2 3.9 reduce-scatter.12.cloned.1.call-done
  (331 shorter events, 148.2 us)
Async XLA Ops:
  7.2 68.0 %all-gather.5.cloned.1.call-start = ((), (), s32[]{:S(2)}) async-start(), calls=%async_computation.5 | async-start | bytes 3604480 | tf_op jit(solution)/shard_map/all_gather | solution.py:706
  13.1 121.5 %all-gather.7.cloned.1.call-start = ((), (), s32[]{:S(2)}) async-start(), calls=%async_computation.6 | async-start | bytes 3604480 | tf_op jit(solution)/shard_map/all_gather | solution.py:706
  13.2 32.2 %collective-permute-start.1 = (bf16[320,2048]{1,0:T(8,128)(2,1)}, bf16[320,2048]{1,0:T(8,128)(2,1)}, u32[]{:S(2)}, u32[]{:S(2)}) collective-permute-start(bf16[320,2048]{1,0:T(8,128)(2,1)} %rows.1), channel_id=1, source_target_pairs={{0,2},{2,0},{1,3},{3,1},{4,6},{6,4},{5,7},{7,5},{8,10},{10,8},{9,1... | collective-permute-start | bytes 3932168 | tf_op jit(solution)/shard_map/ppermute | solution.py:700
  16.2 17.9 %collective-permute-start.3 = (bf16[256,1408]{1,0:T(8,128)(2,1)}, bf16[256,1408]{1,0:T(8,128)(2,1)}, u32[]{:S(2)}, u32[]{:S(2)}) collective-permute-start(bf16[256,1408]{1,0:T(8,128)(2,1)} %param.23), channel_id=1, source_target_pairs={{4,0},{0,4},{5,1},{1,5},{6,2},{2,6},{7,3},{3,7},{12,8},{8,12},{13,... | collective-permute-start | bytes 2162696 | tf_op jit(solution)/shard_map/ppermute | solution.py:697
  17.7 178.0 %all-gather.9.cloned.1.call-start = ((), (), s32[]{:S(2)}) async-start(), calls=%async_computation.7 | async-start | bytes 3604480 | tf_op jit(solution)/shard_map/all_gather | solution.py:706
  17.8 27.5 %collective-permute-start.2 = (f32[320]{0:T(512)S(1)}, f32[320]{0:T(512)S(1)}, u32[]{:S(2)}, u32[]{:S(2)}) collective-permute-start(f32[320]{0:T(512)S(1)} %subtract_convert_fusion), channel_id=1, source_target_pairs={{0,2},{2,0},{1,3},{3,1},{4,6},{6,4},{5,7},{7,5},{8,10},{10,8},{9,1... | collective-permute-start | bytes 3848 | tf_op jit(solution)/shard_map/ppermute | solution.py:700
  46.8 5.1 collective-permute-start.4
  46.9 31.5 %collective-permute-start = (bf16[320,2048]{1,0:T(8,128)(2,1)}, bf16[320,2048]{1,0:T(8,128)(2,1)}, u32[]{:S(2)}, u32[]{:S(2)}) collective-permute-start(bf16[320,2048]{1,0:T(8,128)(2,1)} %param.25), channel_id=1, source_target_pairs={{0,2},{2,0},{1,3},{3,1},{4,6},{6,4},{5,7},{7,5},{8,10},{10,8},{9,1... | collective-permute-start | bytes 3932168 | tf_op jit(solution)/shard_map/ppermute | solution.py:700
  75.2 64.5 %collective-permute-start.5 = (bf16[1024,1408]{1,0:T(8,128)(2,1)}, bf16[1024,1408]{1,0:T(8,128)(2,1)}, u32[]{:S(2)}, u32[]{:S(2)}) collective-permute-start(bf16[1024,1408]{1,0:T(8,128)(2,1)} %all-gather.5.cloned.1.call-done.refs_0_.refs_2_.refs_1_), channel_id=1, source_target_pairs={{4,0},{0,4},{5,1},{1,5},{6,2},{2,6},{7,3},{3,7},{12,8},{8,12},{13,... | collective-permute-start | bytes 8650760 | tf_op jit(solution)/shard_map/ppermute | solution.py:697
  82.9 60.2 %copy-start.97 = (s32[1,10]{1,0:T(1,128)S(1)}, s32[1,10]{1,0:T(1,128)}, u32[]{:S(2)}) copy-start(s32[1,10]{1,0:T(1,128)} %param.15) | copy-start | bytes 124
  82.9 60.3 %copy-start = (bf16[1024,1408]{1,0:T(8,128)(2,1)S(1)}, bf16[1024,1408]{1,0:T(8,128)(2,1)}, u32[]{:S(2)}) copy-start(bf16[1024,1408]{1,0:T(8,128)(2,1)} %all-gather.5.cloned.1.call-done.refs_0_.refs_2_.refs_1_) | copy-start | bytes 8650756
  86.0 5.3 collective-permute-start.6
  86.0 224.4 %all-gather.11.cloned.1.call-start = ((), (), s32[]{:S(2)}) async-start(), calls=%async_computation.8 | async-start | bytes 7208960 | tf_op jit(solution)/shard_map/all_gather | solution.py:706
  141.7 17.3 %collective-permute-start.7 = (bf16[256,1408]{1,0:T(8,128)(2,1)}, bf16[256,1408]{1,0:T(8,128)(2,1)}, u32[]{:S(2)}, u32[]{:S(2)}) collective-permute-start(bf16[256,1408]{1,0:T(8,128)(2,1)} %slice.58), channel_id=1, source_target_pairs={{4,0},{0,4},{5,1},{1,5},{6,2},{2,6},{7,3},{3,7},{12,8},{8,12},{13,... | collective-permute-start | bytes 2162696 | tf_op jit(solution)/shard_map/ppermute | solution.py:697
  160.1 16.4 %collective-permute-start.8 = (bf16[256,1408]{1,0:T(8,128)(2,1)S(1)}, bf16[256,1408]{1,0:T(8,128)(2,1)S(1)}, u32[]{:S(2)}, u32[]{:S(2)}) collective-permute-start(bf16[256,1408]{1,0:T(8,128)(2,1)S(1)} %slice.59), channel_id=1, source_target_pairs={{4,0},{0,4},{5,1},{1,5},{6,2},{2,6},{7,3},{3,7},{12,8},{8,12},{13,... | collective-permute-start | bytes 2162696 | tf_op jit(solution)/shard_map/ppermute | solution.py:697
  182.4 8.9 %collective-permute-start.9 = (bf16[640,2048]{1,0:T(8,128)(2,1)}, bf16[640,2048]{1,0:T(8,128)(2,1)}, u32[]{:S(2)}, u32[]{:S(2)}) collective-permute-start(bf16[640,2048]{1,0:T(8,128)(2,1)} %attended_far.1), channel_id=1, source_target_pairs={{0,1},{1,0},{2,3},{3,2},{4,5},{5,4},{6,7},{7,6},{8,9},{9,8},{10,11... | collective-permute-start | bytes 7864328 | tf_op jit(solution)/shard_map/ppermute | solution.py:700
  182.5 317.5 %reduce-scatter.6.cloned.1.call-start = ((), (), s32[]{:S(2)}) async-start(), calls=%async_computation.9 | async-start | bytes 7208960 | tf_op jit(solution)/shard_map/reduce_scatter | solution.py:709
  185.1 18.9 %collective-permute-start.10 = (bf16[256,1408]{1,0:T(8,128)(2,1)}, bf16[256,1408]{1,0:T(8,128)(2,1)}, u32[]{:S(2)}, u32[]{:S(2)}) collective-permute-start(bf16[256,1408]{1,0:T(8,128)(2,1)} %get-tuple-element.186), channel_id=1, source_target_pairs={{4,0},{0,4},{5,1},{1,5},{6,2},{2,6},{7,3},{3,7},{12,8},{8,12},{13,... | collective-permute-start | bytes 2162696 | tf_op jit(solution)/shard_map/ppermute | solution.py:697
  204.0 58.7 %collective-permute-start.11 = (bf16[640,2048]{1,0:T(8,128)(2,1)}, bf16[640,2048]{1,0:T(8,128)(2,1)S(1)}, u32[]{:S(2)}, u32[]{:S(2)}) collective-permute-start(bf16[640,2048]{1,0:T(8,128)(2,1)} %add_convert_fusion.3.mine), channel_id=1, source_target_pairs={{0,2},{2,0},{1,3},{3,1},{4,6},{6,4},{5,7},{7,5},{8,10},{10,8},{9,1... | collective-permute-start | bytes 7864328 | tf_op jit(solution)/shard_map/ppermute | solution.py:700
  205.5 19.3 %collective-permute-start.12 = (bf16[256,1408]{1,0:T(8,128)(2,1)}, bf16[256,1408]{1,0:T(8,128)(2,1)S(1)}, u32[]{:S(2)}, u32[]{:S(2)}) collective-permute-start(bf16[256,1408]{1,0:T(8,128)(2,1)} %get-tuple-element.185), channel_id=1, source_target_pairs={{4,0},{0,4},{5,1},{1,5},{6,2},{2,6},{7,3},{3,7},{12,8},{8,12},{13,... | collective-permute-start | bytes 2162696 | tf_op jit(solution)/shard_map/ppermute | solution.py:697
  206.7 78.3 %collective-permute-start.14 = (bf16[1024,1408]{1,0:T(8,128)(2,1)}, bf16[1024,1408]{1,0:T(8,128)(2,1)S(1)}, u32[]{:S(2)}, u32[]{:S(2)}) collective-permute-start(bf16[1024,1408]{1,0:T(8,128)(2,1)} %all-gather.9.cloned.1.call-done.refs_3_.refs_1_), channel_id=1, source_target_pairs={{4,0},{0,4},{5,1},{1,5},{6,2},{2,6},{7,3},{3,7},{12,8},{8,12},{13,... | collective-permute-start | bytes 8650760 | tf_op jit(solution)/shard_map/ppermute | solution.py:697
  227.8 35.0 %copy-start.48 = (bf16[640,2048]{1,0:T(8,128)(2,1)S(1)}, bf16[640,2048]{1,0:T(8,128)(2,1)}, u32[]{:S(2)}) copy-start(bf16[640,2048]{1,0:T(8,128)(2,1)} %add_convert_fusion.3.mine) | copy-start | bytes 7864324
  239.5 45.5 %copy-start.27 = (bf16[1280,1408]{1,0:T(8,128)(2,1)}, bf16[1280,1408]{1,0:T(8,128)(2,1)S(1)}, u32[]{:S(2)}) copy-start(bf16[1280,1408]{1,0:T(8,128)(2,1)S(1)} %hidden_grad.1.refs_2_) | copy-start | bytes 10813444
  267.8 17.2 %collective-permute-start.13 = (bf16[640,2048]{1,0:T(8,128)(2,1)S(1)}, bf16[640,2048]{1,0:T(8,128)(2,1)S(1)}, u32[]{:S(2)}, u32[]{:S(2)}) collective-permute-start(bf16[640,2048]{1,0:T(8,128)(2,1)S(1)} %get-tuple-element.122.refs_0_.near_rows), channel_id=1, source_target_pairs={{0,1},{1,0},{2,3},{3,2},{4,5},{5,4},{6,7},{7,6},{8,9},{9,8},{10,11... | collective-permute-start | bytes 7864328 | tf_op jit(solution)/shard_map/ppermute | solution.py:700
  310.4 255.9 %reduce-scatter.10.cloned.1.call-start = ((), (), s32[]{:S(2)}) async-start(), calls=%async_computation.11 | async-start | bytes 2621440 | tf_op jit(solution)/shard_map/reduce_scatter | solution.py:709
  352.4 6.7 %collective-permute-start.15 = (bf16[640,2048]{1,0:T(8,128)(2,1)S(1)}, bf16[640,2048]{1,0:T(8,128)(2,1)S(1)}, u32[]{:S(2)}, u32[]{:S(2)}) collective-permute-start(bf16[640,2048]{1,0:T(8,128)(2,1)S(1)} %normed_ff_grad_far.1), channel_id=1, source_target_pairs={{0,1},{1,0},{2,3},{3,2},{4,5},{5,4},{6,7},{7,6},{8,9},{9,8},{10,11... | collective-permute-start | bytes 7864328 | tf_op jit(solution)/shard_map/ppermute | solution.py:700
  376.8 189.4 %reduce-scatter.8.cloned.1.call-start = ((), (), s32[]{:S(2)}) async-start(), calls=%async_computation.10 | async-start | bytes 3604480 | tf_op jit(solution)/shard_map/reduce_scatter | solution.py:709
  376.8 65.1 %collective-permute-start.17 = (bf16[1024,1408]{1,0:T(8,128)(2,1)}, bf16[1024,1408]{1,0:T(8,128)(2,1)S(1)}, u32[]{:S(2)}, u32[]{:S(2)}) collective-permute-start(bf16[1024,1408]{1,0:T(8,128)(2,1)} %grad_down.2), channel_id=1, source_target_pairs={{4,0},{0,4},{5,1},{1,5},{6,2},{2,6},{7,3},{3,7},{12,8},{8,12},{13,... | collective-permute-start | bytes 8650760 | tf_op jit(solution)/shard_map/ppermute | solution.py:697
  378.3 66.0 %collective-permute-start.16 = (bf16[640,2048]{1,0:T(8,128)(2,1)}, bf16[640,2048]{1,0:T(8,128)(2,1)}, u32[]{:S(2)}, u32[]{:S(2)}) collective-permute-start(bf16[640,2048]{1,0:T(8,128)(2,1)} %normed_ff_grad_near.1.mine), channel_id=1, source_target_pairs={{0,2},{2,0},{1,3},{3,1},{4,6},{6,4},{5,7},{7,5},{8,10},{10,8},{9,1... | collective-permute-start | bytes 7864328 | tf_op jit(solution)/shard_map/ppermute | solution.py:700
  406.0 36.0 %copy-start.86 = (bf16[1024,1408]{1,0:T(8,128)(2,1)S(1)}, bf16[1024,1408]{1,0:T(8,128)(2,1)}, u32[]{:S(2)}) copy-start(bf16[1024,1408]{1,0:T(8,128)(2,1)} %grad_down.3) | copy-start | bytes 8650756
  444.3 133.3 %reduce-scatter.14.cloned.1.call-start = ((), (), s32[]{:S(2)}) async-start(), calls=%async_computation.13 | async-start | bytes 2293760 | tf_op jit(solution)/shard_map/reduce_scatter | solution.py:709
  457.5 4.9 collective-permute-start.18
  457.5 42.5 %collective-permute-start.20 = (bf16[1024,896]{1,0:T(8,128)(2,1)S(1)}, bf16[1024,896]{1,0:T(8,128)(2,1)}, u32[]{:S(2)}, u32[]{:S(2)}) collective-permute-start(bf16[1024,896]{1,0:T(8,128)(2,1)S(1)} %copy-done.92), channel_id=1, source_target_pairs={{4,0},{0,4},{5,1},{1,5},{6,2},{2,6},{7,3},{3,7},{12,8},{8,12},{13,... | collective-permute-start | bytes 5505032 | tf_op jit(solution)/shard_map/ppermute | solution.py:697
  500.0 12.1 %collective-permute-start.22 = (bf16[640,2048]{1,0:T(8,128)(2,1)}, bf16[640,2048]{1,0:T(8,128)(2,1)}, u32[]{:S(2)}, u32[]{:S(2)}) collective-permute-start(bf16[640,2048]{1,0:T(8,128)(2,1)} %copy-done.72), channel_id=1, source_target_pairs={{0,1},{1,0},{2,3},{3,2},{4,5},{5,4},{6,7},{7,6},{8,9},{9,8},{10,11... | collective-permute-start | bytes 7864328 | tf_op jit(solution)/shard_map/ppermute | solution.py:700
  500.0 18.1 %collective-permute-start.24 = (bf16[640,2048]{1,0:T(8,128)(2,1)}, bf16[640,2048]{1,0:T(8,128)(2,1)}, u32[]{:S(2)}, u32[]{:S(2)}) collective-permute-start(bf16[640,2048]{1,0:T(8,128)(2,1)} %copy-done.71), channel_id=1, source_target_pairs={{0,1},{1,0},{2,3},{3,2},{4,5},{5,4},{6,7},{7,6},{8,9},{9,8},{10,11... | collective-permute-start | bytes 7864328 | tf_op jit(solution)/shard_map/ppermute | solution.py:700
  504.3 112.8 %reduce-scatter.12.cloned.1.call-start = ((), (), s32[]{:S(2)}) async-start(), calls=%async_computation.12 | async-start | bytes 3276800 | tf_op jit(solution)/shard_map/reduce_scatter | solution.py:709
  504.4 59.1 %collective-permute-start.21 = (bf16[1024,768]{1,0:T(8,128)(2,1)}, bf16[1024,768]{1,0:T(8,128)(2,1)S(1)}, u32[]{:S(2)}, u32[]{:S(2)}) collective-permute-start(bf16[1024,768]{1,0:T(8,128)(2,1)} %grad_joint.2), channel_id=1, source_target_pairs={{4,0},{0,4},{5,1},{1,5},{6,2},{2,6},{7,3},{3,7},{12,8},{8,12},{13,... | collective-permute-start | bytes 4718600 | tf_op jit(solution)/shard_map/ppermute | solution.py:697
  516.7 46.7 %collective-permute-start.23 = (bf16[320,2048]{1,0:T(8,128)(2,1)S(1)}, bf16[320,2048]{1,0:T(8,128)(2,1)S(1)}, u32[]{:S(2)}, u32[]{:S(2)}) collective-permute-start(bf16[320,2048]{1,0:T(8,128)(2,1)S(1)} %slice.76), channel_id=1, source_target_pairs={{0,2},{2,0},{1,3},{3,1},{4,6},{6,4},{5,7},{7,5},{8,10},{10,8},{9,1... | collective-permute-start | bytes 3932168 | tf_op jit(solution)/shard_map/ppermute | solution.py:700
  517.1 46.3 %collective-permute-start.19 = (bf16[1024,512]{1,0:T(8,128)(2,1)S(1)}, bf16[1024,512]{1,0:T(8,128)(2,1)S(1)}, u32[]{:S(2)}, u32[]{:S(2)}) collective-permute-start(bf16[1024,512]{1,0:T(8,128)(2,1)S(1)} %copy-done.93), channel_id=1, source_target_pairs={{4,0},{0,4},{5,1},{1,5},{6,2},{2,6},{7,3},{3,7},{12,8},{8,12},{13,... | collective-permute-start | bytes 3145736 | tf_op jit(solution)/shard_map/ppermute | solution.py:697
  526.8 36.6 %copy-start.88 = (bf16[1024,512]{1,0:T(8,128)(2,1)S(1)}, bf16[1024,512]{1,0:T(8,128)(2,1)}, u32[]{:S(2)}) copy-start(bf16[1024,512]{1,0:T(8,128)(2,1)} %grad_output.2) | copy-start | bytes 3145732
  570.8 23.1 %collective-permute-start.30 = (bf16[256,1920]{1,0:T(8,128)(2,1)}, bf16[256,1920]{1,0:T(8,128)(2,1)}, u32[]{:S(2)}, u32[]{:S(2)}) collective-permute-start(bf16[256,1920]{1,0:T(8,128)(2,1)} %pad_maximum_fusion.3), channel_id=1, source_target_pairs={{4,0},{0,4},{5,1},{1,5},{6,2},{2,6},{7,3},{3,7},{12,8},{8,12},{13,... | collective-permute-start | bytes 2949128 | tf_op jit(solution)/shard_map/ppermute | solution.py:697
  572.7 1.2 collective-permute-start.26
  573.9 3.6 collective-permute-start.27
  577.5 11.5 %collective-permute-start.28 = (f32[1,1024]{1,0:T(1,128)S(1)}, f32[1,1024]{1,0:T(1,128)S(1)}, u32[]{:S(2)}, u32[]{:S(2)}) collective-permute-start(f32[1,1024]{1,0:T(1,128)S(1)} %add.203), channel_id=1, source_target_pairs={{8,0},{0,8},{24,16},{16,24},{9,1},{1,9},{25,17},{17,25},{10,2},{2,... | collective-permute-start | bytes 12296 | tf_op jit(solution)/shard_map/ppermute | solution.py:1015
  580.4 30.8 %collective-permute-start.25 = (bf16[320,2048]{1,0:T(8,128)(2,1)S(1)}, bf16[320,2048]{1,0:T(8,128)(2,1)S(1)}, u32[]{:S(2)}, u32[]{:S(2)}) collective-permute-start(bf16[320,2048]{1,0:T(8,128)(2,1)S(1)} %slice.63), channel_id=1, source_target_pairs={{0,2},{2,0},{1,3},{3,1},{4,6},{6,4},{5,7},{7,5},{8,10},{10,8},{9,1... | collective-permute-start | bytes 3932168 | tf_op jit(solution)/shard_map/ppermute | solution.py:700
  589.1 8.9 %collective-permute-start.29 = (f32[1,1024]{1,0:T(1,128)S(1)}, f32[1,1024]{1,0:T(1,128)S(1)}, u32[]{:S(2)}, u32[]{:S(2)}) collective-permute-start(f32[1,1024]{1,0:T(1,128)S(1)} %add.204), channel_id=1, source_target_pairs={{16,0},{24,8},{0,16},{8,24},{17,1},{25,9},{1,17},{9,25},{18,2},{26... | collective-permute-start | bytes 12296 | tf_op jit(solution)/shard_map/ppermute | solution.py:1015
  598.0 1.1 collective-permute-start.31
  599.1 11.5 %collective-permute-start.32 = (f32[1,256]{1,0:T(1,128)S(1)}, f32[1,256]{1,0:T(1,128)S(1)}, u32[]{:S(2)}, u32[]{:S(2)}) collective-permute-start(f32[1,256]{1,0:T(1,128)S(1)} %add.211), channel_id=1, source_target_pairs={{0,2},{2,0},{1,3},{3,1},{4,6},{6,4},{5,7},{7,5},{8,10},{10,8},{9,1... | collective-permute-start | bytes 3080 | tf_op jit(solution)/shard_map/ppermute | solution.py:700
  (94 other events, 685.3 us)
Sparse Core Ops, SparseCore 0:
  13.2 61.8 all-gather.4
  76.7 57.8 all-gather.6
  136.2 57.8 all-gather.8
  196.1 105.3 all-gather.10
  310.5 100.4 reduce-scatter.5
  413.1 44.3 reduce-scatter.9
  459.9 55.4 reduce-scatter.7
  517.9 39.2 reduce-scatter.13
  566.4 50.6 reduce-scatter.11
